TPU v7x, 32 devices: a whole 2x2x4 slice. The times are simulated.
32 devices in a mesh: parts: 2 (over y), expert: 4 (over z), hidden: 2 (over x), rep: 2 (over core).
Axes of the slice: x: 2, y: 2, z: 4, core: 2. Of those that a mesh axis runs over, the one named last changes fastest.
Arguments:
- tokens: bfloat16 [1024, 4096], P(('parts', 'expert', 'rep'), 'hidden'), parts along dimension 0, may hold values from -6 to 6
- route_ids: int32 [1024, 2], P(('parts', 'expert', 'rep')), parts along dimension 0, may hold values from 0 to 3, all different within a row; in each aligned block of 64 rows (0 to 63, 64 to 127, ...) at most 48 rows name the same one
- route_weight: float32 [1024, 2], P(('parts', 'expert', 'rep')), parts along dimension 0, may hold values from 0.1 to 1
- user_slot: int32 [128, 4], P(('parts', 'expert', 'rep')), parts along dimension 0, may hold values from 0 to 15
- gate_weight: bfloat16 [4, 4096, 1536], P('expert', None, 'hidden'), may hold values from -0.09375 to 0.09375
- up_weight: bfloat16 [4, 4096, 1536], P('expert', None, 'hidden'), may hold values from -0.09375 to 0.09375
- down_weight: bfloat16 [4, 1536, 4096], P('expert', 'hidden'), may hold values from -0.15625 to 0.15625
- adapter_down: bfloat16 [4, 4096, 128], P('expert', 'hidden'), may hold values from -0.09375 to 0.09375
- adapter_up: bfloat16 [4, 128, 1536], P('expert', None, 'hidden'), may hold values from -2 to 2
Outputs:
- mixed: bfloat16 [1024, 4096], P(('parts', 'expert', 'rep'), 'hidden'), parts along dimension 0
There are 2 independent parts, one for each index of `parts`. A program takes and returns all parts, laid end to end along the dimension named above; an argument that names none is the same for every part. Nothing has to cross between parts.
Inputs may be any that keep to these rules, and one draw needn't show every extreme that they name: `route_ids`: each row names 2 different experts. Among the 64 rows of one device (aligned blocks), no expert is named by more than 48 rows, a bound that some block reaches.
All inputs are finite; a program needn't handle non-finite values.
Results may differ from a plain program's by a relative error of at most 0.015.
Values may be sent and summed in bfloat16 or wider, within the bound.
No kernel may reach another device: no remote copies, remote signals or barrier semaphores. Data moves between devices by JAX's collectives and lax.ppermute only.
A program may use at most 64 MiB of HBM per device.

v0:
```python
import jax
import jax.numpy as jnp
from jax import lax
from jax.sharding import PartitionSpec as P

RANK = 8
USER_TOK = 8


def local(
    tokens,
    route_ids,
    route_weight,
    user_slot,
    gate_weight,
    up_weight,
    down_weight,
    adapter_down,
    adapter_up,
):
    experts = lax.axis_size("expert")
    tok_rows, choices_each = route_ids.shape
    expert_capacity = tok_rows * choices_each * 3 // (2 * experts)
    width = gate_weight.shape[1]
    shard_width = tokens.shape[1]
    adapt_cols = adapter_down.shape[2]
    source_rows = lax.all_gather(tokens, "hidden", axis=1, tiled=True)
    sent_width = source_rows.shape[1]
    flat_ids = route_ids.reshape(-1)
    choose = (flat_ids[:, None] == jnp.arange(experts)[None, :]).astype(jnp.int32)
    position = jnp.sum((jnp.cumsum(choose, axis=0) - 1) * choose, axis=1)
    slot_index = flat_ids * expert_capacity + position
    dispatch = slot_index[:, None] == jnp.arange(experts * expert_capacity)[None, :]
    token_of = jnp.arange(tok_rows * choices_each) // choices_each
    owning = token_of[:, None] == jnp.arange(tok_rows)[None, :]
    send_map = jnp.dot(
        dispatch.T.astype(jnp.bfloat16),
        owning.astype(jnp.bfloat16),
        preferred_element_type=jnp.float32,
    ).astype(jnp.bfloat16)
    send_rows = (
        jnp.dot(send_map, source_rows, preferred_element_type=jnp.float32)
        .astype(jnp.bfloat16)
        .reshape(experts, expert_capacity, sent_width)
    )
    user_of = token_of // USER_TOK
    user_pick = user_of[:, None] == jnp.arange(user_slot.shape[0])[None, :]
    user_rows = jnp.sum(jnp.where(user_pick[:, :, None], user_slot[None, :, :], 0), axis=1)
    slot_code = jnp.sum(choose * user_rows, axis=1)
    send_codes = (
        jnp.sum(jnp.where(dispatch, slot_code[:, None], 0), axis=0)
        .astype(jnp.bfloat16)
        .reshape(experts, expert_capacity)
    )
    factor_full = lax.all_gather(adapter_down[0], "hidden", axis=0, tiled=True)
    rows = lax.all_to_all(send_rows, "expert", split_axis=0, concat_axis=0, tiled=True)
    codes = lax.all_to_all(send_codes, "expert", split_axis=0, concat_axis=0, tiled=True)
    sources = rows.shape[0]
    per_source = rows.shape[1]
    flattened = rows.reshape(sources * per_source, width)
    gate_values = jnp.dot(flattened, gate_weight[0], preferred_element_type=jnp.float32)
    up_values = jnp.dot(flattened, up_weight[0], preferred_element_type=jnp.float32)
    rank_full = jnp.dot(flattened, factor_full, preferred_element_type=jnp.float32)
    slot_mask = (
        codes.reshape(-1).astype(jnp.int32)[:, None] == (jnp.arange(adapt_cols) // RANK)[None, :]
    )
    rank_portion = jnp.where(slot_mask, rank_full, 0.0).astype(jnp.bfloat16)
    up_values = up_values + jnp.dot(rank_portion, adapter_up[0], preferred_element_type=jnp.float32)
    hidden_act = (jax.nn.silu(gate_values) * up_values).astype(jnp.bfloat16)
    partial_value = jnp.dot(hidden_act, down_weight[0], preferred_element_type=jnp.float32).reshape(
        sources, per_source, width
    )
    result = lax.psum_scatter(
        partial_value.astype(jnp.bfloat16), "hidden", scatter_dimension=2, tiled=True
    ).astype(jnp.float32)
    returned = lax.all_to_all(
        result.astype(jnp.bfloat16), "expert", split_axis=0, concat_axis=0, tiled=True
    ).astype(result.dtype)
    picked = jnp.take(
        returned.reshape(experts * expert_capacity, shard_width), slot_index, axis=0
    ).reshape(tok_rows, choices_each, shard_width)
    mixed = jnp.sum(picked * route_weight[:, :, None], axis=1)
    return mixed.astype(jnp.bfloat16)


def solution(mesh):
    in_specs = (
        P(("parts", "expert", "rep"), "hidden"),
        P(("parts", "expert", "rep"), None),
        P(("parts", "expert", "rep"), None),
        P(("parts", "expert", "rep"), None),
        P("expert", None, "hidden"),
        P("expert", None, "hidden"),
        P("expert", "hidden", None),
        P("expert", "hidden", None),
        P("expert", None, "hidden"),
    )
    out_specs = P(("parts", "expert", "rep"), "hidden")
    return jax.shard_map(local, mesh=mesh, in_specs=in_specs, out_specs=out_specs, check_vma=False)
```

profile of v0, /device:TPU:0, one launch (start us, length us, event | category | flops | bytes accessed | tf_op | source)
XLA Modules:
  0.0 145.6 jit_solution(6415885413791973828)
XLA Ops:
  6.5 0.8 copy.28
  7.4 0.1 reshape.157
  7.5 0.1 fusion.16
  7.6 0.8 select_reduce_fusion.3
  8.4 0.1 copy.31
  8.5 0.2 reduce_window_sum.11
  8.7 0.2 select_reduce_fusion.1
  8.8 0.1 select_reduce_fusion
  9.0 0.7 convert_element_type.62
  9.6 6.3 %all-to-all-start.1 = ((bf16[4,1,48]{2,1,0:T(2,128)(2,1)}), bf16[4,1,48]{2,1,0:T(2,128)(2,1)S(1)}, u32[]{:S(2)}, u32[]{:S(2)}) async-start(bf16[4,1,48]{2,1,0:T(2,128)(2,1)} %convert_element_type.62), calls=%async_computation.1 | async-start | bytes 4096 | tf_op jit(solution)/shard_map/all_to_all | solution.py:57
  16.0 8.6 %all_gather.6 = bf16[64,4096]{1,0:T(8,128)(2,1)S(1)} all-gather(bf16[64,2048]{1,0:T(8,128)(2,1)} %param.9), channel_id=1, replica_groups=mesh['parts'=2,'expert'=4,'hidden'=2,'rep'=2] {'hidden'}, dimensions={1}, use_global_device_ids=true | all-gather | bytes 786432 | tf_op jit(solution)/shard_map/all_gather | solution.py:27
  24.6 2.0 %convolution_convert_fusion = bf16[192,4096]{1,0:T(8,128)(2,1)} fusion(bf16[64,4096]{1,0:T(8,128)(2,1)S(1)} %all_gather.6, s32[128]{0:T(128)S(1)} %get-tuple-element.8, s32[128]{0:T(128)S(1)} %get-tuple-element.7), kind=kOutput, calls=%fused_computation.8 | convolution fusion | flops 104640512 | bytes 2098176 | tf_op jit(solution)/shard_map/dot_general | solution.py:42
  26.7 4.8 %all-to-all-start = ((bf16[4,48,4096]{2,1,0:T(8,128)(2,1)}), bf16[4,48,4096]{2,1,0:T(8,128)(2,1)S(1)}, u32[]{:S(2)}, u32[]{:S(2)}) async-start(bf16[4,48,4096]{2,1,0:T(8,128)(2,1)} %bitcast), calls=%async_computation | async-start | bytes 3145728 | tf_op jit(solution)/shard_map/all_to_all | solution.py:56
  31.5 0.7 all-gather.3.cloned.1.call-update
  32.3 0.1 reshape.162
  32.4 34.7 %all-to-all-done = bf16[4,48,4096]{2,1,0:T(8,128)(2,1)S(1)} async-done(((bf16[4,48,4096]{2,1,0:T(8,128)(2,1)}), bf16[4,48,4096]{2,1,0:T(8,128)(2,1)S(1)}, u32[]{:S(2)}, u32[]{:S(2)}) %all-to-all-start) | async-done | bytes 1572896 | tf_op jit(solution)/shard_map/all_to_all | solution.py:56
  67.0 4.2 %fusion.2 = f32[192,768]{1,0:T(8,128)S(1)} fusion(bf16[192,4096]{1,0:T(8,128)(2,1)S(1)} %bitcast.36, bf16[1,4096,768]{2,1,0:T(8,128)(2,1)} %param.14), kind=kOutput, calls=%fused_computation.3 | convolution fusion | flops 1207959552 | bytes 8454144 | tf_op jit(solution)/shard_map/dot_general | solution.py:62
  71.2 5.0 %fusion.4 = f32[192,768]{1,0:T(8,128)} fusion(bf16[192,4096]{1,0:T(8,128)(2,1)S(1)} %bitcast.37, bf16[1,4096,768]{2,1,0:T(8,128)(2,1)} %param.13), kind=kOutput, calls=%fused_computation.5 | convolution fusion | flops 1207959552 | bytes 8454144 | tf_op jit(solution)/shard_map/dot_general | solution.py:61
  76.2 2.2 %fusion.10 = bf16[192,768]{1,0:T(8,128)(2,1)S(1)} fusion(f32[192,768]{1,0:T(8,128)S(1)} %fusion.2, bf16[192,4096]{1,0:T(8,128)(2,1)S(1)} %bitcast.38, bf16[1,4096,128]{2,1,0:T(8,128)(2,1)} %all-gather.3.cloned.1.call-done, f32[192,768]{1,0:T(8,128)} %fusion.4, bf16[1,128,768]{2,1,0:T(8,128)(2,1)S(1)} %copy-done, s32[128]{0:T(128)S(1)} %and_select_fusion, ...), kind=kOutput, calls=%fused_computation.11 | convolution fusion | flops 240181248 | bytes 4293888 | tf_op jit(solution)/shard_map/dot_general | solution.py:68
  78.4 5.3 %fusion.6 = bf16[4,48,4096]{2,1,0:T(8,128)(2,1)} fusion(bf16[4,48,768]{2,1,0:T(8,128)(2,1)S(1)} %bitcast.39, bf16[1,768,4096]{2,1,0:T(8,128)(2,1)} %param.15), kind=kOutput, calls=%fused_computation.7 | convolution fusion | flops 1208745984 | bytes 8159232 | tf_op jit(solution)/shard_map/dot_general | solution.py:70
  83.8 25.4 %reduce-scatter.2.cloned.1.call-done = bf16[4,48,2048]{2,1,0:T(8,128)(2,1)} async-done(((bf16[4,48,4096]{2,1,0:T(8,128)(2,1)}), bf16[4,48,2048]{2,1,0:T(8,128)(2,1)}) %reduce-scatter.2.cloned.1.call-update) | async-done | bytes 786448 | tf_op jit(solution)/shard_map/reduce_scatter | solution.py:73
  109.2 4.6 %all-to-all-start.2 = ((bf16[4,48,2048]{2,1,0:T(8,128)(2,1)}), bf16[4,48,2048]{2,1,0:T(8,128)(2,1)S(1)}, u32[]{:S(2)}, u32[]{:S(2)}) async-start(bf16[4,48,2048]{2,1,0:T(8,128)(2,1)} %reduce-scatter.2.cloned.1.call-done), calls=%async_computation.3 | async-start | bytes 1572864 | tf_op jit(solution)/shard_map/all_to_all | solution.py:76
  113.8 0.1 reduce_sum.50
  113.9 0.1 copy.33
  114.0 0.1 mul.55
  114.2 0.1 copy.30
  114.4 0.1 copy.34
  114.5 19.2 %all-to-all-done.2 = bf16[4,48,2048]{2,1,0:T(8,128)(2,1)S(1)} async-done(((bf16[4,48,2048]{2,1,0:T(8,128)(2,1)}), bf16[4,48,2048]{2,1,0:T(8,128)(2,1)S(1)}, u32[]{:S(2)}, u32[]{:S(2)}) %all-to-all-start.2) | async-done | bytes 786464 | tf_op jit(solution)/shard_map/all_to_all | solution.py:76
  133.7 0.2 bitcast_convert_fusion
  133.9 1.0 gather_fusion
  134.9 0.6 gather.7
  135.6 3.2 %multiply_reduce_fusion = bf16[64,2048]{1,0:T(8,128)(2,1)} fusion(f32[64,2,2048]{2,1,0:T(2,128)S(1)} %gather.7, pred[64,2]{1,0:T(8,128)(4,1)S(1)} %copy.30, f32[64,2]{1,0:T(8,128)S(1)} %copy.34), kind=kLoop, calls=%fused_computation.16 | loop fusion | flops 655360 | bytes 1311360 | tf_op jit(solution)/shard_map/reduce_sum | solution.py:82
  (22 shorter events, 0.2 us)
Async XLA Ops:
  6.5 69.7 %copy-start = (bf16[1,128,768]{2,1,0:T(8,128)(2,1)S(1)}, bf16[1,128,768]{2,1,0:T(8,128)(2,1)}, u32[]{:S(2)}) copy-start(bf16[1,128,768]{2,1,0:T(8,128)(2,1)} %param.17) | copy-start | bytes 589828
  9.6 17.0 %all-to-all-start.1 = ((bf16[4,1,48]{2,1,0:T(2,128)(2,1)}), bf16[4,1,48]{2,1,0:T(2,128)(2,1)S(1)}, u32[]{:S(2)}, u32[]{:S(2)}) async-start(bf16[4,1,48]{2,1,0:T(2,128)(2,1)} %convert_element_type.62), calls=%async_computation.1 | async-start | bytes 4096 | tf_op jit(solution)/shard_map/all_to_all | solution.py:57
  26.7 40.4 %all-to-all-start = ((bf16[4,48,4096]{2,1,0:T(8,128)(2,1)}), bf16[4,48,4096]{2,1,0:T(8,128)(2,1)S(1)}, u32[]{:S(2)}, u32[]{:S(2)}) async-start(bf16[4,48,4096]{2,1,0:T(8,128)(2,1)} %bitcast), calls=%async_computation | async-start | bytes 3145728 | tf_op jit(solution)/shard_map/all_to_all | solution.py:56
  31.5 44.7 %all-gather.3.cloned.1.call-start = ((), (), s32[]{:S(2)}) async-start(), calls=%async_computation.5 | async-start | bytes 1572864 | tf_op jit(solution)/shard_map/all_gather | solution.py:55
  32.2 77.0 %reduce-scatter.2.cloned.1.call-start = ((), (), s32[]{:S(2)}) async-start(), calls=%async_computation.4 | async-start | bytes 2359296 | tf_op jit(solution)/shard_map/reduce_scatter | solution.py:73
  83.7 30.2 %copy-start.1 = (s32[64,2]{0,1:T(2,128)S(1)}, s32[64,2]{0,1:T(2,128)}, u32[]{:S(2)}) copy-start(s32[64,2]{0,1:T(2,128)} %param.10) | copy-start | bytes 1540
  83.7 30.6 %copy-start.2 = (f32[64,2]{0,1:T(2,128)S(1)}, f32[64,2]{0,1:T(2,128)}, u32[]{:S(2)}) copy-start(f32[64,2]{0,1:T(2,128)} %param.11) | copy-start | bytes 1540
  109.2 24.6 %all-to-all-start.2 = ((bf16[4,48,2048]{2,1,0:T(8,128)(2,1)}), bf16[4,48,2048]{2,1,0:T(8,128)(2,1)S(1)}, u32[]{:S(2)}, u32[]{:S(2)}) async-start(bf16[4,48,2048]{2,1,0:T(8,128)(2,1)} %reduce-scatter.2.cloned.1.call-done), calls=%async_computation.3 | async-start | bytes 1572864 | tf_op jit(solution)/shard_map/all_to_all | solution.py:76
Sparse Core Ops, SparseCore 0:
  33.8 22.7 all-gather.2
  83.9 25.2 reduce-scatter.1
where the time goes:
time: 146 us
  waiting for transfers between devices  80 us (55%)
  matrix products  18.7 us (13%)
  starting transfers between devices  15.8 us (11%)
  between operations  13.5 us (9%)
  blocking collectives  8.63 us (6%)
  other arithmetic  4.79 us (3%)
  local copies, waits for them, and re-layouts  4.06 us (3%)
    all_to_all x1, waiting for transfers between devices, local(): lax.all_to_all(send_rows, 'expert', split_axis=0, concat_axis=0, tiled=True)  34.7 us
    reduce_scatter x1, waiting for transfers between devices, local(): lax.psum_scatter(partial_value.astype(jnp.bfloat16), 'hidden', scatter_di...  25.4 us
    all_to_all x1, waiting for transfers between devices, local(): lax.all_to_all(result.astype(jnp.bfloat16), 'expert', split_axis=0, conca...  19.2 us
    all_gather x1, blocking collectives, local(): source_rows = lax.all_gather(tokens, 'hidden', axis=1, tiled=True)  8.63 us
    all_to_all x1, starting transfers between devices, local(): lax.all_to_all(send_codes, 'expert', split_axis=0, concat_axis=0, tiled=T...  6.35 us
    dot_general x1, matrix products, local(): jnp.dot(hidden_act, down_weight[0], preferred_element_type=jnp.float32)  5.34 us
    dot_general x1, matrix products, local(): jnp.dot(flattened, gate_weight[0], preferred_element_type=jnp.float32)  4.98 us
    all_to_all x1, starting transfers between devices, local(): lax.all_to_all(send_rows, 'expert', split_axis=0, concat_axis=0, tiled=True)  4.81 us
  transfers between devices with their start and end apart: 5, of which 3 were waited for; matrix products, arithmetic and copies ran while one was open for 8% of the time, Pallas kernels for 0%

commit v1 on v0

v1 whole, which is shorter than its diff:
```python
import jax
import jax.numpy as jnp
from jax import lax
from jax.experimental import pallas as pl
from jax.experimental.pallas import tpu as pltpu
from jax.sharding import PartitionSpec as P


RANK = 8
USER_TOK = 8
LANES = 128
ROWS = 16
LIMIT = 12 << 20
VMEM = pl.BlockSpec(memory_space=pltpu.VMEM)
ANY = pl.BlockSpec(memory_space=pl.ANY)
HBM = pl.BlockSpec(memory_space=pltpu.HBM)
F32 = jnp.float32
BF16 = jnp.bfloat16


def call(body, outs, ins, in_specs=None, scratch=(), flops=0):
    return pl.pallas_call(
        body,
        out_shape=outs,
        in_specs=in_specs or [VMEM] * len(ins),
        out_specs=[VMEM] * len(outs),
        scratch_shapes=list(scratch),
        compiler_params=pltpu.CompilerParams(vmem_limit_bytes=LIMIT),
        cost_estimate=pl.CostEstimate(flops=flops, bytes_accessed=flops // 160, transcendentals=0),
    )(*ins)


def iota(shape, dim):
    return lax.broadcasted_iota(jnp.int32, shape, dim)


def dot(a, b, dims=((1,), (0,))):
    return lax.dot_general(a, b, (dims, ((), ())), preferred_element_type=F32)


def swaps(count):
    return count & (count - 1) == 0


def target(index, step, count):
    if swaps(count):
        return index ^ step if isinstance(index, int) else lax.bitwise_xor(index, step)
    return (index + step) % count if isinstance(index, int) else lax.rem(index + step, count)


def source(index, step, count):
    return target(index, step if swaps(count) else count - step, count)


def permute(value, axis, step, back=False):
    count = lax.axis_size(axis)
    pairs = [(i, target(i, step, count)) for i in range(count)]
    if back:
        pairs = [(j, i) for i, j in pairs]
    return lax.ppermute(value, axis, pairs)


def routing(ids, experts):
    choices, rows = ids.shape
    padded = -(-experts // ROWS) * ROWS
    expert_of = iota((padded, rows), 0)
    chosen = jnp.zeros((padded, rows), F32)
    for k in range(choices):
        chosen = chosen + jnp.where(ids[k : k + 1, :] == expert_of, 1.0, 0.0)
    before = jnp.where(iota((rows, rows), 0) < iota((rows, rows), 1), 1.0, 0.0)
    place = dot(chosen.astype(BF16), before.astype(BF16))
    return expert_of, chosen, place


def row_of(table, expert_of, expert):
    return jnp.sum(jnp.where(expert_of == expert, table, 0.0), axis=0, keepdims=True)


def selection(chosen, place, expert_of, expert, capacity):
    rows = chosen.shape[1]
    hit = row_of(chosen, expert_of, expert)
    at = row_of(place, expert_of, expert)
    return jnp.where((iota((capacity, rows), 0).astype(F32) == at) & (hit > 0.0), 1.0, 0.0)


class Piece:
    def __init__(self, step, lo, hi, cap, coded):
        self.step, self.lo, self.hi, self.cap, self.coded = step, lo, hi, cap, coded
        self.across = (hi - lo) // LANES
        self.length = cap * self.across + (ROWS if coded else 0)
        self.shape = jax.ShapeDtypeStruct((self.length, LANES), BF16)

    def covers(self, lo, hi):
        return self.lo <= lo and hi <= self.hi

    def place(self, r, c):
        start = (r * self.across + c) * ROWS
        return slice(start, start + ROWS)

    def store(self, ref, lo, value):
        first = (lo - self.lo) // LANES
        for r in range(self.cap // ROWS):
            for c in range(value.shape[1] // LANES):
                ref[self.place(r, first + c), :] = value[
                    r * ROWS : (r + 1) * ROWS, c * LANES : (c + 1) * LANES
                ]

    def load(self, ref, lo, hi):
        first, last = (lo - self.lo) // LANES, (hi - self.lo) // LANES
        rows = []
        for r in range(self.cap // ROWS):
            tiles = [ref[self.place(r, c), :] for c in range(first, last)]
            rows.append(jnp.concatenate(tiles, axis=1))
        return jnp.concatenate(rows, axis=0)

    def codes(self, ref):
        return ref[self.length - ROWS : self.length, :].astype(F32)[0:1, : self.cap]


def gather(pieces, refs, lo, hi):
    return jnp.concatenate(
        [p.load(r, lo, hi) for p, r in zip(pieces, refs) if p.covers(lo, hi)], axis=0
    )


def local(
    tokens,
    route_ids,
    route_weight,
    user_slot,
    gate_weight,
    up_weight,
    down_weight,
    adapter_down,
    adapter_up,
):
    experts = lax.axis_size("expert")
    hiddens = lax.axis_size("hidden")
    tok_rows, choices = route_ids.shape
    limit = tok_rows * choices * 3 // (2 * experts)
    cap = -(-limit // ROWS) * ROWS
    part = tokens.shape[1]
    half, quarter = part // 2, part // 4
    units = gate_weight.shape[2]
    adapt_cols = adapter_down.shape[2]
    slots = adapt_cols // RANK
    total = experts * cap
    users = user_slot.shape[0]
    steps = list(range(1, experts))
    last = experts - 1
    segments = [(0, half), (half, part)]

    there = []
    for k in range(experts):
        if k and k == last:
            there += [Piece(k, 0, half, cap, True), Piece(k, half, part, cap, False)]
        else:
            there += [Piece(k, 0, part, cap, True)]
    home, first = [], experts // 2
    for k in range(experts):
        if k and k == first:
            home += [Piece(k, 0, quarter, cap, False), Piece(k, quarter, part, cap, False)]
        else:
            home += [Piece(k, 0, part, cap, False)]
    home_segments = [(0, quarter), (quarter, half), (half, part)]
    lead = max(0, min(i for i, p in enumerate(home) if p.step == first))

    def dispatch(ids_in, slot_in, tok_in, *refs):
        *outs, ids, slot, tok, sems = refs
        copies = [
            pltpu.make_async_copy(a, b, sems.at[i])
            for i, (a, b) in enumerate([(ids_in, ids), (slot_in, slot), (tok_in, tok)])
        ]
        for c in copies:
            c.start()
        me = lax.axis_index("expert")
        copies[0].wait()
        copies[1].wait()
        expert_of, chosen, place = routing(ids[...], experts)
        user_at = jnp.where(
            iota((users, tok_rows), 1) // USER_TOK == iota((users, tok_rows), 0), 1.0, 0.0
        )
        slots_of = dot(slot[...].astype(F32).astype(BF16), user_at.astype(BF16))
        picks, codes = [], []
        for k in range(experts):
            e = target(me, k, experts)
            pick = selection(chosen, place, expert_of, e, cap)
            pick = jnp.concatenate([pick, jnp.zeros((LANES - cap, tok_rows), F32)]).astype(BF16)
            own = row_of(slots_of, iota(slots_of.shape, 0), e)
            own = jnp.broadcast_to(own, (ROWS, tok_rows)).astype(BF16)
            codes.append(dot(own, pick, ((1,), (1,))).astype(BF16))
            picks.append(pick[:cap])
        copies[2].wait()
        rows = dot(jnp.concatenate(picks, axis=0), tok[...]).astype(BF16)
        for p, ref in zip(there, outs):
            p.store(ref, p.lo, rows[p.step * cap : (p.step + 1) * cap, p.lo : p.hi])
            if p.coded:
                ref[p.length - ROWS : p.length, :] = codes[p.step]

    sent = call(
        dispatch,
        [p.shape for p in there],
        (route_ids.T, user_slot.T, tokens),
        flops=10**10,
        in_specs=[HBM] * 3,
        scratch=[
            pltpu.VMEM(route_ids.T.shape, jnp.int32),
            pltpu.VMEM(user_slot.T.shape, jnp.int32),
            pltpu.VMEM(tokens.shape, BF16),
            pltpu.SemaphoreType.DMA((3,)),
        ],
    )

    def load(*refs):
        sems = refs[6]
        copies = [pltpu.make_async_copy(refs[i], refs[3 + i], sems.at[i]) for i in range(3)]
        for c in copies:
            c.start()
        for c in copies:
            c.wait()

    weights = (gate_weight[0], up_weight[0], down_weight[0])
    gate_w, up_w, down_w = pl.pallas_call(
        load,
        out_shape=[pltpu.VMEM(w.shape, w.dtype) for w in weights],
        in_specs=[ANY] * 3,
        out_specs=[VMEM] * 3,
        scratch_shapes=[pltpu.SemaphoreType.DMA((3,))],
        compiler_params=pltpu.CompilerParams(vmem_limit_bytes=4 << 20),
        name="load",
    )(*weights)

    arrived = [s if p.step == 0 else permute(s, "expert", p.step) for p, s in zip(there, sent)]
    others = [[permute(a, "hidden", d) for a in arrived] for d in range(1, hiddens)]

    def within(lo, hi, values):
        kept = [i for i, p in enumerate(there) if p.covers(lo, hi)]
        return [there[i] for i in kept], [values[i] for i in kept]

    def multiply(x, gate_ref, up_ref, start):
        at = pl.ds(pl.multiple_of(start, LANES), x.shape[1])
        return dot(x, gate_ref[at, :]), dot(x, up_ref[at, :])

    acc = [jax.ShapeDtypeStruct((total, units), F32)] * 2

    def row_codes(pieces, refs):
        return jnp.concatenate([p.codes(r) for p, r in zip(pieces, refs) if p.coded], axis=1)

    def slot_mask(codes):
        return (iota((adapt_cols, total), 0) // RANK).astype(F32) == codes

    ranks, pieces_a, values_a = None, *within(*segments[0], arrived)
    for s, (lo, hi) in enumerate(segments):
        pieces, values = within(lo, hi, arrived)

        def rank_step(*refs, lo=lo, hi=hi, s=s, pieces=pieces):
            x = gather(pieces, refs, lo, hi)
            full = dot(refs[len(pieces)][lo:hi, :], x, ((0,), (1,)))
            if s:
                full = full + refs[len(pieces) + 1][...]
                codes = row_codes(pieces_a, refs[len(pieces) + 2 :])
                full = jnp.where(slot_mask(codes), full, 0.0)
                full = jnp.sum(full.reshape(slots, RANK, total), axis=0)
            refs[-1][...] = full

        extra = () if ranks is None else (ranks, *values_a)
        shape = (adapt_cols if s == 0 else RANK, total)
        (ranks,) = call(
            rank_step, [jax.ShapeDtypeStruct(shape, F32)], (*values, adapter_down[0], *extra)
        )
    rank_others = [permute(ranks, "hidden", d) for d in range(1, hiddens)]

    sums = None
    for s, (lo, hi) in enumerate(segments):
        pieces, values = within(lo, hi, arrived)

        def own_step(*refs, lo=lo, hi=hi, s=s, pieces=pieces):
            n = len(pieces)
            gate, up = multiply(
                gather(pieces, refs, lo, hi),
                refs[n],
                refs[n + 1],
                lax.axis_index("hidden") * part + lo,
            )
            if s:
                gate, up = gate + refs[n + 2][...], up + refs[n + 3][...]
            refs[-2][...] = gate
            refs[-1][...] = up

        sums = call(own_step, acc, (*values, gate_w, up_w, *(sums or ())))

    def partner_parts(refs, lo, hi, gate_ref, up_ref, gate, up, pieces):
        for d in range(1, hiddens):
            base = source(lax.axis_index("hidden"), d, hiddens) * part + lo
            x = gather(pieces, refs[(d - 1) * len(pieces) : d * len(pieces)], lo, hi)
            g, u = multiply(x, gate_ref, up_ref, base)
            gate, up = gate + g, up + u
        return gate, up

    lo, hi = segments[0]
    pieces = within(lo, hi, there)[0]
    values = [v for o in others for v in within(lo, hi, o)[1]]

    def other_step(*refs):
        gate_ref, up_ref, gate_in, up_in, gate_out, up_out = refs[-6:]
        gate_out[...], up_out[...] = partner_parts(
            refs, *segments[0], gate_ref, up_ref, gate_in[...], up_in[...], pieces_a
        )

    sums = call(other_step, acc, (*values, gate_w, up_w, *sums))

    pieces_b = within(*segments[1], there)[0]
    values = [v for o in others for v in within(*segments[1], o)[1]]

    def store_down(act_rows, down_ref, base, lo, hi, pieces, refs, first):
        at = pl.ds(pl.multiple_of(base + lo, LANES), hi - lo)
        y = dot(act_rows, down_ref[:, at]).astype(BF16)
        for p, ref in zip(pieces, refs):
            if p.covers(lo, hi):
                n = p.step * cap - first
                p.store(ref, lo, y[n : n + cap])

    n_b = len(values)

    def activate(*refs):
        codes = row_codes(pieces_a, refs[n_b : n_b + len(pieces_a)])
        rest = refs[n_b + len(pieces_a) :]
        rank_refs, rest = rest[:hiddens], rest[hiddens:]
        gate_in, up_in, gate_ref, up_ref, factor, down_ref, act_ref = rest[:7]
        rank = rank_refs[0][...]
        for r in rank_refs[1:]:
            rank = rank + r[...]
        rank = jnp.broadcast_to(rank[None], (slots, RANK, total)).reshape(adapt_cols, total)
        rank = jnp.where(slot_mask(codes), rank, 0.0).astype(BF16)
        up = up_in[...] + dot(rank, factor[...], ((0,), (0,)))
        gate, up = partner_parts(
            refs, *segments[1], gate_ref, up_ref, gate_in[...], up, pieces_b
        )
        act = (gate / (1.0 + jnp.exp(-gate)) * up).astype(BF16)
        act_ref[...] = act
        p = home[lead]
        for d in range(1, hiddens):
            base = target(lax.axis_index("hidden"), d, hiddens) * part
            rows = act[p.step * cap : (p.step + 1) * cap]
            store_down(rows, down_ref, base, p.lo, p.hi, [p], [rest[6 + d]], p.step * cap)
        base = lax.axis_index("hidden") * part
        store_down(rows, down_ref, base, p.lo, p.hi, [p], [rest[-1]], p.step * cap)

    act, *lead_sent, lead_kept = call(
        activate,
        [jax.ShapeDtypeStruct((total, units), BF16)] + [home[lead].shape] * hiddens,
        (
            *values,
            *within(*segments[0], arrived)[1],
            ranks,
            *rank_others,
            *sums,
            gate_w,
            up_w,
            adapter_up[0],
            down_w,
        ),
    )

    def down(step, pieces):
        def body(act_ref, down_ref, *outs):
            base = target(lax.axis_index("hidden"), step, hiddens) * part if step else (
                lax.axis_index("hidden") * part
            )
            for lo, hi in home_segments:
                if any(p.covers(lo, hi) for p in pieces):
                    store_down(act_ref[...], down_ref, base, lo, hi, pieces, outs, 0)

        return call(body, [p.shape for p in pieces], (act, down_w))

    rest = [i for i in range(len(home)) if i != lead]
    sent_home = []
    for d in range(1, hiddens):
        out = down(d, [home[i] for i in rest])
        sent_home.append({lead: lead_sent[d - 1], **dict(zip(rest, out))})
    kept = {lead: lead_kept, **dict(zip(rest, down(0, [home[i] for i in rest])))}
    order = [lead] + ([lead + 1] if lead else [])
    order += [i for i in reversed(range(len(home))) if i not in order]
    summed = {
        i: [permute(sent_home[d - 1][i], "hidden", d) for d in range(1, hiddens)]
        for i in order
    }

    def add(*refs):
        y = refs[0][...].astype(F32)
        for r in refs[1:-1]:
            y = y + r[...].astype(F32)
        refs[-1][...] = y.astype(BF16)

    returned = {}
    for i in order:
        if home[i].step:
            (y,) = call(add, [home[i].shape], (kept[i], *summed[i]))
            returned[i] = permute(y, "expert", home[i].step, back=True)

    final = max([i for i in range(len(home)) if home[i].step not in (0, first)], default=0)
    early = [i for i in range(len(home)) if home[i].step and i != final]

    def mixing(ids, weight, chosen_steps):
        me = lax.axis_index("expert")
        expert_of, chosen, place = routing(ids, experts)
        weights_of = jnp.zeros(chosen.shape, F32)
        for j in range(choices):
            weights_of = weights_of + jnp.where(ids[j : j + 1] == expert_of, weight[j : j + 1], 0.0)
        mix = []
        for k in chosen_steps:
            e = target(me, k, experts)
            mix.append(
                selection(chosen, place, expert_of, e, cap) * row_of(weights_of, expert_of, e)
            )
        mix = jnp.concatenate(mix, axis=0)
        terms = []
        for _ in range(3):
            terms.append(mix.astype(BF16))
            mix = mix - terms[-1].astype(F32)
        return terms

    def mixed_sum(terms, rows):
        value = dot(terms[0], rows, ((0,), (0,)))
        for t in terms[1:]:
            value = value + dot(t, rows, ((0,), (0,)))
        return value

    early_steps = [0] + [k for k in steps if any(home[i].step == k for i in early)]

    def combine(*refs):
        own, others_in = refs[2 : 2 + hiddens], refs[2 + hiddens : -4]
        terms = mixing(refs[0][...], refs[1][...], early_steps)
        for lo, hi in home_segments:
            y = home[0].load(own[0], lo, hi).astype(F32)
            for r in own[1:]:
                y = y + home[0].load(r, lo, hi).astype(F32)
            rows = [y.astype(BF16)]
            rows += [
                home[i].load(r, lo, hi) for i, r in zip(early, others_in) if home[i].covers(lo, hi)
            ]
            refs[-4][:, lo:hi] = mixed_sum(terms, jnp.concatenate(rows, axis=0))
        for ref, t in zip(refs[-3:], mixing(refs[0][...], refs[1][...], [home[final].step])):
            ref[...] = t

    mixed, *final_terms = call(
        combine,
        [jax.ShapeDtypeStruct((tok_rows, part), F32)]
        + [jax.ShapeDtypeStruct((cap, tok_rows), BF16)] * 3,
        (route_ids.T, route_weight.T, kept[0], *summed[0], *[returned[i] for i in early]),
    )

    def finish(partial, *refs):
        terms, out = [r[...] for r in refs[:3]], refs[-1]
        for lo, hi in home_segments:
            value = partial[:, lo:hi]
            if final:
                value = value + mixed_sum(terms, home[final].load(refs[3], lo, hi))
            out[:, lo:hi] = value.astype(BF16)

    (result,) = call(
        finish,
        [jax.ShapeDtypeStruct((tok_rows, part), BF16)],
        (mixed, *final_terms, *([returned[final]] if final else [])),
    )
    return result


def solution(mesh):
    in_specs = (
        P(("parts", "expert", "rep"), "hidden"),
        P(("parts", "expert", "rep"), None),
        P(("parts", "expert", "rep"), None),
        P(("parts", "expert", "rep"), None),
        P("expert", None, "hidden"),
        P("expert", None, "hidden"),
        P("expert", "hidden", None),
        P("expert", "hidden", None),
        P("expert", None, "hidden"),
    )
    out_specs = P(("parts", "expert", "rep"), "hidden")

    return jax.shard_map(local, mesh=mesh, in_specs=in_specs, out_specs=out_specs, check_vma=False)
```

time: 146 us -> 63.3 us (0.43)
  waiting for transfers between devices: 80 us -> 21.9 us
  matrix products: 18.7 us -> 0 us
  between operations: 13.5 us -> 0.27 us
  starting transfers between devices: 15.8 us -> 27.5 us
  Pallas kernels: 0 us -> 9.74 us
  blocking collectives: 8.63 us -> 0 us
  other arithmetic: 4.79 us -> 0.01 us
    all_to_all x3 -> x0, waiting for transfers between devices: 53.9 us -> none  [the longest x1 34.7 us: local(): lax.all_to_all(send_rows, 'expert', split_axis=0, concat_axis=0, tiled=True)]
    ppermute x0 -> x19, starting transfers between devices: none -> 27.5 us  [permute(): return lax.ppermute(value, axis, pairs)]
    reduce_scatter x1 -> x0, waiting for transfers between devices: 25.4 us -> none  [local(): lax.psum_scatter(partial_value.astype(jnp.bfloat16), 'hidden', scatter_di...]
    ppermute x0 -> x19, waiting for transfers between devices: none -> 21.9 us  [permute(): return lax.ppermute(value, axis, pairs)]
    dot_general x5 -> x0, matrix products: 18.7 us -> none  [the longest x1 5.34 us: local(): jnp.dot(hidden_act, down_weight[0], preferred_element_type=jnp.float32)]
    all_to_all x3 -> x0, starting transfers between devices: 15.8 us -> none  [the longest x1 6.35 us: local(): lax.all_to_all(send_codes, 'expert', split_axis=0, concat_axis=0, tiled=T...]
    pallas_call x0 -> x16, Pallas kernels: none -> 9.74 us  [the longest x15 8.46 us: call(): pl.pallas_call(body, out_shape=outs, in_specs=in_specs or [VMEM] * len(in...]
    all_gather x1 -> x0, blocking collectives: 8.63 us -> none  [local(): source_rows = lax.all_gather(tokens, 'hidden', axis=1, tiled=True)]
  transfers between devices with their start and end apart: 5 -> 19, of which waited for: 3 -> 7; matrix products, arithmetic and copies ran while one was open for 8% -> 0% of each run, Pallas kernels for 0% -> 9%
where the time goes in v1:
time: 63.3 us; the launch traced here: 63.2 us
  starting transfers between devices  27.5 us (43%)
  waiting for transfers between devices  21.9 us (35%)
  Pallas kernels  9.74 us (15%)
  local copies, waits for them, and re-layouts  3.76 us (6%)
    ppermute x19, starting transfers between devices, permute(): return lax.ppermute(value, axis, pairs)  27.5 us
    ppermute x19, waiting for transfers between devices, permute(): return lax.ppermute(value, axis, pairs)  21.9 us
    pallas_call x15, Pallas kernels, call(): pl.pallas_call(body, out_shape=outs, in_specs=in_specs or [VMEM] * len(in...  8.46 us
    unnamed x26, local copies, waits for them, and re-layouts  3.76 us
    pallas_call x1, Pallas kernels, local(): pl.pallas_call(load, out_shape=[pltpu.VMEM(w.shape, w.dtype) for w in wei...  1.29 us
  transfers between devices with their start and end apart: 19, of which 7 were waited for; matrix products, arithmetic and copies ran while one was open for 0% of the time, Pallas kernels for 9%

profile of v1, /device:TPU:0, one launch (start us, length us, event | category | flops | bytes accessed | tf_op | source)
XLA Modules:
  0.0 63.2 jit_solution(6863392276301504981)
XLA Ops:
  0.0 0.8 %copy-done.2 = s32[64,2]{0,1:T(2,128)S(1)} copy-done((s32[64,2]{0,1:T(2,128)S(1)}, s32[64,2]{0,1:T(2,128)}, u32[]{:S(2)}) %copy-start.2) | copy-done | bytes 536
  0.8 1.4 %copy-done.5 = bf16[64,2048]{1,0:T(8,128)(2,1)S(1)} copy-done((bf16[64,2048]{1,0:T(8,128)(2,1)S(1)}, bf16[64,2048]{1,0:T(8,128)(2,1)}, u32[]{:S(2)}) %copy-start.5) | copy-done | bytes 262168
  2.2 1.5 %copy-done.6 = s32[8,4]{0,1:T(4,128)S(1)} copy-done((s32[8,4]{0,1:T(4,128)S(1)}, s32[8,4]{0,1:T(4,128)}, u32[]{:S(2)}) %copy-start.6) | copy-done | bytes 152
  3.7 0.7 %shard_map.91 = (bf16[784,128]{1,0:T(8,128)(2,1)S(1)}, bf16[784,128]{1,0:T(8,128)(2,1)S(1)}, bf16[784,128]{1,0:T(8,128)(2,1)S(1)}, bf16[400,128]{1,0:T(8,128)(2,1)S(1)}, bf16[384,128]{1,0:T(8,128)(2,1)S(1)}) custom-call(s32[2,64]{1,0:T(2,128)S(1)} %bitcast.20, s32[4,8]{1,0:T(4,128)S(1)} %bitcast.23, bf16[64,2048]{1,0:T(8,128)(2,1)S(1)} %copy-done.5), custom_call_target="tpu_custom_call" | custom-call | flops 10000000000 | bytes 62500000 | tf_op jit(solution)/shard_map/pallas_call | solution.py:22
  4.4 3.1 %collective-permute-start.1 = (bf16[784,128]{1,0:T(8,128)(2,1)S(1)}, bf16[784,128]{1,0:T(8,128)(2,1)S(1)}, u32[]{:S(2)}, u32[]{:S(2)}) collective-permute-start(bf16[784,128]{1,0:T(8,128)(2,1)S(1)} %get-tuple-element.35), channel_id=1, source_target_pairs={{0,4},{4,0},{8,12},{12,8},{1,5},{5,1},{9,13},{13,9},{2,6},{6,2},{1... | collective-permute-start | bytes 602120 | tf_op jit(solution)/shard_map/ppermute | solution.py:60
  7.5 2.6 %collective-permute-start.3 = (bf16[784,128]{1,0:T(8,128)(2,1)S(1)}, bf16[784,128]{1,0:T(8,128)(2,1)S(1)}, u32[]{:S(2)}, u32[]{:S(2)}) collective-permute-start(bf16[784,128]{1,0:T(8,128)(2,1)S(1)} %get-tuple-element.36), channel_id=1, source_target_pairs={{0,8},{4,12},{8,0},{12,4},{1,9},{5,13},{9,1},{13,5},{2,10},{6,14},... | collective-permute-start | bytes 602120 | tf_op jit(solution)/shard_map/ppermute | solution.py:60
  10.1 1.5 %collective-permute-start = (bf16[784,128]{1,0:T(8,128)(2,1)S(1)}, bf16[784,128]{1,0:T(8,128)(2,1)S(1)}, u32[]{:S(2)}, u32[]{:S(2)}) collective-permute-start(bf16[784,128]{1,0:T(8,128)(2,1)S(1)} %get-tuple-element.34.refs_0_.refs_6_.refs_4_), channel_id=1, source_target_pairs={{0,2},{2,0},{1,3},{3,1},{4,6},{6,4},{5,7},{7,5},{8,10},{10,8},{9,1... | collective-permute-start | bytes 602120 | tf_op jit(solution)/shard_map/ppermute | solution.py:60
  11.8 4.3 %collective-permute-done.1.refs_1_.refs_7_.refs_5_ = bf16[784,128]{1,0:T(8,128)(2,1)S(1)} collective-permute-done((bf16[784,128]{1,0:T(8,128)(2,1)S(1)}, bf16[784,128]{1,0:T(8,128)(2,1)S(1)}, u32[]{:S(2)}, u32[]{:S(2)}) %collective-permute-start.1) | collective-permute-done | bytes 200736 | tf_op jit(solution)/shard_map/ppermute | solution.py:60
  16.0 1.7 %collective-permute-start.2 = (bf16[784,128]{1,0:T(8,128)(2,1)S(1)}, bf16[784,128]{1,0:T(8,128)(2,1)S(1)}, u32[]{:S(2)}, u32[]{:S(2)}) collective-permute-start(bf16[784,128]{1,0:T(8,128)(2,1)S(1)} %collective-permute-done.1.refs_1_.refs_7_.refs_5_), channel_id=1, source_target_pairs={{0,2},{2,0},{1,3},{3,1},{4,6},{6,4},{5,7},{7,5},{8,10},{10,8},{9,1... | collective-permute-start | bytes 602120 | tf_op jit(solution)/shard_map/ppermute | solution.py:60
  17.7 6.1 %collective-permute-done.3.refs_2_.refs_8_.refs_6_ = bf16[784,128]{1,0:T(8,128)(2,1)S(1)} collective-permute-done((bf16[784,128]{1,0:T(8,128)(2,1)S(1)}, bf16[784,128]{1,0:T(8,128)(2,1)S(1)}, u32[]{:S(2)}, u32[]{:S(2)}) %collective-permute-start.3) | collective-permute-done | bytes 200736 | tf_op jit(solution)/shard_map/ppermute | solution.py:60
  23.8 1.5 %collective-permute-start.4 = (bf16[784,128]{1,0:T(8,128)(2,1)S(1)}, bf16[784,128]{1,0:T(8,128)(2,1)S(1)}, u32[]{:S(2)}, u32[]{:S(2)}) collective-permute-start(bf16[784,128]{1,0:T(8,128)(2,1)S(1)} %collective-permute-done.3.refs_2_.refs_8_.refs_6_), channel_id=1, source_target_pairs={{0,2},{2,0},{1,3},{3,1},{4,6},{6,4},{5,7},{7,5},{8,10},{10,8},{9,1... | collective-permute-start | bytes 602120 | tf_op jit(solution)/shard_map/ppermute | solution.py:60
  25.3 2.5 %collective-permute-start.5 = (bf16[384,128]{1,0:T(8,128)(2,1)S(1)}, bf16[384,128]{1,0:T(8,128)(2,1)S(1)}, u32[]{:S(2)}, u32[]{:S(2)}) collective-permute-start(bf16[384,128]{1,0:T(8,128)(2,1)S(1)} %get-tuple-element.37), channel_id=1, source_target_pairs={{0,12},{4,8},{8,4},{12,0},{1,13},{5,9},{9,5},{13,1},{2,14},{6,10},... | collective-permute-start | bytes 294920 | tf_op jit(solution)/shard_map/ppermute | solution.py:60
  28.3 3.4 %collective-permute-done.5.refs_3_ = bf16[384,128]{1,0:T(8,128)(2,1)S(1)} collective-permute-done((bf16[384,128]{1,0:T(8,128)(2,1)S(1)}, bf16[384,128]{1,0:T(8,128)(2,1)S(1)}, u32[]{:S(2)}, u32[]{:S(2)}) %collective-permute-start.5) | collective-permute-done | bytes 98336 | tf_op jit(solution)/shard_map/ppermute | solution.py:60
  32.9 1.6 %collective-permute-start.8 = (f32[8,192]{1,0:T(8,128)S(1)}, f32[8,192]{1,0:T(8,128)S(1)}, u32[]{:S(2)}, u32[]{:S(2)}) collective-permute-start(f32[8,192]{1,0:T(8,128)S(1)} %shard_map.93.refs_8_), channel_id=1, source_target_pairs={{0,2},{2,0},{1,3},{3,1},{4,6},{6,4},{5,7},{7,5},{8,10},{10,8},{9,1... | collective-permute-start | bytes 18440 | tf_op jit(solution)/shard_map/ppermute | solution.py:60
  34.5 1.3 %load.1 = (bf16[4096,768]{1,0:T(8,128)(2,1)S(1)}, bf16[4096,768]{1,0:T(8,128)(2,1)S(1)}, bf16[768,4096]{1,0:T(8,128)(2,1)S(1)}) custom-call(bf16[4096,768]{1,0:T(8,128)(2,1)S(1)} %bitcast.10, bf16[4096,768]{1,0:T(8,128)(2,1)S(1)} %bitcast.13, bf16[768,4096]{1,0:T(8,128)(2,1)S(1)} %bitcast.16), custom_call_target="tpu_custom_call" | custom-call | tf_op jit(solution)/shard_map/load/pallas_call | solution.py:223
  35.8 0.8 %shard_map.94 = (f32[192,768]{1,0:T(8,128)S(1)}, f32[192,768]{1,0:T(8,128)S(1)}) custom-call(bf16[784,128]{1,0:T(8,128)(2,1)S(1)} %get-tuple-element.34.refs_0_.refs_6_.refs_4_, bf16[784,128]{1,0:T(8,128)(2,1)S(1)} %collective-permute-done.1.refs_1_.refs_7_.refs_5_, bf16[784,128]{1,0:T(8,128)(2,1)S(1)} %collective-permute-done.3.refs_2_.refs_8_.refs_6_, ...), custom_call_target="tpu_custom_call" | custom-call | tf_op jit(solution)/shard_map/pallas_call | solution.py:22
  36.6 0.8 %shard_map.95 = (f32[192,768]{1,0:T(8,128)S(1)}, f32[192,768]{1,0:T(8,128)S(1)}) custom-call(bf16[784,128]{1,0:T(8,128)(2,1)S(1)} %get-tuple-element.34.refs_0_.refs_6_.refs_4_, bf16[784,128]{1,0:T(8,128)(2,1)S(1)} %collective-permute-done.1.refs_1_.refs_7_.refs_5_, bf16[784,128]{1,0:T(8,128)(2,1)S(1)} %collective-permute-done.3.refs_2_.refs_8_.refs_6_, ...), custom_call_target="tpu_custom_call" | custom-call | tf_op jit(solution)/shard_map/pallas_call | solution.py:22
  37.5 0.8 %shard_map.96 = (f32[192,768]{1,0:T(8,128)S(1)}, f32[192,768]{1,0:T(8,128)S(1)}) custom-call(bf16[784,128]{1,0:T(8,128)(2,1)S(1)} %collective-permute-done.refs_0_, bf16[784,128]{1,0:T(8,128)(2,1)S(1)} %collective-permute-done.2.refs_1_, bf16[784,128]{1,0:T(8,128)(2,1)S(1)} %collective-permute-done.4.refs_2_, ...), custom_call_target="tpu_custom_call" | custom-call | tf_op jit(solution)/shard_map/pallas_call | solution.py:22
  38.4 1.3 %shard_map.97 = (bf16[192,768]{1,0:T(8,128)(2,1)S(1)}, bf16[192,128]{1,0:T(8,128)(2,1)S(1)}, bf16[192,128]{1,0:T(8,128)(2,1)S(1)}) custom-call(bf16[784,128]{1,0:T(8,128)(2,1)S(1)} %collective-permute-done.refs_0_, bf16[784,128]{1,0:T(8,128)(2,1)S(1)} %collective-permute-done.2.refs_1_, bf16[784,128]{1,0:T(8,128)(2,1)S(1)} %collective-permute-done.4.refs_2_, ...), custom_call_target="tpu_custom_call" | custom-call | tf_op jit(solution)/shard_map/pallas_call | solution.py:22
  39.7 0.8 %shard_map.99 = (bf16[768,128]{1,0:T(8,128)(2,1)S(1)}, bf16[768,128]{1,0:T(8,128)(2,1)S(1)}, bf16[576,128]{1,0:T(8,128)(2,1)S(1)}, bf16[768,128]{1,0:T(8,128)(2,1)S(1)}) custom-call(bf16[192,768]{1,0:T(8,128)(2,1)S(1)} %get-tuple-element.48.act_ref, bf16[768,4096]{1,0:T(8,128)(2,1)S(1)} %get-tuple-element.47.refs_15_.down_ref), custom_call_target="tpu_custom_call" | custom-call | tf_op jit(solution)/shard_map/pallas_call | solution.py:22
  41.1 1.5 %collective-permute-start.17 = (bf16[768,128]{1,0:T(8,128)(2,1)S(1)}, bf16[768,128]{1,0:T(8,128)(2,1)S(1)}, u32[]{:S(2)}, u32[]{:S(2)}) collective-permute-start(bf16[768,128]{1,0:T(8,128)(2,1)S(1)} %get-tuple-element.62), channel_id=1, source_target_pairs={{0,2},{2,0},{1,3},{3,1},{4,6},{6,4},{5,7},{7,5},{8,10},{10,8},{9,1... | collective-permute-start | bytes 589832 | tf_op jit(solution)/shard_map/ppermute | solution.py:60
  43.1 0.8 %shard_map.98 = (bf16[768,128]{1,0:T(8,128)(2,1)S(1)}, bf16[768,128]{1,0:T(8,128)(2,1)S(1)}, bf16[576,128]{1,0:T(8,128)(2,1)S(1)}, bf16[768,128]{1,0:T(8,128)(2,1)S(1)}) custom-call(bf16[192,768]{1,0:T(8,128)(2,1)S(1)} %get-tuple-element.48.act_ref, bf16[768,4096]{1,0:T(8,128)(2,1)S(1)} %get-tuple-element.47.refs_15_.down_ref), custom_call_target="tpu_custom_call" | custom-call | tf_op jit(solution)/shard_map/pallas_call | solution.py:22
  43.9 1.6 %collective-permute-start.10 = (bf16[768,128]{1,0:T(8,128)(2,1)S(1)}, bf16[768,128]{1,0:T(8,128)(2,1)S(1)}, u32[]{:S(2)}, u32[]{:S(2)}) collective-permute-start(bf16[768,128]{1,0:T(8,128)(2,1)S(1)} %get-tuple-element.50), channel_id=1, source_target_pairs={{0,2},{2,0},{1,3},{3,1},{4,6},{6,4},{5,7},{7,5},{8,10},{10,8},{9,1... | collective-permute-start | bytes 589832 | tf_op jit(solution)/shard_map/ppermute | solution.py:60
  45.5 0.7 %collective-permute-done.11.refs_1_ = bf16[768,128]{1,0:T(8,128)(2,1)S(1)} collective-permute-done((bf16[768,128]{1,0:T(8,128)(2,1)S(1)}, bf16[768,128]{1,0:T(8,128)(2,1)S(1)}, u32[]{:S(2)}, u32[]{:S(2)}) %collective-permute-start.11) | collective-permute-done | bytes 196640 | tf_op jit(solution)/shard_map/ppermute | solution.py:60
  46.4 2.0 %collective-permute-done.17.refs_1_ = bf16[768,128]{1,0:T(8,128)(2,1)S(1)} collective-permute-done((bf16[768,128]{1,0:T(8,128)(2,1)S(1)}, bf16[768,128]{1,0:T(8,128)(2,1)S(1)}, u32[]{:S(2)}, u32[]{:S(2)}) %collective-permute-start.17) | collective-permute-done | bytes 196640 | tf_op jit(solution)/shard_map/ppermute | solution.py:60
  48.4 3.1 %collective-permute-start.18 = (bf16[768,128]{1,0:T(8,128)(2,1)S(1)}, bf16[768,128]{1,0:T(8,128)(2,1)S(1)}, u32[]{:S(2)}, u32[]{:S(2)}) collective-permute-start(bf16[768,128]{1,0:T(8,128)(2,1)S(1)} %shard_map.104), channel_id=1, source_target_pairs={{12,0},{8,4},{4,8},{0,12},{13,1},{9,5},{5,9},{1,13},{14,2},{10,6},... | collective-permute-start | bytes 589832 | tf_op jit(solution)/shard_map/ppermute | solution.py:60
  51.5 0.8 %collective-permute-start.16 = (bf16[576,128]{1,0:T(8,128)(2,1)S(1)}, bf16[576,128]{1,0:T(8,128)(2,1)S(1)}, u32[]{:S(2)}, u32[]{:S(2)}) collective-permute-start(bf16[576,128]{1,0:T(8,128)(2,1)S(1)} %shard_map.102), channel_id=1, source_target_pairs={{8,0},{12,4},{0,8},{4,12},{9,1},{13,5},{1,9},{5,13},{10,2},{14,6},... | collective-permute-start | bytes 442376 | tf_op jit(solution)/shard_map/ppermute | solution.py:60
  52.3 1.5 %collective-permute-start.13 = (bf16[192,128]{1,0:T(8,128)(2,1)S(1)}, bf16[192,128]{1,0:T(8,128)(2,1)S(1)}, u32[]{:S(2)}, u32[]{:S(2)}) collective-permute-start(bf16[192,128]{1,0:T(8,128)(2,1)S(1)} %get-tuple-element.54), channel_id=1, source_target_pairs={{0,2},{2,0},{1,3},{3,1},{4,6},{6,4},{5,7},{7,5},{8,10},{10,8},{9,1... | collective-permute-start | bytes 147464 | tf_op jit(solution)/shard_map/ppermute | solution.py:60
  53.8 2.6 %collective-permute-done.13.refs_1_ = bf16[192,128]{1,0:T(8,128)(2,1)S(1)} collective-permute-done((bf16[192,128]{1,0:T(8,128)(2,1)S(1)}, bf16[192,128]{1,0:T(8,128)(2,1)S(1)}, u32[]{:S(2)}, u32[]{:S(2)}) %collective-permute-start.13) | collective-permute-done | bytes 49184 | tf_op jit(solution)/shard_map/ppermute | solution.py:60
  56.4 2.3 %collective-permute-start.14 = (bf16[192,128]{1,0:T(8,128)(2,1)S(1)}, bf16[192,128]{1,0:T(8,128)(2,1)S(1)}, u32[]{:S(2)}, u32[]{:S(2)}) collective-permute-start(bf16[192,128]{1,0:T(8,128)(2,1)S(1)} %shard_map.101), channel_id=1, source_target_pairs={{8,0},{12,4},{0,8},{4,12},{9,1},{13,5},{1,9},{5,13},{10,2},{14,6},... | collective-permute-start | bytes 147464 | tf_op jit(solution)/shard_map/ppermute | solution.py:60
  58.7 2.8 %collective-permute-done.14.refs_5_ = bf16[192,128]{1,0:T(8,128)(2,1)S(1)} collective-permute-done((bf16[192,128]{1,0:T(8,128)(2,1)S(1)}, bf16[192,128]{1,0:T(8,128)(2,1)S(1)}, u32[]{:S(2)}, u32[]{:S(2)}) %collective-permute-start.14) | collective-permute-done | bytes 49184 | tf_op jit(solution)/shard_map/ppermute | solution.py:60
  62.1 1.1 %shard_map.105 = bf16[64,2048]{1,0:T(8,128)(2,1)} custom-call(f32[64,2048]{1,0:T(8,128)S(1)} %get-tuple-element.57.partial, bf16[48,64]{1,0:T(8,128)(2,1)S(1)} %get-tuple-element.58.refs_0_, bf16[48,64]{1,0:T(8,128)(2,1)S(1)} %get-tuple-element.59.refs_1_, bf16[48,64]{1,0:T(8,128)(2,1)S(1)} %get-tuple-element.60.refs_2_, ...), custom_call_target="tpu_custom_call" | custom-call | tf_op jit(solution)/shard_map/pallas_call | solution.py:22
  (51 shorter events, 4.0 us)
Async XLA Ops:
  0.0 34.4 %slice-start = ((s8[6291456]{0:T(1024)(128)(4,1)}), s8[4194304]{0:T(1024)(128)(4,1)S(1)}, s32[]{:S(2)}) async-start(s8[6291456]{0:T(1024)(128)(4,1)} %bitcast.8), calls=%async_computation | async-start | bytes 8388608
  0.0 34.4 %slice-start.2 = ((s8[6291456]{0:T(1024)(128)(4,1)}), s8[4194304]{0:T(1024)(128)(4,1)S(1)}, s32[]{:S(2)}) async-start(s8[6291456]{0:T(1024)(128)(4,1)} %bitcast.11), calls=%async_computation.2 | async-start | bytes 8388608
  0.0 34.4 %slice-start.4 = ((s8[6291456]{0:T(1024)(128)(4,1)}), s8[4194304]{0:T(1024)(128)(4,1)S(1)}, s32[]{:S(2)}) async-start(s8[6291456]{0:T(1024)(128)(4,1)} %bitcast.14), calls=%async_computation.4 | async-start | bytes 8388608
  0.0 0.8 %copy-start.2 = (s32[64,2]{0,1:T(2,128)S(1)}, s32[64,2]{0,1:T(2,128)}, u32[]{:S(2)}) copy-start(s32[64,2]{0,1:T(2,128)} %param.10) | copy-start | bytes 1540
  0.8 1.4 %copy-start.5 = (bf16[64,2048]{1,0:T(8,128)(2,1)S(1)}, bf16[64,2048]{1,0:T(8,128)(2,1)}, u32[]{:S(2)}) copy-start(bf16[64,2048]{1,0:T(8,128)(2,1)} %tok_in.1) | copy-start | bytes 786436
  2.2 1.5 %copy-start.6 = (s32[8,4]{0,1:T(4,128)S(1)}, s32[8,4]{0,1:T(4,128)}, u32[]{:S(2)}) copy-start(s32[8,4]{0,1:T(4,128)} %param.12) | copy-start | bytes 388
  3.7 28.6 %copy-start = (bf16[1,2048,128]{2,1,0:T(8,128)(2,1)S(1)}, bf16[1,2048,128]{2,1,0:T(8,128)(2,1)}, u32[]{:S(2)}) copy-start(bf16[1,2048,128]{2,1,0:T(8,128)(2,1)} %param.16) | copy-start | bytes 1572868
  3.7 30.8 %slice-start.1 = ((s8[6291456]{0:T(1024)(128)(4,1)}), s8[2097152]{0:T(1024)(128)(4,1)S(1)}, s32[]{:S(2)}) async-start(s8[6291456]{0:T(1024)(128)(4,1)} %bitcast.8), calls=%async_computation.1 | async-start | bytes 4194304
  3.7 30.8 %slice-start.3 = ((s8[6291456]{0:T(1024)(128)(4,1)}), s8[2097152]{0:T(1024)(128)(4,1)S(1)}, s32[]{:S(2)}) async-start(s8[6291456]{0:T(1024)(128)(4,1)} %bitcast.11), calls=%async_computation.3 | async-start | bytes 4194304
  3.7 30.8 %slice-start.5 = ((s8[6291456]{0:T(1024)(128)(4,1)}), s8[2097152]{0:T(1024)(128)(4,1)S(1)}, s32[]{:S(2)}) async-start(s8[6291456]{0:T(1024)(128)(4,1)} %bitcast.14), calls=%async_computation.5 | async-start | bytes 4194304
  4.4 11.7 %collective-permute-start.1 = (bf16[784,128]{1,0:T(8,128)(2,1)S(1)}, bf16[784,128]{1,0:T(8,128)(2,1)S(1)}, u32[]{:S(2)}, u32[]{:S(2)}) collective-permute-start(bf16[784,128]{1,0:T(8,128)(2,1)S(1)} %get-tuple-element.35), channel_id=1, source_target_pairs={{0,4},{4,0},{8,12},{12,8},{1,5},{5,1},{9,13},{13,9},{2,6},{6,2},{1... | collective-permute-start | bytes 602120 | tf_op jit(solution)/shard_map/ppermute | solution.py:60
  7.5 16.3 %collective-permute-start.3 = (bf16[784,128]{1,0:T(8,128)(2,1)S(1)}, bf16[784,128]{1,0:T(8,128)(2,1)S(1)}, u32[]{:S(2)}, u32[]{:S(2)}) collective-permute-start(bf16[784,128]{1,0:T(8,128)(2,1)S(1)} %get-tuple-element.36), channel_id=1, source_target_pairs={{0,8},{4,12},{8,0},{12,4},{1,9},{5,13},{9,1},{13,5},{2,10},{6,14},... | collective-permute-start | bytes 602120 | tf_op jit(solution)/shard_map/ppermute | solution.py:60
  10.1 22.8 %collective-permute-start = (bf16[784,128]{1,0:T(8,128)(2,1)S(1)}, bf16[784,128]{1,0:T(8,128)(2,1)S(1)}, u32[]{:S(2)}, u32[]{:S(2)}) collective-permute-start(bf16[784,128]{1,0:T(8,128)(2,1)S(1)} %get-tuple-element.34.refs_0_.refs_6_.refs_4_), channel_id=1, source_target_pairs={{0,2},{2,0},{1,3},{3,1},{4,6},{6,4},{5,7},{7,5},{8,10},{10,8},{9,1... | collective-permute-start | bytes 602120 | tf_op jit(solution)/shard_map/ppermute | solution.py:60
  11.6 16.2 %collective-permute-start.7 = (bf16[400,128]{1,0:T(8,128)(2,1)S(1)}, bf16[400,128]{1,0:T(8,128)(2,1)S(1)}, u32[]{:S(2)}, u32[]{:S(2)}) collective-permute-start(bf16[400,128]{1,0:T(8,128)(2,1)S(1)} %get-tuple-element.38), channel_id=1, source_target_pairs={{0,12},{4,8},{8,4},{12,0},{1,13},{5,9},{9,5},{13,1},{2,14},{6,10},... | collective-permute-start | bytes 307208 | tf_op jit(solution)/shard_map/ppermute | solution.py:60
  16.0 21.4 %collective-permute-start.2 = (bf16[784,128]{1,0:T(8,128)(2,1)S(1)}, bf16[784,128]{1,0:T(8,128)(2,1)S(1)}, u32[]{:S(2)}, u32[]{:S(2)}) collective-permute-start(bf16[784,128]{1,0:T(8,128)(2,1)S(1)} %collective-permute-done.1.refs_1_.refs_7_.refs_5_), channel_id=1, source_target_pairs={{0,2},{2,0},{1,3},{3,1},{4,6},{6,4},{5,7},{7,5},{8,10},{10,8},{9,1... | collective-permute-start | bytes 602120 | tf_op jit(solution)/shard_map/ppermute | solution.py:60
  23.8 13.6 %collective-permute-start.4 = (bf16[784,128]{1,0:T(8,128)(2,1)S(1)}, bf16[784,128]{1,0:T(8,128)(2,1)S(1)}, u32[]{:S(2)}, u32[]{:S(2)}) collective-permute-start(bf16[784,128]{1,0:T(8,128)(2,1)S(1)} %collective-permute-done.3.refs_2_.refs_8_.refs_6_), channel_id=1, source_target_pairs={{0,2},{2,0},{1,3},{3,1},{4,6},{6,4},{5,7},{7,5},{8,10},{10,8},{9,1... | collective-permute-start | bytes 602120 | tf_op jit(solution)/shard_map/ppermute | solution.py:60
  25.3 6.4 %collective-permute-start.5 = (bf16[384,128]{1,0:T(8,128)(2,1)S(1)}, bf16[384,128]{1,0:T(8,128)(2,1)S(1)}, u32[]{:S(2)}, u32[]{:S(2)}) collective-permute-start(bf16[384,128]{1,0:T(8,128)(2,1)S(1)} %get-tuple-element.37), channel_id=1, source_target_pairs={{0,12},{4,8},{8,4},{12,0},{1,13},{5,9},{9,5},{13,1},{2,14},{6,10},... | collective-permute-start | bytes 294920 | tf_op jit(solution)/shard_map/ppermute | solution.py:60
  27.8 9.6 %collective-permute-start.9 = (bf16[400,128]{1,0:T(8,128)(2,1)S(1)}, bf16[400,128]{1,0:T(8,128)(2,1)S(1)}, u32[]{:S(2)}, u32[]{:S(2)}) collective-permute-start(bf16[400,128]{1,0:T(8,128)(2,1)S(1)} %collective-permute-done.7.refs_3_.refs_9_.refs_7_), channel_id=1, source_target_pairs={{0,2},{2,0},{1,3},{3,1},{4,6},{6,4},{5,7},{7,5},{8,10},{10,8},{9,1... | collective-permute-start | bytes 307208 | tf_op jit(solution)/shard_map/ppermute | solution.py:60
  31.7 6.6 %collective-permute-start.6 = (bf16[384,128]{1,0:T(8,128)(2,1)S(1)}, bf16[384,128]{1,0:T(8,128)(2,1)S(1)}, u32[]{:S(2)}, u32[]{:S(2)}) collective-permute-start(bf16[384,128]{1,0:T(8,128)(2,1)S(1)} %collective-permute-done.5.refs_3_), channel_id=1, source_target_pairs={{0,2},{2,0},{1,3},{3,1},{4,6},{6,4},{5,7},{7,5},{8,10},{10,8},{9,1... | collective-permute-start | bytes 294920 | tf_op jit(solution)/shard_map/ppermute | solution.py:60
  32.9 5.4 %collective-permute-start.8 = (f32[8,192]{1,0:T(8,128)S(1)}, f32[8,192]{1,0:T(8,128)S(1)}, u32[]{:S(2)}, u32[]{:S(2)}) collective-permute-start(f32[8,192]{1,0:T(8,128)S(1)} %shard_map.93.refs_8_), channel_id=1, source_target_pairs={{0,2},{2,0},{1,3},{3,1},{4,6},{6,4},{5,7},{7,5},{8,10},{10,8},{9,1... | collective-permute-start | bytes 18440 | tf_op jit(solution)/shard_map/ppermute | solution.py:60
  37.4 0.9 %copy-start.1 = (bf16[1,128,768]{2,1,0:T(8,128)(2,1)S(1)}, bf16[1,128,768]{2,1,0:T(8,128)(2,1)}, u32[]{:S(2)}) copy-start(bf16[1,128,768]{2,1,0:T(8,128)(2,1)} %param.17) | copy-start | bytes 589828
  39.7 21.8 %copy-start.3 = (s32[64,2]{0,1:T(2,128)S(1)}, s32[64,2]{0,1:T(2,128)}, u32[]{:S(2)}) copy-start(s32[64,2]{0,1:T(2,128)} %param.10) | copy-start | bytes 1540
  39.7 21.8 %copy-start.4 = (f32[64,2]{0,1:T(2,128)S(1)}, f32[64,2]{0,1:T(2,128)}, u32[]{:S(2)}) copy-start(f32[64,2]{0,1:T(2,128)} %param.11) | copy-start | bytes 1540
  40.5 5.7 %collective-permute-start.11 = (bf16[768,128]{1,0:T(8,128)(2,1)S(1)}, bf16[768,128]{1,0:T(8,128)(2,1)S(1)}, u32[]{:S(2)}, u32[]{:S(2)}) collective-permute-start(bf16[768,128]{1,0:T(8,128)(2,1)S(1)} %get-tuple-element.52), channel_id=1, source_target_pairs={{0,2},{2,0},{1,3},{3,1},{4,6},{6,4},{5,7},{7,5},{8,10},{10,8},{9,1... | collective-permute-start | bytes 589832 | tf_op jit(solution)/shard_map/ppermute | solution.py:60
  41.1 7.2 %collective-permute-start.17 = (bf16[768,128]{1,0:T(8,128)(2,1)S(1)}, bf16[768,128]{1,0:T(8,128)(2,1)S(1)}, u32[]{:S(2)}, u32[]{:S(2)}) collective-permute-start(bf16[768,128]{1,0:T(8,128)(2,1)S(1)} %get-tuple-element.62), channel_id=1, source_target_pairs={{0,2},{2,0},{1,3},{3,1},{4,6},{6,4},{5,7},{7,5},{8,10},{10,8},{9,1... | collective-permute-start | bytes 589832 | tf_op jit(solution)/shard_map/ppermute | solution.py:60
  42.6 8.9 %collective-permute-start.15 = (bf16[576,128]{1,0:T(8,128)(2,1)S(1)}, bf16[576,128]{1,0:T(8,128)(2,1)S(1)}, u32[]{:S(2)}, u32[]{:S(2)}) collective-permute-start(bf16[576,128]{1,0:T(8,128)(2,1)S(1)} %get-tuple-element.56), channel_id=1, source_target_pairs={{0,2},{2,0},{1,3},{3,1},{4,6},{6,4},{5,7},{7,5},{8,10},{10,8},{9,1... | collective-permute-start | bytes 442376 | tf_op jit(solution)/shard_map/ppermute | solution.py:60
  43.9 17.5 %collective-permute-start.10 = (bf16[768,128]{1,0:T(8,128)(2,1)S(1)}, bf16[768,128]{1,0:T(8,128)(2,1)S(1)}, u32[]{:S(2)}, u32[]{:S(2)}) collective-permute-start(bf16[768,128]{1,0:T(8,128)(2,1)S(1)} %get-tuple-element.50), channel_id=1, source_target_pairs={{0,2},{2,0},{1,3},{3,1},{4,6},{6,4},{5,7},{7,5},{8,10},{10,8},{9,1... | collective-permute-start | bytes 589832 | tf_op jit(solution)/shard_map/ppermute | solution.py:60
  46.3 15.2 %collective-permute-start.12 = (bf16[768,128]{1,0:T(8,128)(2,1)S(1)}, bf16[768,128]{1,0:T(8,128)(2,1)S(1)}, u32[]{:S(2)}, u32[]{:S(2)}) collective-permute-start(bf16[768,128]{1,0:T(8,128)(2,1)S(1)} %shard_map.100), channel_id=1, source_target_pairs={{4,0},{0,4},{12,8},{8,12},{5,1},{1,5},{13,9},{9,13},{6,2},{2,6},{1... | collective-permute-start | bytes 589832 | tf_op jit(solution)/shard_map/ppermute | solution.py:60
  48.4 13.7 %collective-permute-start.18 = (bf16[768,128]{1,0:T(8,128)(2,1)S(1)}, bf16[768,128]{1,0:T(8,128)(2,1)S(1)}, u32[]{:S(2)}, u32[]{:S(2)}) collective-permute-start(bf16[768,128]{1,0:T(8,128)(2,1)S(1)} %shard_map.104), channel_id=1, source_target_pairs={{12,0},{8,4},{4,8},{0,12},{13,1},{9,5},{5,9},{1,13},{14,2},{10,6},... | collective-permute-start | bytes 589832 | tf_op jit(solution)/shard_map/ppermute | solution.py:60
  51.5 9.9 %collective-permute-start.16 = (bf16[576,128]{1,0:T(8,128)(2,1)S(1)}, bf16[576,128]{1,0:T(8,128)(2,1)S(1)}, u32[]{:S(2)}, u32[]{:S(2)}) collective-permute-start(bf16[576,128]{1,0:T(8,128)(2,1)S(1)} %shard_map.102), channel_id=1, source_target_pairs={{8,0},{12,4},{0,8},{4,12},{9,1},{13,5},{1,9},{5,13},{10,2},{14,6},... | collective-permute-start | bytes 442376 | tf_op jit(solution)/shard_map/ppermute | solution.py:60
  52.3 4.1 %collective-permute-start.13 = (bf16[192,128]{1,0:T(8,128)(2,1)S(1)}, bf16[192,128]{1,0:T(8,128)(2,1)S(1)}, u32[]{:S(2)}, u32[]{:S(2)}) collective-permute-start(bf16[192,128]{1,0:T(8,128)(2,1)S(1)} %get-tuple-element.54), channel_id=1, source_target_pairs={{0,2},{2,0},{1,3},{3,1},{4,6},{6,4},{5,7},{7,5},{8,10},{10,8},{9,1... | collective-permute-start | bytes 147464 | tf_op jit(solution)/shard_map/ppermute | solution.py:60
  56.4 5.1 %collective-permute-start.14 = (bf16[192,128]{1,0:T(8,128)(2,1)S(1)}, bf16[192,128]{1,0:T(8,128)(2,1)S(1)}, u32[]{:S(2)}, u32[]{:S(2)}) collective-permute-start(bf16[192,128]{1,0:T(8,128)(2,1)S(1)} %shard_map.101), channel_id=1, source_target_pairs={{8,0},{12,4},{0,8},{4,12},{9,1},{13,5},{1,9},{5,13},{10,2},{14,6},... | collective-permute-start | bytes 147464 | tf_op jit(solution)/shard_map/ppermute | solution.py:60

commit v2 on v1

--- a/solution.py
+++ b/solution.py
@@ -152,7 +152,7 @@
 
     there = []
     for k in range(experts):
-        if k and k == last:
+        if k and k in (1, last):
             there += [Piece(k, 0, half, cap, True), Piece(k, half, part, cap, False)]
         else:
             there += [Piece(k, 0, part, cap, True)]
@@ -200,8 +200,7 @@
     sent = call(
         dispatch,
         [p.shape for p in there],
-        (route_ids.T, user_slot.T, tokens),
-        flops=10**10,
+        tuple(pltpu.with_memory_space_constraint(v, pltpu.HBM) for v in (route_ids.T, user_slot.T, tokens)),
         in_specs=[HBM] * 3,
         scratch=[
             pltpu.VMEM(route_ids.T.shape, jnp.int32),
@@ -210,6 +209,11 @@
             pltpu.SemaphoreType.DMA((3,)),
         ],
     )
+
+    def pace(inp, out):
+        out[...] = inp[...]
+
+    sent = [*call(pace, [there[0].shape], (sent[0],), flops=10**10), *sent[1:]]
 
     def load(*refs):
         sems = refs[6]

time: 63.3 us -> 64.6 us (1.021)
  local copies, waits for them, and re-layouts: 3.76 us -> 0.08 us
  waiting for transfers between devices: 21.9 us -> 24.2 us
  starting transfers between devices: 27.5 us -> 29.4 us
  Pallas kernels: 9.74 us -> 10.5 us
    unnamed x26 -> x20, local copies, waits for them, and re-layouts: 3.76 us -> 0.08 us
    ppermute x19 -> x21, waiting for transfers between devices: 21.9 us -> 24.2 us  [permute(): return lax.ppermute(value, axis, pairs)]
    ppermute x19 -> x21, starting transfers between devices: 27.5 us -> 29.4 us  [permute(): return lax.ppermute(value, axis, pairs)]
    pallas_call x15 -> x16, Pallas kernels: 8.46 us -> 9.17 us  [call(): pl.pallas_call(body, out_shape=outs, in_specs=in_specs or [VMEM] * len(in...]
  transfers between devices with their start and end apart: 19 -> 21, of which waited for: 7 -> 6; matrix products, arithmetic and copies ran while one was open for 0% -> 0% of each run, Pallas kernels for 9% -> 9%
where the time goes in v2:
time: 64.6 us; the launch traced here: 64.5 us
  starting transfers between devices  29.4 us (46%)
  waiting for transfers between devices  24.2 us (37%)
  Pallas kernels  10.5 us (16%)
    ppermute x21, starting transfers between devices, permute(): return lax.ppermute(value, axis, pairs)  29.4 us
    ppermute x21, waiting for transfers between devices, permute(): return lax.ppermute(value, axis, pairs)  24.2 us
    pallas_call x16, Pallas kernels, call(): pl.pallas_call(body, out_shape=outs, in_specs=in_specs or [VMEM] * len(in...  9.17 us
  transfers between devices with their start and end apart: 21, of which 6 were waited for; matrix products, arithmetic and copies ran while one was open for 0% of the time, Pallas kernels for 9%

profile of v2, /device:TPU:0, one launch (start us, length us, event | category | flops | bytes accessed | tf_op | source)
XLA Modules:
  0.0 64.5 jit_solution(17990275420628341408)
XLA Ops:
  0.0 1.4 %shard_map.91 = (bf16[784,128]{1,0:T(8,128)(2,1)S(1)}, bf16[400,128]{1,0:T(8,128)(2,1)S(1)}, bf16[384,128]{1,0:T(8,128)(2,1)S(1)}, bf16[784,128]{1,0:T(8,128)(2,...) custom-call(s32[2,64]{1,0:T(2,128)} %bitcast.20, s32[4,8]{1,0:T(4,128)} %bitcast.23, ...), custom_call_target="tpu_custom_call" | custom-call | tf_op jit(solution)/shard_map/pallas_call | solution.py:22
  1.4 4.1 %collective-permute-start.3 = (bf16[784,128]{1,0:T(8,128)(2,1)S(1)}, bf16[784,128]{1,0:T(8,128)(2,1)S(1)}, u32[]{:S(2)}, u32[]{:S(2)}) collective-permute-start(bf16[784,128]{1,0:T(8,128)(2,1)S(1)} %get-tuple-element.37), channel_id=1, source_target_pairs={{0,8},{4,12},{8,0},{12,4},{1,9},{5,13},{9,1},{13,5},{2,10},{6,14},... | collective-permute-start | bytes 602120 | tf_op jit(solution)/shard_map/ppermute | solution.py:60
  5.6 1.6 %collective-permute-start = (bf16[784,128]{1,0:T(8,128)(2,1)S(1)}, bf16[784,128]{1,0:T(8,128)(2,1)S(1)}, u32[]{:S(2)}, u32[]{:S(2)}) collective-permute-start(bf16[784,128]{1,0:T(8,128)(2,1)S(1)} %shard_map.92.refs_0_.refs_6_.refs_4_), channel_id=1, source_target_pairs={{0,2},{2,0},{1,3},{3,1},{4,6},{6,4},{5,7},{7,5},{8,10},{10,8},{9,1... | collective-permute-start | bytes 602120 | tf_op jit(solution)/shard_map/ppermute | solution.py:60
  7.1 1.6 %collective-permute-start.1 = (bf16[384,128]{1,0:T(8,128)(2,1)S(1)}, bf16[384,128]{1,0:T(8,128)(2,1)S(1)}, u32[]{:S(2)}, u32[]{:S(2)}) collective-permute-start(bf16[384,128]{1,0:T(8,128)(2,1)S(1)} %get-tuple-element.36), channel_id=1, source_target_pairs={{0,4},{4,0},{8,12},{12,8},{1,5},{5,1},{9,13},{13,9},{2,6},{6,2},{1... | collective-permute-start | bytes 294920 | tf_op jit(solution)/shard_map/ppermute | solution.py:60
  8.7 0.4 collective-permute-start.7
  9.1 1.3 %collective-permute-start.8 = (bf16[400,128]{1,0:T(8,128)(2,1)S(1)}, bf16[400,128]{1,0:T(8,128)(2,1)S(1)}, u32[]{:S(2)}, u32[]{:S(2)}) collective-permute-start(bf16[400,128]{1,0:T(8,128)(2,1)S(1)} %get-tuple-element.40), channel_id=1, source_target_pairs={{0,12},{4,8},{8,4},{12,0},{1,13},{5,9},{9,5},{13,1},{2,14},{6,10},... | collective-permute-start | bytes 307208 | tf_op jit(solution)/shard_map/ppermute | solution.py:60
  10.5 6.1 %collective-permute-done.3.refs_2_.refs_8_.refs_6_ = bf16[784,128]{1,0:T(8,128)(2,1)S(1)} collective-permute-done((bf16[784,128]{1,0:T(8,128)(2,1)S(1)}, bf16[784,128]{1,0:T(8,128)(2,1)S(1)}, u32[]{:S(2)}, u32[]{:S(2)}) %collective-permute-start.3) | collective-permute-done | bytes 200736 | tf_op jit(solution)/shard_map/ppermute | solution.py:60
  16.6 2.0 %collective-permute-start.4 = (bf16[784,128]{1,0:T(8,128)(2,1)S(1)}, bf16[784,128]{1,0:T(8,128)(2,1)S(1)}, u32[]{:S(2)}, u32[]{:S(2)}) collective-permute-start(bf16[784,128]{1,0:T(8,128)(2,1)S(1)} %collective-permute-done.3.refs_2_.refs_8_.refs_6_), channel_id=1, source_target_pairs={{0,2},{2,0},{1,3},{3,1},{4,6},{6,4},{5,7},{7,5},{8,10},{10,8},{9,1... | collective-permute-start | bytes 602120 | tf_op jit(solution)/shard_map/ppermute | solution.py:60
  18.6 2.5 %collective-permute-start.5 = (bf16[384,128]{1,0:T(8,128)(2,1)S(1)}, bf16[384,128]{1,0:T(8,128)(2,1)S(1)}, u32[]{:S(2)}, u32[]{:S(2)}) collective-permute-start(bf16[384,128]{1,0:T(8,128)(2,1)S(1)} %get-tuple-element.38), channel_id=1, source_target_pairs={{0,12},{4,8},{8,4},{12,0},{1,13},{5,9},{9,5},{13,1},{2,14},{6,10},... | collective-permute-start | bytes 294920 | tf_op jit(solution)/shard_map/ppermute | solution.py:60
  21.0 0.6 collective-permute-start.10
  21.6 1.5 %collective-permute-start.11 = (bf16[400,128]{1,0:T(8,128)(2,1)S(1)}, bf16[400,128]{1,0:T(8,128)(2,1)S(1)}, u32[]{:S(2)}, u32[]{:S(2)}) collective-permute-start(bf16[400,128]{1,0:T(8,128)(2,1)S(1)} %collective-permute-done.8.refs_3_.refs_9_.refs_7_), channel_id=1, source_target_pairs={{0,2},{2,0},{1,3},{3,1},{4,6},{6,4},{5,7},{7,5},{8,10},{10,8},{9,1... | collective-permute-start | bytes 307208 | tf_op jit(solution)/shard_map/ppermute | solution.py:60
  23.1 1.9 %collective-permute-done.5.refs_3_ = bf16[384,128]{1,0:T(8,128)(2,1)S(1)} collective-permute-done((bf16[384,128]{1,0:T(8,128)(2,1)S(1)}, bf16[384,128]{1,0:T(8,128)(2,1)S(1)}, u32[]{:S(2)}, u32[]{:S(2)}) %collective-permute-start.5) | collective-permute-done | bytes 98336 | tf_op jit(solution)/shard_map/ppermute | solution.py:60
  25.0 2.0 %collective-permute-start.6 = (bf16[384,128]{1,0:T(8,128)(2,1)S(1)}, bf16[384,128]{1,0:T(8,128)(2,1)S(1)}, u32[]{:S(2)}, u32[]{:S(2)}) collective-permute-start(bf16[384,128]{1,0:T(8,128)(2,1)S(1)} %collective-permute-done.5.refs_3_), channel_id=1, source_target_pairs={{0,2},{2,0},{1,3},{3,1},{4,6},{6,4},{5,7},{7,5},{8,10},{10,8},{9,1... | collective-permute-start | bytes 294920 | tf_op jit(solution)/shard_map/ppermute | solution.py:60
  27.8 1.3 %load.1 = (bf16[4096,768]{1,0:T(8,128)(2,1)S(1)}, bf16[4096,768]{1,0:T(8,128)(2,1)S(1)}, bf16[768,4096]{1,0:T(8,128)(2,1)S(1)}) custom-call(bf16[4096,768]{1,0:T(8,128)(2,1)S(1)} %bitcast.10, bf16[4096,768]{1,0:T(8,128)(2,1)S(1)} %bitcast.13, bf16[768,4096]{1,0:T(8,128)(2,1)S(1)} %bitcast.16), custom_call_target="tpu_custom_call" | custom-call | tf_op jit(solution)/shard_map/load/pallas_call | solution.py:227
  29.1 0.8 %shard_map.95 = (f32[192,768]{1,0:T(8,128)S(1)}, f32[192,768]{1,0:T(8,128)S(1)}) custom-call(bf16[784,128]{1,0:T(8,128)(2,1)S(1)} %shard_map.92.refs_0_.refs_6_.refs_4_, bf16[400,128]{1,0:T(8,128)(2,1)S(1)} %collective-permute-done.7.refs_1_.refs_7_.refs_5_, bf16[784,128]{1,0:T(8,128)(2,1)S(1)} %collective-permute-done.3.refs_2_.refs_8_.refs_6_, ...), custom_call_target="tpu_custom_call" | custom-call | tf_op jit(solution)/shard_map/pallas_call | solution.py:22
  29.9 0.8 %shard_map.96 = (f32[192,768]{1,0:T(8,128)S(1)}, f32[192,768]{1,0:T(8,128)S(1)}) custom-call(bf16[784,128]{1,0:T(8,128)(2,1)S(1)} %shard_map.92.refs_0_.refs_6_.refs_4_, bf16[384,128]{1,0:T(8,128)(2,1)S(1)} %collective-permute-done.1.refs_1_, bf16[784,128]{1,0:T(8,128)(2,1)S(1)} %collective-permute-done.3.refs_2_.refs_8_.refs_6_, ...), custom_call_target="tpu_custom_call" | custom-call | tf_op jit(solution)/shard_map/pallas_call | solution.py:22
  30.8 0.8 %shard_map.97 = (f32[192,768]{1,0:T(8,128)S(1)}, f32[192,768]{1,0:T(8,128)S(1)}) custom-call(bf16[784,128]{1,0:T(8,128)(2,1)S(1)} %collective-permute-done.refs_0_, bf16[400,128]{1,0:T(8,128)(2,1)S(1)} %collective-permute-done.10.refs_1_, bf16[784,128]{1,0:T(8,128)(2,1)S(1)} %collective-permute-done.4.refs_2_, ...), custom_call_target="tpu_custom_call" | custom-call | tf_op jit(solution)/shard_map/pallas_call | solution.py:22
  31.7 1.3 %shard_map.98 = (bf16[192,768]{1,0:T(8,128)(2,1)S(1)}, bf16[192,128]{1,0:T(8,128)(2,1)S(1)}, bf16[192,128]{1,0:T(8,128)(2,1)S(1)}) custom-call(bf16[784,128]{1,0:T(8,128)(2,1)S(1)} %collective-permute-done.refs_0_, bf16[384,128]{1,0:T(8,128)(2,1)S(1)} %collective-permute-done.2.refs_1_, bf16[784,128]{1,0:T(8,128)(2,1)S(1)} %collective-permute-done.4.refs_2_, ...), custom_call_target="tpu_custom_call" | custom-call | tf_op jit(solution)/shard_map/pallas_call | solution.py:22
  33.0 0.8 %shard_map.100 = (bf16[768,128]{1,0:T(8,128)(2,1)S(1)}, bf16[768,128]{1,0:T(8,128)(2,1)S(1)}, bf16[576,128]{1,0:T(8,128)(2,1)S(1)}, bf16[768,128]{1,0:T(8,128)(2,1)S(1)}) custom-call(bf16[192,768]{1,0:T(8,128)(2,1)S(1)} %get-tuple-element.50.act_ref, bf16[768,4096]{1,0:T(8,128)(2,1)S(1)} %get-tuple-element.49.refs_15_.down_ref), custom_call_target="tpu_custom_call" | custom-call | tf_op jit(solution)/shard_map/pallas_call | solution.py:22
  33.8 2.1 %collective-permute-start.13 = (bf16[768,128]{1,0:T(8,128)(2,1)S(1)}, bf16[768,128]{1,0:T(8,128)(2,1)S(1)}, u32[]{:S(2)}, u32[]{:S(2)}) collective-permute-start(bf16[768,128]{1,0:T(8,128)(2,1)S(1)} %get-tuple-element.54), channel_id=1, source_target_pairs={{0,2},{2,0},{1,3},{3,1},{4,6},{6,4},{5,7},{7,5},{8,10},{10,8},{9,1... | collective-permute-start | bytes 589832 | tf_op jit(solution)/shard_map/ppermute | solution.py:60
  36.0 1.9 %collective-permute-start.17 = (bf16[576,128]{1,0:T(8,128)(2,1)S(1)}, bf16[576,128]{1,0:T(8,128)(2,1)S(1)}, u32[]{:S(2)}, u32[]{:S(2)}) collective-permute-start(bf16[576,128]{1,0:T(8,128)(2,1)S(1)} %get-tuple-element.58), channel_id=1, source_target_pairs={{0,2},{2,0},{1,3},{3,1},{4,6},{6,4},{5,7},{7,5},{8,10},{10,8},{9,1... | collective-permute-start | bytes 442376 | tf_op jit(solution)/shard_map/ppermute | solution.py:60
  37.9 0.8 %shard_map.99 = (bf16[768,128]{1,0:T(8,128)(2,1)S(1)}, bf16[768,128]{1,0:T(8,128)(2,1)S(1)}, bf16[576,128]{1,0:T(8,128)(2,1)S(1)}, bf16[768,128]{1,0:T(8,128)(2,1)S(1)}) custom-call(bf16[192,768]{1,0:T(8,128)(2,1)S(1)} %get-tuple-element.50.act_ref, bf16[768,4096]{1,0:T(8,128)(2,1)S(1)} %get-tuple-element.49.refs_15_.down_ref), custom_call_target="tpu_custom_call" | custom-call | tf_op jit(solution)/shard_map/pallas_call | solution.py:22
  38.9 2.8 %collective-permute-done.13.refs_1_ = bf16[768,128]{1,0:T(8,128)(2,1)S(1)} collective-permute-done((bf16[768,128]{1,0:T(8,128)(2,1)S(1)}, bf16[768,128]{1,0:T(8,128)(2,1)S(1)}, u32[]{:S(2)}, u32[]{:S(2)}) %collective-permute-start.13) | collective-permute-done | bytes 196640 | tf_op jit(solution)/shard_map/ppermute | solution.py:60
  41.7 0.7 %collective-permute-start.14 = (bf16[768,128]{1,0:T(8,128)(2,1)S(1)}, bf16[768,128]{1,0:T(8,128)(2,1)S(1)}, u32[]{:S(2)}, u32[]{:S(2)}) collective-permute-start(bf16[768,128]{1,0:T(8,128)(2,1)S(1)} %shard_map.101), channel_id=1, source_target_pairs={{4,0},{0,4},{12,8},{8,12},{5,1},{1,5},{13,9},{9,13},{6,2},{2,6},{1... | collective-permute-start | bytes 589832 | tf_op jit(solution)/shard_map/ppermute | solution.py:60
  42.4 3.5 %collective-permute-done.19.refs_1_ = bf16[768,128]{1,0:T(8,128)(2,1)S(1)} collective-permute-done((bf16[768,128]{1,0:T(8,128)(2,1)S(1)}, bf16[768,128]{1,0:T(8,128)(2,1)S(1)}, u32[]{:S(2)}, u32[]{:S(2)}) %collective-permute-start.19) | collective-permute-done | bytes 196640 | tf_op jit(solution)/shard_map/ppermute | solution.py:60
  45.9 3.5 %collective-permute-start.20 = (bf16[768,128]{1,0:T(8,128)(2,1)S(1)}, bf16[768,128]{1,0:T(8,128)(2,1)S(1)}, u32[]{:S(2)}, u32[]{:S(2)}) collective-permute-start(bf16[768,128]{1,0:T(8,128)(2,1)S(1)} %shard_map.105), channel_id=1, source_target_pairs={{12,0},{8,4},{4,8},{0,12},{13,1},{9,5},{5,9},{1,13},{14,2},{10,6},... | collective-permute-start | bytes 589832 | tf_op jit(solution)/shard_map/ppermute | solution.py:60
  49.4 2.2 %collective-permute-start.18 = (bf16[576,128]{1,0:T(8,128)(2,1)S(1)}, bf16[576,128]{1,0:T(8,128)(2,1)S(1)}, u32[]{:S(2)}, u32[]{:S(2)}) collective-permute-start(bf16[576,128]{1,0:T(8,128)(2,1)S(1)} %shard_map.103), channel_id=1, source_target_pairs={{8,0},{12,4},{0,8},{4,12},{9,1},{13,5},{1,9},{5,13},{10,2},{14,6},... | collective-permute-start | bytes 442376 | tf_op jit(solution)/shard_map/ppermute | solution.py:60
  52.0 3.8 %collective-permute-done.15.refs_1_ = bf16[192,128]{1,0:T(8,128)(2,1)S(1)} collective-permute-done((bf16[192,128]{1,0:T(8,128)(2,1)S(1)}, bf16[192,128]{1,0:T(8,128)(2,1)S(1)}, u32[]{:S(2)}, u32[]{:S(2)}) %collective-permute-start.15) | collective-permute-done | bytes 49184 | tf_op jit(solution)/shard_map/ppermute | solution.py:60
  55.7 0.9 %collective-permute-start.16 = (bf16[192,128]{1,0:T(8,128)(2,1)S(1)}, bf16[192,128]{1,0:T(8,128)(2,1)S(1)}, u32[]{:S(2)}, u32[]{:S(2)}) collective-permute-start(bf16[192,128]{1,0:T(8,128)(2,1)S(1)} %shard_map.102), channel_id=1, source_target_pairs={{8,0},{12,4},{0,8},{4,12},{9,1},{13,5},{1,9},{5,13},{10,2},{14,6},... | collective-permute-start | bytes 147464 | tf_op jit(solution)/shard_map/ppermute | solution.py:60
  56.6 6.1 %collective-permute-done.16.refs_5_ = bf16[192,128]{1,0:T(8,128)(2,1)S(1)} collective-permute-done((bf16[192,128]{1,0:T(8,128)(2,1)S(1)}, bf16[192,128]{1,0:T(8,128)(2,1)S(1)}, u32[]{:S(2)}, u32[]{:S(2)}) %collective-permute-start.16) | collective-permute-done | bytes 49184 | tf_op jit(solution)/shard_map/ppermute | solution.py:60
  62.8 0.6 shard_map.104
  63.4 1.1 %shard_map.106 = bf16[64,2048]{1,0:T(8,128)(2,1)} custom-call(f32[64,2048]{1,0:T(8,128)S(1)} %get-tuple-element.59.partial, bf16[48,64]{1,0:T(8,128)(2,1)S(1)} %get-tuple-element.60.refs_0_, bf16[48,64]{1,0:T(8,128)(2,1)S(1)} %get-tuple-element.61.refs_1_, bf16[48,64]{1,0:T(8,128)(2,1)S(1)} %get-tuple-element.62.refs_2_, ...), custom_call_target="tpu_custom_call" | custom-call | tf_op jit(solution)/shard_map/pallas_call | solution.py:22
  (50 shorter events, 1.5 us)
Async XLA Ops:
  1.4 15.2 %collective-permute-start.3 = (bf16[784,128]{1,0:T(8,128)(2,1)S(1)}, bf16[784,128]{1,0:T(8,128)(2,1)S(1)}, u32[]{:S(2)}, u32[]{:S(2)}) collective-permute-start(bf16[784,128]{1,0:T(8,128)(2,1)S(1)} %get-tuple-element.37), channel_id=1, source_target_pairs={{0,8},{4,12},{8,0},{12,4},{1,9},{5,13},{9,1},{13,5},{2,10},{6,14},... | collective-permute-start | bytes 602120 | tf_op jit(solution)/shard_map/ppermute | solution.py:60
  5.5 22.2 %slice-start = ((s8[6291456]{0:T(1024)(128)(4,1)}), s8[4194304]{0:T(1024)(128)(4,1)S(1)}, s32[]{:S(2)}) async-start(s8[6291456]{0:T(1024)(128)(4,1)} %bitcast.8), calls=%async_computation | async-start | bytes 8388608
  5.5 22.2 %slice-start.2 = ((s8[6291456]{0:T(1024)(128)(4,1)}), s8[4194304]{0:T(1024)(128)(4,1)S(1)}, s32[]{:S(2)}) async-start(s8[6291456]{0:T(1024)(128)(4,1)} %bitcast.11), calls=%async_computation.2 | async-start | bytes 8388608
  5.5 22.2 %slice-start.4 = ((s8[6291456]{0:T(1024)(128)(4,1)}), s8[4194304]{0:T(1024)(128)(4,1)S(1)}, s32[]{:S(2)}) async-start(s8[6291456]{0:T(1024)(128)(4,1)} %bitcast.14), calls=%async_computation.4 | async-start | bytes 8388608
  5.5 21.5 %copy-start = (bf16[1,2048,128]{2,1,0:T(8,128)(2,1)S(1)}, bf16[1,2048,128]{2,1,0:T(8,128)(2,1)}, u32[]{:S(2)}) copy-start(bf16[1,2048,128]{2,1,0:T(8,128)(2,1)} %param.16) | copy-start | bytes 1572868
  5.5 22.2 %slice-start.1 = ((s8[6291456]{0:T(1024)(128)(4,1)}), s8[2097152]{0:T(1024)(128)(4,1)S(1)}, s32[]{:S(2)}) async-start(s8[6291456]{0:T(1024)(128)(4,1)} %bitcast.8), calls=%async_computation.1 | async-start | bytes 4194304
  5.5 22.2 %slice-start.3 = ((s8[6291456]{0:T(1024)(128)(4,1)}), s8[2097152]{0:T(1024)(128)(4,1)S(1)}, s32[]{:S(2)}) async-start(s8[6291456]{0:T(1024)(128)(4,1)} %bitcast.11), calls=%async_computation.3 | async-start | bytes 4194304
  5.5 22.2 %slice-start.5 = ((s8[6291456]{0:T(1024)(128)(4,1)}), s8[2097152]{0:T(1024)(128)(4,1)S(1)}, s32[]{:S(2)}) async-start(s8[6291456]{0:T(1024)(128)(4,1)} %bitcast.14), calls=%async_computation.5 | async-start | bytes 4194304
  5.6 19.4 %collective-permute-start = (bf16[784,128]{1,0:T(8,128)(2,1)S(1)}, bf16[784,128]{1,0:T(8,128)(2,1)S(1)}, u32[]{:S(2)}, u32[]{:S(2)}) collective-permute-start(bf16[784,128]{1,0:T(8,128)(2,1)S(1)} %shard_map.92.refs_0_.refs_6_.refs_4_), channel_id=1, source_target_pairs={{0,2},{2,0},{1,3},{3,1},{4,6},{6,4},{5,7},{7,5},{8,10},{10,8},{9,1... | collective-permute-start | bytes 602120 | tf_op jit(solution)/shard_map/ppermute | solution.py:60
  7.1 11.4 %collective-permute-start.1 = (bf16[384,128]{1,0:T(8,128)(2,1)S(1)}, bf16[384,128]{1,0:T(8,128)(2,1)S(1)}, u32[]{:S(2)}, u32[]{:S(2)}) collective-permute-start(bf16[384,128]{1,0:T(8,128)(2,1)S(1)} %get-tuple-element.36), channel_id=1, source_target_pairs={{0,4},{4,0},{8,12},{12,8},{1,5},{5,1},{9,13},{13,9},{2,6},{6,2},{1... | collective-permute-start | bytes 294920 | tf_op jit(solution)/shard_map/ppermute | solution.py:60
  8.7 12.3 %collective-permute-start.7 = (bf16[400,128]{1,0:T(8,128)(2,1)S(1)}, bf16[400,128]{1,0:T(8,128)(2,1)S(1)}, u32[]{:S(2)}, u32[]{:S(2)}) collective-permute-start(bf16[400,128]{1,0:T(8,128)(2,1)S(1)} %get-tuple-element.39), channel_id=1, source_target_pairs={{0,4},{4,0},{8,12},{12,8},{1,5},{5,1},{9,13},{13,9},{2,6},{6,2},{1... | collective-permute-start | bytes 307208 | tf_op jit(solution)/shard_map/ppermute | solution.py:60
  9.1 12.5 %collective-permute-start.8 = (bf16[400,128]{1,0:T(8,128)(2,1)S(1)}, bf16[400,128]{1,0:T(8,128)(2,1)S(1)}, u32[]{:S(2)}, u32[]{:S(2)}) collective-permute-start(bf16[400,128]{1,0:T(8,128)(2,1)S(1)} %get-tuple-element.40), channel_id=1, source_target_pairs={{0,12},{4,8},{8,4},{12,0},{1,13},{5,9},{9,5},{13,1},{2,14},{6,10},... | collective-permute-start | bytes 307208 | tf_op jit(solution)/shard_map/ppermute | solution.py:60
  16.6 14.2 %collective-permute-start.4 = (bf16[784,128]{1,0:T(8,128)(2,1)S(1)}, bf16[784,128]{1,0:T(8,128)(2,1)S(1)}, u32[]{:S(2)}, u32[]{:S(2)}) collective-permute-start(bf16[784,128]{1,0:T(8,128)(2,1)S(1)} %collective-permute-done.3.refs_2_.refs_8_.refs_6_), channel_id=1, source_target_pairs={{0,2},{2,0},{1,3},{3,1},{4,6},{6,4},{5,7},{7,5},{8,10},{10,8},{9,1... | collective-permute-start | bytes 602120 | tf_op jit(solution)/shard_map/ppermute | solution.py:60
  18.6 6.4 %collective-permute-start.5 = (bf16[384,128]{1,0:T(8,128)(2,1)S(1)}, bf16[384,128]{1,0:T(8,128)(2,1)S(1)}, u32[]{:S(2)}, u32[]{:S(2)}) collective-permute-start(bf16[384,128]{1,0:T(8,128)(2,1)S(1)} %get-tuple-element.38), channel_id=1, source_target_pairs={{0,12},{4,8},{8,4},{12,0},{1,13},{5,9},{9,5},{13,1},{2,14},{6,10},... | collective-permute-start | bytes 294920 | tf_op jit(solution)/shard_map/ppermute | solution.py:60
  21.0 6.6 %collective-permute-start.10 = (bf16[400,128]{1,0:T(8,128)(2,1)S(1)}, bf16[400,128]{1,0:T(8,128)(2,1)S(1)}, u32[]{:S(2)}, u32[]{:S(2)}) collective-permute-start(bf16[400,128]{1,0:T(8,128)(2,1)S(1)} %collective-permute-done.7.refs_1_.refs_7_.refs_5_), channel_id=1, source_target_pairs={{0,2},{2,0},{1,3},{3,1},{4,6},{6,4},{5,7},{7,5},{8,10},{10,8},{9,1... | collective-permute-start | bytes 307208 | tf_op jit(solution)/shard_map/ppermute | solution.py:60
  21.6 9.1 %collective-permute-start.11 = (bf16[400,128]{1,0:T(8,128)(2,1)S(1)}, bf16[400,128]{1,0:T(8,128)(2,1)S(1)}, u32[]{:S(2)}, u32[]{:S(2)}) collective-permute-start(bf16[400,128]{1,0:T(8,128)(2,1)S(1)} %collective-permute-done.8.refs_3_.refs_9_.refs_7_), channel_id=1, source_target_pairs={{0,2},{2,0},{1,3},{3,1},{4,6},{6,4},{5,7},{7,5},{8,10},{10,8},{9,1... | collective-permute-start | bytes 307208 | tf_op jit(solution)/shard_map/ppermute | solution.py:60
  25.0 6.6 %collective-permute-start.2 = (bf16[384,128]{1,0:T(8,128)(2,1)S(1)}, bf16[384,128]{1,0:T(8,128)(2,1)S(1)}, u32[]{:S(2)}, u32[]{:S(2)}) collective-permute-start(bf16[384,128]{1,0:T(8,128)(2,1)S(1)} %collective-permute-done.1.refs_1_), channel_id=1, source_target_pairs={{0,2},{2,0},{1,3},{3,1},{4,6},{6,4},{5,7},{7,5},{8,10},{10,8},{9,1... | collective-permute-start | bytes 294920 | tf_op jit(solution)/shard_map/ppermute | solution.py:60
  25.0 6.6 %collective-permute-start.6 = (bf16[384,128]{1,0:T(8,128)(2,1)S(1)}, bf16[384,128]{1,0:T(8,128)(2,1)S(1)}, u32[]{:S(2)}, u32[]{:S(2)}) collective-permute-start(bf16[384,128]{1,0:T(8,128)(2,1)S(1)} %collective-permute-done.5.refs_3_), channel_id=1, source_target_pairs={{0,2},{2,0},{1,3},{3,1},{4,6},{6,4},{5,7},{7,5},{8,10},{10,8},{9,1... | collective-permute-start | bytes 294920 | tf_op jit(solution)/shard_map/ppermute | solution.py:60
  27.6 4.0 %collective-permute-start.9 = (f32[8,192]{1,0:T(8,128)S(1)}, f32[8,192]{1,0:T(8,128)S(1)}, u32[]{:S(2)}, u32[]{:S(2)}) collective-permute-start(f32[8,192]{1,0:T(8,128)S(1)} %shard_map.94.refs_8_), channel_id=1, source_target_pairs={{0,2},{2,0},{1,3},{3,1},{4,6},{6,4},{5,7},{7,5},{8,10},{10,8},{9,1... | collective-permute-start | bytes 18440 | tf_op jit(solution)/shard_map/ppermute | solution.py:60
  30.8 0.9 %copy-start.1 = (bf16[1,128,768]{2,1,0:T(8,128)(2,1)S(1)}, bf16[1,128,768]{2,1,0:T(8,128)(2,1)}, u32[]{:S(2)}) copy-start(bf16[1,128,768]{2,1,0:T(8,128)(2,1)} %param.17) | copy-start | bytes 589828
  33.0 29.8 %copy-start.2 = (s32[64,2]{0,1:T(2,128)S(1)}, s32[64,2]{0,1:T(2,128)}, u32[]{:S(2)}) copy-start(s32[64,2]{0,1:T(2,128)} %param.10) | copy-start | bytes 1540
  33.0 29.8 %copy-start.3 = (f32[64,2]{0,1:T(2,128)S(1)}, f32[64,2]{0,1:T(2,128)}, u32[]{:S(2)}) copy-start(f32[64,2]{0,1:T(2,128)} %param.11) | copy-start | bytes 1540
  33.8 7.8 %collective-permute-start.13 = (bf16[768,128]{1,0:T(8,128)(2,1)S(1)}, bf16[768,128]{1,0:T(8,128)(2,1)S(1)}, u32[]{:S(2)}, u32[]{:S(2)}) collective-permute-start(bf16[768,128]{1,0:T(8,128)(2,1)S(1)} %get-tuple-element.54), channel_id=1, source_target_pairs={{0,2},{2,0},{1,3},{3,1},{4,6},{6,4},{5,7},{7,5},{8,10},{10,8},{9,1... | collective-permute-start | bytes 589832 | tf_op jit(solution)/shard_map/ppermute | solution.py:60
  35.9 10.0 %collective-permute-start.19 = (bf16[768,128]{1,0:T(8,128)(2,1)S(1)}, bf16[768,128]{1,0:T(8,128)(2,1)S(1)}, u32[]{:S(2)}, u32[]{:S(2)}) collective-permute-start(bf16[768,128]{1,0:T(8,128)(2,1)S(1)} %get-tuple-element.64), channel_id=1, source_target_pairs={{0,2},{2,0},{1,3},{3,1},{4,6},{6,4},{5,7},{7,5},{8,10},{10,8},{9,1... | collective-permute-start | bytes 589832 | tf_op jit(solution)/shard_map/ppermute | solution.py:60
  36.0 13.4 %collective-permute-start.17 = (bf16[576,128]{1,0:T(8,128)(2,1)S(1)}, bf16[576,128]{1,0:T(8,128)(2,1)S(1)}, u32[]{:S(2)}, u32[]{:S(2)}) collective-permute-start(bf16[576,128]{1,0:T(8,128)(2,1)S(1)} %get-tuple-element.58), channel_id=1, source_target_pairs={{0,2},{2,0},{1,3},{3,1},{4,6},{6,4},{5,7},{7,5},{8,10},{10,8},{9,1... | collective-permute-start | bytes 442376 | tf_op jit(solution)/shard_map/ppermute | solution.py:60
  38.7 24.0 %collective-permute-start.12 = (bf16[768,128]{1,0:T(8,128)(2,1)S(1)}, bf16[768,128]{1,0:T(8,128)(2,1)S(1)}, u32[]{:S(2)}, u32[]{:S(2)}) collective-permute-start(bf16[768,128]{1,0:T(8,128)(2,1)S(1)} %get-tuple-element.52), channel_id=1, source_target_pairs={{0,2},{2,0},{1,3},{3,1},{4,6},{6,4},{5,7},{7,5},{8,10},{10,8},{9,1... | collective-permute-start | bytes 589832 | tf_op jit(solution)/shard_map/ppermute | solution.py:60
  41.7 21.0 %collective-permute-start.14 = (bf16[768,128]{1,0:T(8,128)(2,1)S(1)}, bf16[768,128]{1,0:T(8,128)(2,1)S(1)}, u32[]{:S(2)}, u32[]{:S(2)}) collective-permute-start(bf16[768,128]{1,0:T(8,128)(2,1)S(1)} %shard_map.101), channel_id=1, source_target_pairs={{4,0},{0,4},{12,8},{8,12},{5,1},{1,5},{13,9},{9,13},{6,2},{2,6},{1... | collective-permute-start | bytes 589832 | tf_op jit(solution)/shard_map/ppermute | solution.py:60
  45.9 17.4 %collective-permute-start.20 = (bf16[768,128]{1,0:T(8,128)(2,1)S(1)}, bf16[768,128]{1,0:T(8,128)(2,1)S(1)}, u32[]{:S(2)}, u32[]{:S(2)}) collective-permute-start(bf16[768,128]{1,0:T(8,128)(2,1)S(1)} %shard_map.105), channel_id=1, source_target_pairs={{12,0},{8,4},{4,8},{0,12},{13,1},{9,5},{5,9},{1,13},{14,2},{10,6},... | collective-permute-start | bytes 589832 | tf_op jit(solution)/shard_map/ppermute | solution.py:60
  49.4 13.3 %collective-permute-start.18 = (bf16[576,128]{1,0:T(8,128)(2,1)S(1)}, bf16[576,128]{1,0:T(8,128)(2,1)S(1)}, u32[]{:S(2)}, u32[]{:S(2)}) collective-permute-start(bf16[576,128]{1,0:T(8,128)(2,1)S(1)} %shard_map.103), channel_id=1, source_target_pairs={{8,0},{12,4},{0,8},{4,12},{9,1},{13,5},{1,9},{5,13},{10,2},{14,6},... | collective-permute-start | bytes 442376 | tf_op jit(solution)/shard_map/ppermute | solution.py:60
  51.6 4.1 %collective-permute-start.15 = (bf16[192,128]{1,0:T(8,128)(2,1)S(1)}, bf16[192,128]{1,0:T(8,128)(2,1)S(1)}, u32[]{:S(2)}, u32[]{:S(2)}) collective-permute-start(bf16[192,128]{1,0:T(8,128)(2,1)S(1)} %get-tuple-element.56), channel_id=1, source_target_pairs={{0,2},{2,0},{1,3},{3,1},{4,6},{6,4},{5,7},{7,5},{8,10},{10,8},{9,1... | collective-permute-start | bytes 147464 | tf_op jit(solution)/shard_map/ppermute | solution.py:60
  55.7 7.0 %collective-permute-start.16 = (bf16[192,128]{1,0:T(8,128)(2,1)S(1)}, bf16[192,128]{1,0:T(8,128)(2,1)S(1)}, u32[]{:S(2)}, u32[]{:S(2)}) collective-permute-start(bf16[192,128]{1,0:T(8,128)(2,1)S(1)} %shard_map.102), channel_id=1, source_target_pairs={{8,0},{12,4},{0,8},{4,12},{9,1},{13,5},{1,9},{5,13},{10,2},{14,6},... | collective-permute-start | bytes 147464 | tf_op jit(solution)/shard_map/ppermute | solution.py:60

commit v3 on v2

--- a/solution.py
+++ b/solution.py
@@ -18,12 +18,12 @@
 BF16 = jnp.bfloat16
 
 
-def call(body, outs, ins, in_specs=None, scratch=(), flops=0):
+def call(body, outs, ins, in_specs=None, scratch=(), flops=0, out_specs=None):
     return pl.pallas_call(
         body,
         out_shape=outs,
         in_specs=in_specs or [VMEM] * len(ins),
-        out_specs=[VMEM] * len(outs),
+        out_specs=out_specs or [VMEM] * len(outs),
         scratch_shapes=list(scratch),
         compiler_params=pltpu.CompilerParams(vmem_limit_bytes=LIMIT),
         cost_estimate=pl.CostEstimate(flops=flops, bytes_accessed=flops // 160, transcendentals=0),
@@ -443,7 +443,9 @@
             rows += [
                 home[i].load(r, lo, hi) for i, r in zip(early, others_in) if home[i].covers(lo, hi)
             ]
-            refs[-4][:, lo:hi] = mixed_sum(terms, jnp.concatenate(rows, axis=0))
+            n = len(rows) * cap
+            rows = jnp.concatenate(rows, axis=0)
+            refs[-4][:, lo:hi] = mixed_sum([t[:n] for t in terms], rows)
         for ref, t in zip(refs[-3:], mixing(refs[0][...], refs[1][...], [home[final].step])):
             ref[...] = t
 
@@ -455,17 +457,29 @@
     )
 
     def finish(partial, *refs):
-        terms, out = [r[...] for r in refs[:3]], refs[-1]
-        for lo, hi in home_segments:
+        terms, out, staged, sems = [r[...] for r in refs[:3]], refs[-3], refs[-2], refs[-1]
+        copies = []
+        for i, (lo, hi) in enumerate(home_segments):
             value = partial[:, lo:hi]
-            if final:
+            if final and home[final].covers(lo, hi):
                 value = value + mixed_sum(terms, home[final].load(refs[3], lo, hi))
-            out[:, lo:hi] = value.astype(BF16)
+            staged[:, lo:hi] = value.astype(BF16)
+            copies.append(
+                pltpu.make_async_copy(staged.at[:, lo:hi], out.at[:, lo:hi], sems.at[i])
+            )
+            copies[-1].start()
+        for c in copies:
+            c.wait()
 
     (result,) = call(
         finish,
         [jax.ShapeDtypeStruct((tok_rows, part), BF16)],
         (mixed, *final_terms, *([returned[final]] if final else [])),
+        out_specs=[ANY],
+        scratch=[
+            pltpu.VMEM((tok_rows, part), BF16),
+            pltpu.SemaphoreType.DMA((len(home_segments),)),
+        ],
     )
     return result
 

time: 64.6 us -> 64.6 us (level)
  no operation moved by 1% of the time
where the time goes in v3:
time: 64.6 us; the launch traced here: 64.4 us
  starting transfers between devices  29.4 us (46%)
  waiting for transfers between devices  24.2 us (37%)
  Pallas kernels  10.4 us (16%)
    ppermute x21, starting transfers between devices, permute(): return lax.ppermute(value, axis, pairs)  29.4 us
    ppermute x21, waiting for transfers between devices, permute(): return lax.ppermute(value, axis, pairs)  24.2 us
    pallas_call x16, Pallas kernels, call(): pl.pallas_call(body, out_shape=outs, in_specs=in_specs or [VMEM] * len(in...  9.15 us
  transfers between devices with their start and end apart: 21, of which 6 were waited for; matrix products, arithmetic and copies ran while one was open for 0% of the time, Pallas kernels for 9%

profile of v3, /device:TPU:0, one launch (start us, length us, event | category | flops | bytes accessed | tf_op | source)
XLA Modules:
  0.0 64.4 jit_solution(9062623399030324823)
XLA Ops:
  0.0 1.4 %shard_map.91 = (bf16[784,128]{1,0:T(8,128)(2,1)S(1)}, bf16[400,128]{1,0:T(8,128)(2,1)S(1)}, bf16[384,128]{1,0:T(8,128)(2,1)S(1)}, bf16[784,128]{1,0:T(8,128)(2,...) custom-call(s32[2,64]{1,0:T(2,128)} %bitcast.20, s32[4,8]{1,0:T(4,128)} %bitcast.23, ...), custom_call_target="tpu_custom_call" | custom-call | tf_op jit(solution)/shard_map/pallas_call | solution.py:22
  1.4 4.1 %collective-permute-start.3 = (bf16[784,128]{1,0:T(8,128)(2,1)S(1)}, bf16[784,128]{1,0:T(8,128)(2,1)S(1)}, u32[]{:S(2)}, u32[]{:S(2)}) collective-permute-start(bf16[784,128]{1,0:T(8,128)(2,1)S(1)} %get-tuple-element.37), channel_id=1, source_target_pairs={{0,8},{4,12},{8,0},{12,4},{1,9},{5,13},{9,1},{13,5},{2,10},{6,14},... | collective-permute-start | bytes 602120 | tf_op jit(solution)/shard_map/ppermute | solution.py:60
  5.6 1.6 %collective-permute-start = (bf16[784,128]{1,0:T(8,128)(2,1)S(1)}, bf16[784,128]{1,0:T(8,128)(2,1)S(1)}, u32[]{:S(2)}, u32[]{:S(2)}) collective-permute-start(bf16[784,128]{1,0:T(8,128)(2,1)S(1)} %shard_map.92.refs_0_.refs_6_.refs_4_), channel_id=1, source_target_pairs={{0,2},{2,0},{1,3},{3,1},{4,6},{6,4},{5,7},{7,5},{8,10},{10,8},{9,1... | collective-permute-start | bytes 602120 | tf_op jit(solution)/shard_map/ppermute | solution.py:60
  7.1 1.6 %collective-permute-start.1 = (bf16[384,128]{1,0:T(8,128)(2,1)S(1)}, bf16[384,128]{1,0:T(8,128)(2,1)S(1)}, u32[]{:S(2)}, u32[]{:S(2)}) collective-permute-start(bf16[384,128]{1,0:T(8,128)(2,1)S(1)} %get-tuple-element.36), channel_id=1, source_target_pairs={{0,4},{4,0},{8,12},{12,8},{1,5},{5,1},{9,13},{13,9},{2,6},{6,2},{1... | collective-permute-start | bytes 294920 | tf_op jit(solution)/shard_map/ppermute | solution.py:60
  8.7 0.4 collective-permute-start.7
  9.1 1.3 %collective-permute-start.8 = (bf16[400,128]{1,0:T(8,128)(2,1)S(1)}, bf16[400,128]{1,0:T(8,128)(2,1)S(1)}, u32[]{:S(2)}, u32[]{:S(2)}) collective-permute-start(bf16[400,128]{1,0:T(8,128)(2,1)S(1)} %get-tuple-element.40), channel_id=1, source_target_pairs={{0,12},{4,8},{8,4},{12,0},{1,13},{5,9},{9,5},{13,1},{2,14},{6,10},... | collective-permute-start | bytes 307208 | tf_op jit(solution)/shard_map/ppermute | solution.py:60
  10.5 6.1 %collective-permute-done.3.refs_2_.refs_8_.refs_6_ = bf16[784,128]{1,0:T(8,128)(2,1)S(1)} collective-permute-done((bf16[784,128]{1,0:T(8,128)(2,1)S(1)}, bf16[784,128]{1,0:T(8,128)(2,1)S(1)}, u32[]{:S(2)}, u32[]{:S(2)}) %collective-permute-start.3) | collective-permute-done | bytes 200736 | tf_op jit(solution)/shard_map/ppermute | solution.py:60
  16.6 2.0 %collective-permute-start.4 = (bf16[784,128]{1,0:T(8,128)(2,1)S(1)}, bf16[784,128]{1,0:T(8,128)(2,1)S(1)}, u32[]{:S(2)}, u32[]{:S(2)}) collective-permute-start(bf16[784,128]{1,0:T(8,128)(2,1)S(1)} %collective-permute-done.3.refs_2_.refs_8_.refs_6_), channel_id=1, source_target_pairs={{0,2},{2,0},{1,3},{3,1},{4,6},{6,4},{5,7},{7,5},{8,10},{10,8},{9,1... | collective-permute-start | bytes 602120 | tf_op jit(solution)/shard_map/ppermute | solution.py:60
  18.6 2.5 %collective-permute-start.5 = (bf16[384,128]{1,0:T(8,128)(2,1)S(1)}, bf16[384,128]{1,0:T(8,128)(2,1)S(1)}, u32[]{:S(2)}, u32[]{:S(2)}) collective-permute-start(bf16[384,128]{1,0:T(8,128)(2,1)S(1)} %get-tuple-element.38), channel_id=1, source_target_pairs={{0,12},{4,8},{8,4},{12,0},{1,13},{5,9},{9,5},{13,1},{2,14},{6,10},... | collective-permute-start | bytes 294920 | tf_op jit(solution)/shard_map/ppermute | solution.py:60
  21.0 0.6 collective-permute-start.10
  21.6 1.5 %collective-permute-start.11 = (bf16[400,128]{1,0:T(8,128)(2,1)S(1)}, bf16[400,128]{1,0:T(8,128)(2,1)S(1)}, u32[]{:S(2)}, u32[]{:S(2)}) collective-permute-start(bf16[400,128]{1,0:T(8,128)(2,1)S(1)} %collective-permute-done.8.refs_3_.refs_9_.refs_7_), channel_id=1, source_target_pairs={{0,2},{2,0},{1,3},{3,1},{4,6},{6,4},{5,7},{7,5},{8,10},{10,8},{9,1... | collective-permute-start | bytes 307208 | tf_op jit(solution)/shard_map/ppermute | solution.py:60
  23.1 1.9 %collective-permute-done.5.refs_3_ = bf16[384,128]{1,0:T(8,128)(2,1)S(1)} collective-permute-done((bf16[384,128]{1,0:T(8,128)(2,1)S(1)}, bf16[384,128]{1,0:T(8,128)(2,1)S(1)}, u32[]{:S(2)}, u32[]{:S(2)}) %collective-permute-start.5) | collective-permute-done | bytes 98336 | tf_op jit(solution)/shard_map/ppermute | solution.py:60
  25.0 2.0 %collective-permute-start.6 = (bf16[384,128]{1,0:T(8,128)(2,1)S(1)}, bf16[384,128]{1,0:T(8,128)(2,1)S(1)}, u32[]{:S(2)}, u32[]{:S(2)}) collective-permute-start(bf16[384,128]{1,0:T(8,128)(2,1)S(1)} %collective-permute-done.5.refs_3_), channel_id=1, source_target_pairs={{0,2},{2,0},{1,3},{3,1},{4,6},{6,4},{5,7},{7,5},{8,10},{10,8},{9,1... | collective-permute-start | bytes 294920 | tf_op jit(solution)/shard_map/ppermute | solution.py:60
  27.8 1.3 %load.1 = (bf16[4096,768]{1,0:T(8,128)(2,1)S(1)}, bf16[4096,768]{1,0:T(8,128)(2,1)S(1)}, bf16[768,4096]{1,0:T(8,128)(2,1)S(1)}) custom-call(bf16[4096,768]{1,0:T(8,128)(2,1)S(1)} %bitcast.10, bf16[4096,768]{1,0:T(8,128)(2,1)S(1)} %bitcast.13, bf16[768,4096]{1,0:T(8,128)(2,1)S(1)} %bitcast.16), custom_call_target="tpu_custom_call" | custom-call | tf_op jit(solution)/shard_map/load/pallas_call | solution.py:227
  29.1 0.8 %shard_map.95 = (f32[192,768]{1,0:T(8,128)S(1)}, f32[192,768]{1,0:T(8,128)S(1)}) custom-call(bf16[784,128]{1,0:T(8,128)(2,1)S(1)} %shard_map.92.refs_0_.refs_6_.refs_4_, bf16[400,128]{1,0:T(8,128)(2,1)S(1)} %collective-permute-done.7.refs_1_.refs_7_.refs_5_, bf16[784,128]{1,0:T(8,128)(2,1)S(1)} %collective-permute-done.3.refs_2_.refs_8_.refs_6_, ...), custom_call_target="tpu_custom_call" | custom-call | tf_op jit(solution)/shard_map/pallas_call | solution.py:22
  29.9 0.8 %shard_map.96 = (f32[192,768]{1,0:T(8,128)S(1)}, f32[192,768]{1,0:T(8,128)S(1)}) custom-call(bf16[784,128]{1,0:T(8,128)(2,1)S(1)} %shard_map.92.refs_0_.refs_6_.refs_4_, bf16[384,128]{1,0:T(8,128)(2,1)S(1)} %collective-permute-done.1.refs_1_, bf16[784,128]{1,0:T(8,128)(2,1)S(1)} %collective-permute-done.3.refs_2_.refs_8_.refs_6_, ...), custom_call_target="tpu_custom_call" | custom-call | tf_op jit(solution)/shard_map/pallas_call | solution.py:22
  30.8 0.8 %shard_map.97 = (f32[192,768]{1,0:T(8,128)S(1)}, f32[192,768]{1,0:T(8,128)S(1)}) custom-call(bf16[784,128]{1,0:T(8,128)(2,1)S(1)} %collective-permute-done.refs_0_, bf16[400,128]{1,0:T(8,128)(2,1)S(1)} %collective-permute-done.10.refs_1_, bf16[784,128]{1,0:T(8,128)(2,1)S(1)} %collective-permute-done.4.refs_2_, ...), custom_call_target="tpu_custom_call" | custom-call | tf_op jit(solution)/shard_map/pallas_call | solution.py:22
  31.7 1.3 %shard_map.98 = (bf16[192,768]{1,0:T(8,128)(2,1)S(1)}, bf16[192,128]{1,0:T(8,128)(2,1)S(1)}, bf16[192,128]{1,0:T(8,128)(2,1)S(1)}) custom-call(bf16[784,128]{1,0:T(8,128)(2,1)S(1)} %collective-permute-done.refs_0_, bf16[384,128]{1,0:T(8,128)(2,1)S(1)} %collective-permute-done.2.refs_1_, bf16[784,128]{1,0:T(8,128)(2,1)S(1)} %collective-permute-done.4.refs_2_, ...), custom_call_target="tpu_custom_call" | custom-call | tf_op jit(solution)/shard_map/pallas_call | solution.py:22
  33.0 0.8 %shard_map.100 = (bf16[768,128]{1,0:T(8,128)(2,1)S(1)}, bf16[768,128]{1,0:T(8,128)(2,1)S(1)}, bf16[576,128]{1,0:T(8,128)(2,1)S(1)}, bf16[768,128]{1,0:T(8,128)(2,1)S(1)}) custom-call(bf16[192,768]{1,0:T(8,128)(2,1)S(1)} %get-tuple-element.50.act_ref, bf16[768,4096]{1,0:T(8,128)(2,1)S(1)} %get-tuple-element.49.refs_15_.down_ref), custom_call_target="tpu_custom_call" | custom-call | tf_op jit(solution)/shard_map/pallas_call | solution.py:22
  33.8 2.1 %collective-permute-start.13 = (bf16[768,128]{1,0:T(8,128)(2,1)S(1)}, bf16[768,128]{1,0:T(8,128)(2,1)S(1)}, u32[]{:S(2)}, u32[]{:S(2)}) collective-permute-start(bf16[768,128]{1,0:T(8,128)(2,1)S(1)} %get-tuple-element.54), channel_id=1, source_target_pairs={{0,2},{2,0},{1,3},{3,1},{4,6},{6,4},{5,7},{7,5},{8,10},{10,8},{9,1... | collective-permute-start | bytes 589832 | tf_op jit(solution)/shard_map/ppermute | solution.py:60
  36.0 1.9 %collective-permute-start.17 = (bf16[576,128]{1,0:T(8,128)(2,1)S(1)}, bf16[576,128]{1,0:T(8,128)(2,1)S(1)}, u32[]{:S(2)}, u32[]{:S(2)}) collective-permute-start(bf16[576,128]{1,0:T(8,128)(2,1)S(1)} %get-tuple-element.58), channel_id=1, source_target_pairs={{0,2},{2,0},{1,3},{3,1},{4,6},{6,4},{5,7},{7,5},{8,10},{10,8},{9,1... | collective-permute-start | bytes 442376 | tf_op jit(solution)/shard_map/ppermute | solution.py:60
  37.9 0.8 %shard_map.99 = (bf16[768,128]{1,0:T(8,128)(2,1)S(1)}, bf16[768,128]{1,0:T(8,128)(2,1)S(1)}, bf16[576,128]{1,0:T(8,128)(2,1)S(1)}, bf16[768,128]{1,0:T(8,128)(2,1)S(1)}) custom-call(bf16[192,768]{1,0:T(8,128)(2,1)S(1)} %get-tuple-element.50.act_ref, bf16[768,4096]{1,0:T(8,128)(2,1)S(1)} %get-tuple-element.49.refs_15_.down_ref), custom_call_target="tpu_custom_call" | custom-call | tf_op jit(solution)/shard_map/pallas_call | solution.py:22
  38.9 2.8 %collective-permute-done.13.refs_1_ = bf16[768,128]{1,0:T(8,128)(2,1)S(1)} collective-permute-done((bf16[768,128]{1,0:T(8,128)(2,1)S(1)}, bf16[768,128]{1,0:T(8,128)(2,1)S(1)}, u32[]{:S(2)}, u32[]{:S(2)}) %collective-permute-start.13) | collective-permute-done | bytes 196640 | tf_op jit(solution)/shard_map/ppermute | solution.py:60
  41.7 0.7 %collective-permute-start.14 = (bf16[768,128]{1,0:T(8,128)(2,1)S(1)}, bf16[768,128]{1,0:T(8,128)(2,1)S(1)}, u32[]{:S(2)}, u32[]{:S(2)}) collective-permute-start(bf16[768,128]{1,0:T(8,128)(2,1)S(1)} %shard_map.101), channel_id=1, source_target_pairs={{4,0},{0,4},{12,8},{8,12},{5,1},{1,5},{13,9},{9,13},{6,2},{2,6},{1... | collective-permute-start | bytes 589832 | tf_op jit(solution)/shard_map/ppermute | solution.py:60
  42.4 3.5 %collective-permute-done.19.refs_1_ = bf16[768,128]{1,0:T(8,128)(2,1)S(1)} collective-permute-done((bf16[768,128]{1,0:T(8,128)(2,1)S(1)}, bf16[768,128]{1,0:T(8,128)(2,1)S(1)}, u32[]{:S(2)}, u32[]{:S(2)}) %collective-permute-start.19) | collective-permute-done | bytes 196640 | tf_op jit(solution)/shard_map/ppermute | solution.py:60
  45.9 3.5 %collective-permute-start.20 = (bf16[768,128]{1,0:T(8,128)(2,1)S(1)}, bf16[768,128]{1,0:T(8,128)(2,1)S(1)}, u32[]{:S(2)}, u32[]{:S(2)}) collective-permute-start(bf16[768,128]{1,0:T(8,128)(2,1)S(1)} %shard_map.105), channel_id=1, source_target_pairs={{12,0},{8,4},{4,8},{0,12},{13,1},{9,5},{5,9},{1,13},{14,2},{10,6},... | collective-permute-start | bytes 589832 | tf_op jit(solution)/shard_map/ppermute | solution.py:60
  49.4 2.2 %collective-permute-start.18 = (bf16[576,128]{1,0:T(8,128)(2,1)S(1)}, bf16[576,128]{1,0:T(8,128)(2,1)S(1)}, u32[]{:S(2)}, u32[]{:S(2)}) collective-permute-start(bf16[576,128]{1,0:T(8,128)(2,1)S(1)} %shard_map.103), channel_id=1, source_target_pairs={{8,0},{12,4},{0,8},{4,12},{9,1},{13,5},{1,9},{5,13},{10,2},{14,6},... | collective-permute-start | bytes 442376 | tf_op jit(solution)/shard_map/ppermute | solution.py:60
  52.0 3.8 %collective-permute-done.15.refs_1_ = bf16[192,128]{1,0:T(8,128)(2,1)S(1)} collective-permute-done((bf16[192,128]{1,0:T(8,128)(2,1)S(1)}, bf16[192,128]{1,0:T(8,128)(2,1)S(1)}, u32[]{:S(2)}, u32[]{:S(2)}) %collective-permute-start.15) | collective-permute-done | bytes 49184 | tf_op jit(solution)/shard_map/ppermute | solution.py:60
  55.7 0.9 %collective-permute-start.16 = (bf16[192,128]{1,0:T(8,128)(2,1)S(1)}, bf16[192,128]{1,0:T(8,128)(2,1)S(1)}, u32[]{:S(2)}, u32[]{:S(2)}) collective-permute-start(bf16[192,128]{1,0:T(8,128)(2,1)S(1)} %shard_map.102), channel_id=1, source_target_pairs={{8,0},{12,4},{0,8},{4,12},{9,1},{13,5},{1,9},{5,13},{10,2},{14,6},... | collective-permute-start | bytes 147464 | tf_op jit(solution)/shard_map/ppermute | solution.py:60
  56.6 6.1 %collective-permute-done.16.refs_5_ = bf16[192,128]{1,0:T(8,128)(2,1)S(1)} collective-permute-done((bf16[192,128]{1,0:T(8,128)(2,1)S(1)}, bf16[192,128]{1,0:T(8,128)(2,1)S(1)}, u32[]{:S(2)}, u32[]{:S(2)}) %collective-permute-start.16) | collective-permute-done | bytes 49184 | tf_op jit(solution)/shard_map/ppermute | solution.py:60
  62.8 0.6 shard_map.104
  63.4 1.1 %shard_map.106 = bf16[64,2048]{1,0:T(8,128)(2,1)} custom-call(f32[64,2048]{1,0:T(8,128)S(1)} %get-tuple-element.59.partial, bf16[48,64]{1,0:T(8,128)(2,1)S(1)} %get-tuple-element.60.refs_0_, bf16[48,64]{1,0:T(8,128)(2,1)S(1)} %get-tuple-element.61.refs_1_, bf16[48,64]{1,0:T(8,128)(2,1)S(1)} %get-tuple-element.62.refs_2_, ...), custom_call_target="tpu_custom_call" | custom-call | tf_op jit(solution)/shard_map/pallas_call | solution.py:22
  (50 shorter events, 1.5 us)
Async XLA Ops:
  1.4 15.2 %collective-permute-start.3 = (bf16[784,128]{1,0:T(8,128)(2,1)S(1)}, bf16[784,128]{1,0:T(8,128)(2,1)S(1)}, u32[]{:S(2)}, u32[]{:S(2)}) collective-permute-start(bf16[784,128]{1,0:T(8,128)(2,1)S(1)} %get-tuple-element.37), channel_id=1, source_target_pairs={{0,8},{4,12},{8,0},{12,4},{1,9},{5,13},{9,1},{13,5},{2,10},{6,14},... | collective-permute-start | bytes 602120 | tf_op jit(solution)/shard_map/ppermute | solution.py:60
  5.5 22.2 %slice-start = ((s8[6291456]{0:T(1024)(128)(4,1)}), s8[4194304]{0:T(1024)(128)(4,1)S(1)}, s32[]{:S(2)}) async-start(s8[6291456]{0:T(1024)(128)(4,1)} %bitcast.8), calls=%async_computation | async-start | bytes 8388608
  5.5 22.2 %slice-start.2 = ((s8[6291456]{0:T(1024)(128)(4,1)}), s8[4194304]{0:T(1024)(128)(4,1)S(1)}, s32[]{:S(2)}) async-start(s8[6291456]{0:T(1024)(128)(4,1)} %bitcast.11), calls=%async_computation.2 | async-start | bytes 8388608
  5.5 22.2 %slice-start.4 = ((s8[6291456]{0:T(1024)(128)(4,1)}), s8[4194304]{0:T(1024)(128)(4,1)S(1)}, s32[]{:S(2)}) async-start(s8[6291456]{0:T(1024)(128)(4,1)} %bitcast.14), calls=%async_computation.4 | async-start | bytes 8388608
  5.5 21.5 %copy-start = (bf16[1,2048,128]{2,1,0:T(8,128)(2,1)S(1)}, bf16[1,2048,128]{2,1,0:T(8,128)(2,1)}, u32[]{:S(2)}) copy-start(bf16[1,2048,128]{2,1,0:T(8,128)(2,1)} %param.16) | copy-start | bytes 1572868
  5.5 22.2 %slice-start.1 = ((s8[6291456]{0:T(1024)(128)(4,1)}), s8[2097152]{0:T(1024)(128)(4,1)S(1)}, s32[]{:S(2)}) async-start(s8[6291456]{0:T(1024)(128)(4,1)} %bitcast.8), calls=%async_computation.1 | async-start | bytes 4194304
  5.5 22.2 %slice-start.3 = ((s8[6291456]{0:T(1024)(128)(4,1)}), s8[2097152]{0:T(1024)(128)(4,1)S(1)}, s32[]{:S(2)}) async-start(s8[6291456]{0:T(1024)(128)(4,1)} %bitcast.11), calls=%async_computation.3 | async-start | bytes 4194304
  5.5 22.2 %slice-start.5 = ((s8[6291456]{0:T(1024)(128)(4,1)}), s8[2097152]{0:T(1024)(128)(4,1)S(1)}, s32[]{:S(2)}) async-start(s8[6291456]{0:T(1024)(128)(4,1)} %bitcast.14), calls=%async_computation.5 | async-start | bytes 4194304
  5.6 19.4 %collective-permute-start = (bf16[784,128]{1,0:T(8,128)(2,1)S(1)}, bf16[784,128]{1,0:T(8,128)(2,1)S(1)}, u32[]{:S(2)}, u32[]{:S(2)}) collective-permute-start(bf16[784,128]{1,0:T(8,128)(2,1)S(1)} %shard_map.92.refs_0_.refs_6_.refs_4_), channel_id=1, source_target_pairs={{0,2},{2,0},{1,3},{3,1},{4,6},{6,4},{5,7},{7,5},{8,10},{10,8},{9,1... | collective-permute-start | bytes 602120 | tf_op jit(solution)/shard_map/ppermute | solution.py:60
  7.1 11.4 %collective-permute-start.1 = (bf16[384,128]{1,0:T(8,128)(2,1)S(1)}, bf16[384,128]{1,0:T(8,128)(2,1)S(1)}, u32[]{:S(2)}, u32[]{:S(2)}) collective-permute-start(bf16[384,128]{1,0:T(8,128)(2,1)S(1)} %get-tuple-element.36), channel_id=1, source_target_pairs={{0,4},{4,0},{8,12},{12,8},{1,5},{5,1},{9,13},{13,9},{2,6},{6,2},{1... | collective-permute-start | bytes 294920 | tf_op jit(solution)/shard_map/ppermute | solution.py:60
  8.7 12.3 %collective-permute-start.7 = (bf16[400,128]{1,0:T(8,128)(2,1)S(1)}, bf16[400,128]{1,0:T(8,128)(2,1)S(1)}, u32[]{:S(2)}, u32[]{:S(2)}) collective-permute-start(bf16[400,128]{1,0:T(8,128)(2,1)S(1)} %get-tuple-element.39), channel_id=1, source_target_pairs={{0,4},{4,0},{8,12},{12,8},{1,5},{5,1},{9,13},{13,9},{2,6},{6,2},{1... | collective-permute-start | bytes 307208 | tf_op jit(solution)/shard_map/ppermute | solution.py:60
  9.1 12.5 %collective-permute-start.8 = (bf16[400,128]{1,0:T(8,128)(2,1)S(1)}, bf16[400,128]{1,0:T(8,128)(2,1)S(1)}, u32[]{:S(2)}, u32[]{:S(2)}) collective-permute-start(bf16[400,128]{1,0:T(8,128)(2,1)S(1)} %get-tuple-element.40), channel_id=1, source_target_pairs={{0,12},{4,8},{8,4},{12,0},{1,13},{5,9},{9,5},{13,1},{2,14},{6,10},... | collective-permute-start | bytes 307208 | tf_op jit(solution)/shard_map/ppermute | solution.py:60
  16.6 14.2 %collective-permute-start.4 = (bf16[784,128]{1,0:T(8,128)(2,1)S(1)}, bf16[784,128]{1,0:T(8,128)(2,1)S(1)}, u32[]{:S(2)}, u32[]{:S(2)}) collective-permute-start(bf16[784,128]{1,0:T(8,128)(2,1)S(1)} %collective-permute-done.3.refs_2_.refs_8_.refs_6_), channel_id=1, source_target_pairs={{0,2},{2,0},{1,3},{3,1},{4,6},{6,4},{5,7},{7,5},{8,10},{10,8},{9,1... | collective-permute-start | bytes 602120 | tf_op jit(solution)/shard_map/ppermute | solution.py:60
  18.6 6.4 %collective-permute-start.5 = (bf16[384,128]{1,0:T(8,128)(2,1)S(1)}, bf16[384,128]{1,0:T(8,128)(2,1)S(1)}, u32[]{:S(2)}, u32[]{:S(2)}) collective-permute-start(bf16[384,128]{1,0:T(8,128)(2,1)S(1)} %get-tuple-element.38), channel_id=1, source_target_pairs={{0,12},{4,8},{8,4},{12,0},{1,13},{5,9},{9,5},{13,1},{2,14},{6,10},... | collective-permute-start | bytes 294920 | tf_op jit(solution)/shard_map/ppermute | solution.py:60
  21.0 6.6 %collective-permute-start.10 = (bf16[400,128]{1,0:T(8,128)(2,1)S(1)}, bf16[400,128]{1,0:T(8,128)(2,1)S(1)}, u32[]{:S(2)}, u32[]{:S(2)}) collective-permute-start(bf16[400,128]{1,0:T(8,128)(2,1)S(1)} %collective-permute-done.7.refs_1_.refs_7_.refs_5_), channel_id=1, source_target_pairs={{0,2},{2,0},{1,3},{3,1},{4,6},{6,4},{5,7},{7,5},{8,10},{10,8},{9,1... | collective-permute-start | bytes 307208 | tf_op jit(solution)/shard_map/ppermute | solution.py:60
  21.6 9.1 %collective-permute-start.11 = (bf16[400,128]{1,0:T(8,128)(2,1)S(1)}, bf16[400,128]{1,0:T(8,128)(2,1)S(1)}, u32[]{:S(2)}, u32[]{:S(2)}) collective-permute-start(bf16[400,128]{1,0:T(8,128)(2,1)S(1)} %collective-permute-done.8.refs_3_.refs_9_.refs_7_), channel_id=1, source_target_pairs={{0,2},{2,0},{1,3},{3,1},{4,6},{6,4},{5,7},{7,5},{8,10},{10,8},{9,1... | collective-permute-start | bytes 307208 | tf_op jit(solution)/shard_map/ppermute | solution.py:60
  25.0 6.6 %collective-permute-start.2 = (bf16[384,128]{1,0:T(8,128)(2,1)S(1)}, bf16[384,128]{1,0:T(8,128)(2,1)S(1)}, u32[]{:S(2)}, u32[]{:S(2)}) collective-permute-start(bf16[384,128]{1,0:T(8,128)(2,1)S(1)} %collective-permute-done.1.refs_1_), channel_id=1, source_target_pairs={{0,2},{2,0},{1,3},{3,1},{4,6},{6,4},{5,7},{7,5},{8,10},{10,8},{9,1... | collective-permute-start | bytes 294920 | tf_op jit(solution)/shard_map/ppermute | solution.py:60
  25.0 6.6 %collective-permute-start.6 = (bf16[384,128]{1,0:T(8,128)(2,1)S(1)}, bf16[384,128]{1,0:T(8,128)(2,1)S(1)}, u32[]{:S(2)}, u32[]{:S(2)}) collective-permute-start(bf16[384,128]{1,0:T(8,128)(2,1)S(1)} %collective-permute-done.5.refs_3_), channel_id=1, source_target_pairs={{0,2},{2,0},{1,3},{3,1},{4,6},{6,4},{5,7},{7,5},{8,10},{10,8},{9,1... | collective-permute-start | bytes 294920 | tf_op jit(solution)/shard_map/ppermute | solution.py:60
  27.6 4.0 %collective-permute-start.9 = (f32[8,192]{1,0:T(8,128)S(1)}, f32[8,192]{1,0:T(8,128)S(1)}, u32[]{:S(2)}, u32[]{:S(2)}) collective-permute-start(f32[8,192]{1,0:T(8,128)S(1)} %shard_map.94.refs_8_), channel_id=1, source_target_pairs={{0,2},{2,0},{1,3},{3,1},{4,6},{6,4},{5,7},{7,5},{8,10},{10,8},{9,1... | collective-permute-start | bytes 18440 | tf_op jit(solution)/shard_map/ppermute | solution.py:60
  30.8 0.9 %copy-start.1 = (bf16[1,128,768]{2,1,0:T(8,128)(2,1)S(1)}, bf16[1,128,768]{2,1,0:T(8,128)(2,1)}, u32[]{:S(2)}) copy-start(bf16[1,128,768]{2,1,0:T(8,128)(2,1)} %param.17) | copy-start | bytes 589828
  33.0 29.8 %copy-start.2 = (s32[64,2]{0,1:T(2,128)S(1)}, s32[64,2]{0,1:T(2,128)}, u32[]{:S(2)}) copy-start(s32[64,2]{0,1:T(2,128)} %param.10) | copy-start | bytes 1540
  33.0 29.8 %copy-start.3 = (f32[64,2]{0,1:T(2,128)S(1)}, f32[64,2]{0,1:T(2,128)}, u32[]{:S(2)}) copy-start(f32[64,2]{0,1:T(2,128)} %param.11) | copy-start | bytes 1540
  33.8 7.8 %collective-permute-start.13 = (bf16[768,128]{1,0:T(8,128)(2,1)S(1)}, bf16[768,128]{1,0:T(8,128)(2,1)S(1)}, u32[]{:S(2)}, u32[]{:S(2)}) collective-permute-start(bf16[768,128]{1,0:T(8,128)(2,1)S(1)} %get-tuple-element.54), channel_id=1, source_target_pairs={{0,2},{2,0},{1,3},{3,1},{4,6},{6,4},{5,7},{7,5},{8,10},{10,8},{9,1... | collective-permute-start | bytes 589832 | tf_op jit(solution)/shard_map/ppermute | solution.py:60
  35.9 10.0 %collective-permute-start.19 = (bf16[768,128]{1,0:T(8,128)(2,1)S(1)}, bf16[768,128]{1,0:T(8,128)(2,1)S(1)}, u32[]{:S(2)}, u32[]{:S(2)}) collective-permute-start(bf16[768,128]{1,0:T(8,128)(2,1)S(1)} %get-tuple-element.64), channel_id=1, source_target_pairs={{0,2},{2,0},{1,3},{3,1},{4,6},{6,4},{5,7},{7,5},{8,10},{10,8},{9,1... | collective-permute-start | bytes 589832 | tf_op jit(solution)/shard_map/ppermute | solution.py:60
  36.0 13.4 %collective-permute-start.17 = (bf16[576,128]{1,0:T(8,128)(2,1)S(1)}, bf16[576,128]{1,0:T(8,128)(2,1)S(1)}, u32[]{:S(2)}, u32[]{:S(2)}) collective-permute-start(bf16[576,128]{1,0:T(8,128)(2,1)S(1)} %get-tuple-element.58), channel_id=1, source_target_pairs={{0,2},{2,0},{1,3},{3,1},{4,6},{6,4},{5,7},{7,5},{8,10},{10,8},{9,1... | collective-permute-start | bytes 442376 | tf_op jit(solution)/shard_map/ppermute | solution.py:60
  38.7 24.0 %collective-permute-start.12 = (bf16[768,128]{1,0:T(8,128)(2,1)S(1)}, bf16[768,128]{1,0:T(8,128)(2,1)S(1)}, u32[]{:S(2)}, u32[]{:S(2)}) collective-permute-start(bf16[768,128]{1,0:T(8,128)(2,1)S(1)} %get-tuple-element.52), channel_id=1, source_target_pairs={{0,2},{2,0},{1,3},{3,1},{4,6},{6,4},{5,7},{7,5},{8,10},{10,8},{9,1... | collective-permute-start | bytes 589832 | tf_op jit(solution)/shard_map/ppermute | solution.py:60
  41.7 21.0 %collective-permute-start.14 = (bf16[768,128]{1,0:T(8,128)(2,1)S(1)}, bf16[768,128]{1,0:T(8,128)(2,1)S(1)}, u32[]{:S(2)}, u32[]{:S(2)}) collective-permute-start(bf16[768,128]{1,0:T(8,128)(2,1)S(1)} %shard_map.101), channel_id=1, source_target_pairs={{4,0},{0,4},{12,8},{8,12},{5,1},{1,5},{13,9},{9,13},{6,2},{2,6},{1... | collective-permute-start | bytes 589832 | tf_op jit(solution)/shard_map/ppermute | solution.py:60
  45.9 17.4 %collective-permute-start.20 = (bf16[768,128]{1,0:T(8,128)(2,1)S(1)}, bf16[768,128]{1,0:T(8,128)(2,1)S(1)}, u32[]{:S(2)}, u32[]{:S(2)}) collective-permute-start(bf16[768,128]{1,0:T(8,128)(2,1)S(1)} %shard_map.105), channel_id=1, source_target_pairs={{12,0},{8,4},{4,8},{0,12},{13,1},{9,5},{5,9},{1,13},{14,2},{10,6},... | collective-permute-start | bytes 589832 | tf_op jit(solution)/shard_map/ppermute | solution.py:60
  49.4 13.3 %collective-permute-start.18 = (bf16[576,128]{1,0:T(8,128)(2,1)S(1)}, bf16[576,128]{1,0:T(8,128)(2,1)S(1)}, u32[]{:S(2)}, u32[]{:S(2)}) collective-permute-start(bf16[576,128]{1,0:T(8,128)(2,1)S(1)} %shard_map.103), channel_id=1, source_target_pairs={{8,0},{12,4},{0,8},{4,12},{9,1},{13,5},{1,9},{5,13},{10,2},{14,6},... | collective-permute-start | bytes 442376 | tf_op jit(solution)/shard_map/ppermute | solution.py:60
  51.6 4.1 %collective-permute-start.15 = (bf16[192,128]{1,0:T(8,128)(2,1)S(1)}, bf16[192,128]{1,0:T(8,128)(2,1)S(1)}, u32[]{:S(2)}, u32[]{:S(2)}) collective-permute-start(bf16[192,128]{1,0:T(8,128)(2,1)S(1)} %get-tuple-element.56), channel_id=1, source_target_pairs={{0,2},{2,0},{1,3},{3,1},{4,6},{6,4},{5,7},{7,5},{8,10},{10,8},{9,1... | collective-permute-start | bytes 147464 | tf_op jit(solution)/shard_map/ppermute | solution.py:60
  55.7 7.0 %collective-permute-start.16 = (bf16[192,128]{1,0:T(8,128)(2,1)S(1)}, bf16[192,128]{1,0:T(8,128)(2,1)S(1)}, u32[]{:S(2)}, u32[]{:S(2)}) collective-permute-start(bf16[192,128]{1,0:T(8,128)(2,1)S(1)} %shard_map.102), channel_id=1, source_target_pairs={{8,0},{12,4},{0,8},{4,12},{9,1},{13,5},{1,9},{5,13},{10,2},{14,6},... | collective-permute-start | bytes 147464 | tf_op jit(solution)/shard_map/ppermute | solution.py:60

commit v4 on v3

--- a/solution.py
+++ b/solution.py
@@ -159,7 +159,7 @@
     home, first = [], experts // 2
     for k in range(experts):
         if k and k == first:
-            home += [Piece(k, 0, quarter, cap, False), Piece(k, quarter, part, cap, False)]
+            home += [Piece(k, 0, half, cap, False), Piece(k, half, part, cap, False)]
         else:
             home += [Piece(k, 0, part, cap, False)]
     home_segments = [(0, quarter), (quarter, half), (half, part)]
@@ -347,12 +347,10 @@
             base = target(lax.axis_index("hidden"), d, hiddens) * part
             rows = act[p.step * cap : (p.step + 1) * cap]
             store_down(rows, down_ref, base, p.lo, p.hi, [p], [rest[6 + d]], p.step * cap)
-        base = lax.axis_index("hidden") * part
-        store_down(rows, down_ref, base, p.lo, p.hi, [p], [rest[-1]], p.step * cap)
-
-    act, *lead_sent, lead_kept = call(
+
+    act, *lead_sent = call(
         activate,
-        [jax.ShapeDtypeStruct((total, units), BF16)] + [home[lead].shape] * hiddens,
+        [jax.ShapeDtypeStruct((total, units), BF16)] + [home[lead].shape] * (hiddens - 1),
         (
             *values,
             *within(*segments[0], arrived)[1],
@@ -366,8 +364,13 @@
         ),
     )
 
-    def down(step, pieces):
+    def down(step, pieces, lead_too=False):
         def body(act_ref, down_ref, *outs):
+            if lead_too:
+                p = home[lead]
+                rows = act_ref[p.step * cap : (p.step + 1) * cap, :]
+                base = lax.axis_index("hidden") * part
+                store_down(rows, down_ref, base, p.lo, p.hi, [p], outs[-1:], p.step * cap)
             base = target(lax.axis_index("hidden"), step, hiddens) * part if step else (
                 lax.axis_index("hidden") * part
             )
@@ -375,12 +378,15 @@
                 if any(p.covers(lo, hi) for p in pieces):
                     store_down(act_ref[...], down_ref, base, lo, hi, pieces, outs, 0)
 
-        return call(body, [p.shape for p in pieces], (act, down_w))
+        shapes = [p.shape for p in pieces] + [home[lead].shape] * lead_too
+        return call(body, shapes, (act, down_w))
 
     rest = [i for i in range(len(home)) if i != lead]
     sent_home = []
     for d in range(1, hiddens):
-        out = down(d, [home[i] for i in rest])
+        out = down(d, [home[i] for i in rest], d == 1)
+        if d == 1:
+            *out, lead_kept = out
         sent_home.append({lead: lead_sent[d - 1], **dict(zip(rest, out))})
     kept = {lead: lead_kept, **dict(zip(rest, down(0, [home[i] for i in rest])))}
     order = [lead] + ([lead + 1] if lead else [])
@@ -388,6 +394,7 @@
     summed = {
         i: [permute(sent_home[d - 1][i], "hidden", d) for d in range(1, hiddens)]
         for i in order
+        if home[i].step > 1
     }
 
     def add(*refs):
@@ -398,12 +405,12 @@
 
     returned = {}
     for i in order:
-        if home[i].step:
+        if home[i].step > 1:
             (y,) = call(add, [home[i].shape], (kept[i], *summed[i]))
             returned[i] = permute(y, "expert", home[i].step, back=True)
 
     final = max([i for i in range(len(home)) if home[i].step not in (0, first)], default=0)
-    early = [i for i in range(len(home)) if home[i].step and i != final]
+    early = [i for i in range(len(home)) if home[i].step > 1 and i != final]
 
     def mixing(ids, weight, chosen_steps):
         me = lax.axis_index("expert")
@@ -425,27 +432,43 @@
         return terms
 
     def mixed_sum(terms, rows):
-        value = dot(terms[0], rows, ((0,), (0,)))
-        for t in terms[1:]:
-            value = value + dot(t, rows, ((0,), (0,)))
-        return value
-
-    early_steps = [0] + [k for k in steps if any(home[i].step == k for i in early)]
+        value = dot(jnp.concatenate(terms, axis=1), rows, ((0,), (0,)))
+        return value[:tok_rows] + value[tok_rows : 2 * tok_rows] + value[2 * tok_rows :]
+
+    early_steps = [k for k in steps if any(home[i].step == k for i in early)]
+    tokens_tile = Piece(None, 0, part, tok_rows, False)
+
+    near = [0, 1]
+    near_parts = [[kept[i] for i in near]]
+    near_parts += [[sent_home[d - 1][i] for i in near] for d in range(1, hiddens)]
+    near_parts = [[own, permute(row, "expert", 1, back=True)] for own, row in near_parts]
+
+    def near_mix(ids, weight, *refs):
+        terms = mixing(ids[...], weight[...], near)
+        for d in range(hiddens):
+            own, row = refs[2 * d : 2 * d + 2]
+            for lo, hi in segments:
+                rows = jnp.concatenate(
+                    [home[0].load(own, lo, hi), home[1].load(row, lo, hi)], axis=0
+                )
+                value = mixed_sum(terms, rows)
+                if d:
+                    tokens_tile.store(refs[2 * hiddens + d], lo, value.astype(BF16))
+                else:
+                    refs[2 * hiddens][:, lo:hi] = value
+
+    near_kept, *near_away = call(
+        near_mix,
+        [jax.ShapeDtypeStruct((tok_rows, part), F32)] + [tokens_tile.shape] * (hiddens - 1),
+        (route_ids.T, route_weight.T, *[v for pair in near_parts for v in pair]),
+    )
+    near_others = [permute(near_away[d - 1], "hidden", d) for d in range(1, hiddens)]
 
     def combine(*refs):
-        own, others_in = refs[2 : 2 + hiddens], refs[2 + hiddens : -4]
         terms = mixing(refs[0][...], refs[1][...], early_steps)
         for lo, hi in home_segments:
-            y = home[0].load(own[0], lo, hi).astype(F32)
-            for r in own[1:]:
-                y = y + home[0].load(r, lo, hi).astype(F32)
-            rows = [y.astype(BF16)]
-            rows += [
-                home[i].load(r, lo, hi) for i, r in zip(early, others_in) if home[i].covers(lo, hi)
-            ]
-            n = len(rows) * cap
-            rows = jnp.concatenate(rows, axis=0)
-            refs[-4][:, lo:hi] = mixed_sum([t[:n] for t in terms], rows)
+            rows = [home[i].load(r, lo, hi) for i, r in zip(early, refs[2:]) if home[i].covers(lo, hi)]
+            refs[-4][:, lo:hi] = mixed_sum(terms, jnp.concatenate(rows, axis=0))
         for ref, t in zip(refs[-3:], mixing(refs[0][...], refs[1][...], [home[final].step])):
             ref[...] = t
 
@@ -453,16 +476,19 @@
         combine,
         [jax.ShapeDtypeStruct((tok_rows, part), F32)]
         + [jax.ShapeDtypeStruct((cap, tok_rows), BF16)] * 3,
-        (route_ids.T, route_weight.T, kept[0], *summed[0], *[returned[i] for i in early]),
-    )
-
-    def finish(partial, *refs):
-        terms, out, staged, sems = [r[...] for r in refs[:3]], refs[-3], refs[-2], refs[-1]
+        (route_ids.T, route_weight.T, *[returned[i] for i in early]),
+    )
+
+    def finish(partial, kept_sum, *refs):
+        terms, refs = [r[...] for r in refs[:3]], refs[3:]
+        row, others_in = refs[0], refs[1:hiddens]
+        out, staged, sems = refs[-3:]
         copies = []
         for i, (lo, hi) in enumerate(home_segments):
-            value = partial[:, lo:hi]
-            if final and home[final].covers(lo, hi):
-                value = value + mixed_sum(terms, home[final].load(refs[3], lo, hi))
+            value = partial[:, lo:hi] + kept_sum[:, lo:hi]
+            for r in others_in:
+                value = value + tokens_tile.load(r, lo, hi).astype(F32)
+            value = value + mixed_sum(terms, home[final].load(row, lo, hi))
             staged[:, lo:hi] = value.astype(BF16)
             copies.append(
                 pltpu.make_async_copy(staged.at[:, lo:hi], out.at[:, lo:hi], sems.at[i])
@@ -474,7 +500,7 @@
     (result,) = call(
         finish,
         [jax.ShapeDtypeStruct((tok_rows, part), BF16)],
-        (mixed, *final_terms, *([returned[final]] if final else [])),
+        (mixed, near_kept, *final_terms, returned[final], *near_others),
         out_specs=[ANY],
         scratch=[
             pltpu.VMEM((tok_rows, part), BF16),

time: 64.6 us -> 68.8 us (1.065)
  starting transfers between devices: 29.4 us -> 33.8 us
  waiting for transfers between devices: 24.2 us -> 22.9 us
  Pallas kernels: 10.4 us -> 11.6 us
    ppermute x21, starting transfers between devices: 29.4 us -> 33.8 us  [permute(): return lax.ppermute(value, axis, pairs)]
    ppermute x21, waiting for transfers between devices: 24.2 us -> 22.9 us  [permute(): return lax.ppermute(value, axis, pairs)]
    pallas_call x16, Pallas kernels: 9.15 us -> 10.3 us  [call(): pl.pallas_call(body, out_shape=outs, in_specs=in_specs or [VMEM] * len(in...]
  transfers between devices with their start and end apart: 21 -> 21, of which waited for: 6 -> 7; matrix products, arithmetic and copies ran while one was open for 0% -> 0% of each run, Pallas kernels for 9% -> 9%
where the time goes in v4:
time: 68.8 us; the launch traced here: 68.6 us
  starting transfers between devices  33.8 us (49%)
  waiting for transfers between devices  22.9 us (33%)
  Pallas kernels  11.6 us (17%)
    ppermute x21, starting transfers between devices, permute(): return lax.ppermute(value, axis, pairs)  33.8 us
    ppermute x21, waiting for transfers between devices, permute(): return lax.ppermute(value, axis, pairs)  22.9 us
    pallas_call x16, Pallas kernels, call(): pl.pallas_call(body, out_shape=outs, in_specs=in_specs or [VMEM] * len(in...  10.3 us
  transfers between devices with their start and end apart: 21, of which 7 were waited for; matrix products, arithmetic and copies ran while one was open for 0% of the time, Pallas kernels for 9%

profile of v4, /device:TPU:0, one launch (start us, length us, event | category | flops | bytes accessed | tf_op | source)
XLA Modules:
  0.0 68.6 jit_solution(2733226375131423501)
XLA Ops:
  0.0 1.4 %shard_map.91 = (bf16[784,128]{1,0:T(8,128)(2,1)S(1)}, bf16[400,128]{1,0:T(8,128)(2,1)S(1)}, bf16[384,128]{1,0:T(8,128)(2,1)S(1)}, bf16[784,128]{1,0:T(8,128)(2,...) custom-call(s32[2,64]{1,0:T(2,128)} %bitcast.20, s32[4,8]{1,0:T(4,128)} %bitcast.25, ...), custom_call_target="tpu_custom_call" | custom-call | tf_op jit(solution)/shard_map/pallas_call | solution.py:22
  1.4 4.1 %collective-permute-start.3 = (bf16[784,128]{1,0:T(8,128)(2,1)S(1)}, bf16[784,128]{1,0:T(8,128)(2,1)S(1)}, u32[]{:S(2)}, u32[]{:S(2)}) collective-permute-start(bf16[784,128]{1,0:T(8,128)(2,1)S(1)} %get-tuple-element.39), channel_id=1, source_target_pairs={{0,8},{4,12},{8,0},{12,4},{1,9},{5,13},{9,1},{13,5},{2,10},{6,14},... | collective-permute-start | bytes 602120 | tf_op jit(solution)/shard_map/ppermute | solution.py:60
  5.6 1.6 %collective-permute-start = (bf16[784,128]{1,0:T(8,128)(2,1)S(1)}, bf16[784,128]{1,0:T(8,128)(2,1)S(1)}, u32[]{:S(2)}, u32[]{:S(2)}) collective-permute-start(bf16[784,128]{1,0:T(8,128)(2,1)S(1)} %shard_map.92.refs_0_.refs_6_.refs_4_), channel_id=1, source_target_pairs={{0,2},{2,0},{1,3},{3,1},{4,6},{6,4},{5,7},{7,5},{8,10},{10,8},{9,1... | collective-permute-start | bytes 602120 | tf_op jit(solution)/shard_map/ppermute | solution.py:60
  7.1 1.6 %collective-permute-start.1 = (bf16[384,128]{1,0:T(8,128)(2,1)S(1)}, bf16[384,128]{1,0:T(8,128)(2,1)S(1)}, u32[]{:S(2)}, u32[]{:S(2)}) collective-permute-start(bf16[384,128]{1,0:T(8,128)(2,1)S(1)} %get-tuple-element.38), channel_id=1, source_target_pairs={{0,4},{4,0},{8,12},{12,8},{1,5},{5,1},{9,13},{13,9},{2,6},{6,2},{1... | collective-permute-start | bytes 294920 | tf_op jit(solution)/shard_map/ppermute | solution.py:60
  9.1 1.3 %collective-permute-start.8 = (bf16[400,128]{1,0:T(8,128)(2,1)S(1)}, bf16[400,128]{1,0:T(8,128)(2,1)S(1)}, u32[]{:S(2)}, u32[]{:S(2)}) collective-permute-start(bf16[400,128]{1,0:T(8,128)(2,1)S(1)} %get-tuple-element.42), channel_id=1, source_target_pairs={{0,12},{4,8},{8,4},{12,0},{1,13},{5,9},{9,5},{13,1},{2,14},{6,10},... | collective-permute-start | bytes 307208 | tf_op jit(solution)/shard_map/ppermute | solution.py:60
  10.5 6.1 %collective-permute-done.3.refs_2_.refs_8_.refs_6_ = bf16[784,128]{1,0:T(8,128)(2,1)S(1)} collective-permute-done((bf16[784,128]{1,0:T(8,128)(2,1)S(1)}, bf16[784,128]{1,0:T(8,128)(2,1)S(1)}, u32[]{:S(2)}, u32[]{:S(2)}) %collective-permute-start.3) | collective-permute-done | bytes 200736 | tf_op jit(solution)/shard_map/ppermute | solution.py:60
  16.6 2.0 %collective-permute-start.4 = (bf16[784,128]{1,0:T(8,128)(2,1)S(1)}, bf16[784,128]{1,0:T(8,128)(2,1)S(1)}, u32[]{:S(2)}, u32[]{:S(2)}) collective-permute-start(bf16[784,128]{1,0:T(8,128)(2,1)S(1)} %collective-permute-done.3.refs_2_.refs_8_.refs_6_), channel_id=1, source_target_pairs={{0,2},{2,0},{1,3},{3,1},{4,6},{6,4},{5,7},{7,5},{8,10},{10,8},{9,1... | collective-permute-start | bytes 602120 | tf_op jit(solution)/shard_map/ppermute | solution.py:60
  18.6 2.5 %collective-permute-start.5 = (bf16[384,128]{1,0:T(8,128)(2,1)S(1)}, bf16[384,128]{1,0:T(8,128)(2,1)S(1)}, u32[]{:S(2)}, u32[]{:S(2)}) collective-permute-start(bf16[384,128]{1,0:T(8,128)(2,1)S(1)} %get-tuple-element.40), channel_id=1, source_target_pairs={{0,12},{4,8},{8,4},{12,0},{1,13},{5,9},{9,5},{13,1},{2,14},{6,10},... | collective-permute-start | bytes 294920 | tf_op jit(solution)/shard_map/ppermute | solution.py:60
  21.6 1.5 %collective-permute-start.11 = (bf16[400,128]{1,0:T(8,128)(2,1)S(1)}, bf16[400,128]{1,0:T(8,128)(2,1)S(1)}, u32[]{:S(2)}, u32[]{:S(2)}) collective-permute-start(bf16[400,128]{1,0:T(8,128)(2,1)S(1)} %collective-permute-done.8.refs_3_.refs_9_.refs_7_), channel_id=1, source_target_pairs={{0,2},{2,0},{1,3},{3,1},{4,6},{6,4},{5,7},{7,5},{8,10},{10,8},{9,1... | collective-permute-start | bytes 307208 | tf_op jit(solution)/shard_map/ppermute | solution.py:60
  23.1 1.9 %collective-permute-done.5.refs_3_ = bf16[384,128]{1,0:T(8,128)(2,1)S(1)} collective-permute-done((bf16[384,128]{1,0:T(8,128)(2,1)S(1)}, bf16[384,128]{1,0:T(8,128)(2,1)S(1)}, u32[]{:S(2)}, u32[]{:S(2)}) %collective-permute-start.5) | collective-permute-done | bytes 98336 | tf_op jit(solution)/shard_map/ppermute | solution.py:60
  25.0 2.0 %collective-permute-start.6 = (bf16[384,128]{1,0:T(8,128)(2,1)S(1)}, bf16[384,128]{1,0:T(8,128)(2,1)S(1)}, u32[]{:S(2)}, u32[]{:S(2)}) collective-permute-start(bf16[384,128]{1,0:T(8,128)(2,1)S(1)} %collective-permute-done.5.refs_3_), channel_id=1, source_target_pairs={{0,2},{2,0},{1,3},{3,1},{4,6},{6,4},{5,7},{7,5},{8,10},{10,8},{9,1... | collective-permute-start | bytes 294920 | tf_op jit(solution)/shard_map/ppermute | solution.py:60
  27.8 1.3 %load.1 = (bf16[4096,768]{1,0:T(8,128)(2,1)S(1)}, bf16[4096,768]{1,0:T(8,128)(2,1)S(1)}, bf16[768,4096]{1,0:T(8,128)(2,1)S(1)}) custom-call(bf16[4096,768]{1,0:T(8,128)(2,1)S(1)} %bitcast.10, bf16[4096,768]{1,0:T(8,128)(2,1)S(1)} %bitcast.13, bf16[768,4096]{1,0:T(8,128)(2,1)S(1)} %bitcast.16), custom_call_target="tpu_custom_call" | custom-call | tf_op jit(solution)/shard_map/load/pallas_call | solution.py:227
  29.1 0.8 %shard_map.95 = (f32[192,768]{1,0:T(8,128)S(1)}, f32[192,768]{1,0:T(8,128)S(1)}) custom-call(bf16[784,128]{1,0:T(8,128)(2,1)S(1)} %shard_map.92.refs_0_.refs_6_.refs_4_, bf16[400,128]{1,0:T(8,128)(2,1)S(1)} %collective-permute-done.7.refs_1_.refs_7_.refs_5_, bf16[784,128]{1,0:T(8,128)(2,1)S(1)} %collective-permute-done.3.refs_2_.refs_8_.refs_6_, ...), custom_call_target="tpu_custom_call" | custom-call | tf_op jit(solution)/shard_map/pallas_call | solution.py:22
  29.9 0.8 %shard_map.96 = (f32[192,768]{1,0:T(8,128)S(1)}, f32[192,768]{1,0:T(8,128)S(1)}) custom-call(bf16[784,128]{1,0:T(8,128)(2,1)S(1)} %shard_map.92.refs_0_.refs_6_.refs_4_, bf16[384,128]{1,0:T(8,128)(2,1)S(1)} %collective-permute-done.1.refs_1_, bf16[784,128]{1,0:T(8,128)(2,1)S(1)} %collective-permute-done.3.refs_2_.refs_8_.refs_6_, ...), custom_call_target="tpu_custom_call" | custom-call | tf_op jit(solution)/shard_map/pallas_call | solution.py:22
  30.8 0.8 %shard_map.97 = (f32[192,768]{1,0:T(8,128)S(1)}, f32[192,768]{1,0:T(8,128)S(1)}) custom-call(bf16[784,128]{1,0:T(8,128)(2,1)S(1)} %collective-permute-done.refs_0_, bf16[400,128]{1,0:T(8,128)(2,1)S(1)} %collective-permute-done.10.refs_1_, bf16[784,128]{1,0:T(8,128)(2,1)S(1)} %collective-permute-done.4.refs_2_, ...), custom_call_target="tpu_custom_call" | custom-call | tf_op jit(solution)/shard_map/pallas_call | solution.py:22
  31.7 1.3 %shard_map.98 = (bf16[192,768]{1,0:T(8,128)(2,1)S(1)}, bf16[384,128]{1,0:T(8,128)(2,1)S(1)}) custom-call(bf16[784,128]{1,0:T(8,128)(2,1)S(1)} %collective-permute-done.refs_0_, bf16[384,128]{1,0:T(8,128)(2,1)S(1)} %collective-permute-done.2.refs_1_, bf16[784,128]{1,0:T(8,128)(2,1)S(1)} %collective-permute-done.4.refs_2_, ...), custom_call_target="tpu_custom_call" | custom-call | tf_op jit(solution)/shard_map/pallas_call | solution.py:22
  33.0 0.8 %shard_map.101 = (bf16[768,128]{1,0:T(8,128)(2,1)S(1)}, bf16[768,128]{1,0:T(8,128)(2,1)S(1)}, bf16[384,128]{1,0:T(8,128)(2,1)S(1)}, bf16[768,128]{1,0:T(8,128)(2,1)S(1)}) custom-call(bf16[192,768]{1,0:T(8,128)(2,1)S(1)} %get-tuple-element.52.act_ref, bf16[768,4096]{1,0:T(8,128)(2,1)S(1)} %get-tuple-element.51.refs_15_.down_ref), custom_call_target="tpu_custom_call" | custom-call | tf_op jit(solution)/shard_map/pallas_call | solution.py:22
  33.8 1.1 %shard_map.99 = (bf16[768,128]{1,0:T(8,128)(2,1)S(1)}, bf16[768,128]{1,0:T(8,128)(2,1)S(1)}, bf16[384,128]{1,0:T(8,128)(2,1)S(1)}, bf16[768,128]{1,0:T(8,128)(2,1)S(1)}, bf16[384,128]{1,0:T(8,128)(2,1)S(1)}) custom-call(bf16[192,768]{1,0:T(8,128)(2,1)S(1)} %get-tuple-element.52.act_ref, bf16[768,4096]{1,0:T(8,128)(2,1)S(1)} %get-tuple-element.51.refs_15_.down_ref), custom_call_target="tpu_custom_call" | custom-call | tf_op jit(solution)/shard_map/pallas_call | solution.py:22
  35.6 1.4 %collective-permute-start.17 = (bf16[768,128]{1,0:T(8,128)(2,1)S(1)}, bf16[768,128]{1,0:T(8,128)(2,1)S(1)}, u32[]{:S(2)}, u32[]{:S(2)}) collective-permute-start(bf16[768,128]{1,0:T(8,128)(2,1)S(1)} %get-tuple-element.61), channel_id=1, source_target_pairs={{4,0},{0,4},{12,8},{8,12},{5,1},{1,5},{13,9},{9,13},{6,2},{2,6},{1... | collective-permute-start | bytes 589832 | tf_op jit(solution)/shard_map/ppermute | solution.py:60
  37.0 2.0 %collective-permute-start.18 = (bf16[768,128]{1,0:T(8,128)(2,1)S(1)}, bf16[768,128]{1,0:T(8,128)(2,1)S(1)}, u32[]{:S(2)}, u32[]{:S(2)}) collective-permute-start(bf16[768,128]{1,0:T(8,128)(2,1)S(1)} %get-tuple-element.67), channel_id=1, source_target_pairs={{0,2},{2,0},{1,3},{3,1},{4,6},{6,4},{5,7},{7,5},{8,10},{10,8},{9,1... | collective-permute-start | bytes 589832 | tf_op jit(solution)/shard_map/ppermute | solution.py:60
  39.0 3.2 %collective-permute-done.16.refs_1_ = bf16[768,128]{1,0:T(8,128)(2,1)S(1)} collective-permute-done((bf16[768,128]{1,0:T(8,128)(2,1)S(1)}, bf16[768,128]{1,0:T(8,128)(2,1)S(1)}, u32[]{:S(2)}, u32[]{:S(2)}) %collective-permute-start.16) | collective-permute-done | bytes 196640 | tf_op jit(solution)/shard_map/ppermute | solution.py:60
  42.2 2.1 %collective-permute-done.17.refs_3_ = bf16[768,128]{1,0:T(8,128)(2,1)S(1)} collective-permute-done((bf16[768,128]{1,0:T(8,128)(2,1)S(1)}, bf16[768,128]{1,0:T(8,128)(2,1)S(1)}, u32[]{:S(2)}, u32[]{:S(2)}) %collective-permute-start.17) | collective-permute-done | bytes 196640 | tf_op jit(solution)/shard_map/ppermute | solution.py:60
  44.3 0.8 %shard_map.104 = (f32[64,2048]{1,0:T(8,128)S(1)}, bf16[1024,128]{1,0:T(8,128)(2,1)S(1)}) custom-call(s32[2,64]{1,0:T(2,128)S(1)} %bitcast.21, f32[2,64]{1,0:T(2,128)S(1)} %bitcast.23, bf16[768,128]{1,0:T(8,128)(2,1)S(1)} %get-tuple-element.58.refs_0_, bf16[768,128]{1,0:T(8,128)(2,1)S(1)} %collective-permute-done.16.refs_1_, ...), custom_call_target="tpu_custom_call" | custom-call | tf_op jit(solution)/shard_map/pallas_call | solution.py:22
  45.2 2.3 %collective-permute-start.20 = (bf16[1024,128]{1,0:T(8,128)(2,1)S(1)}, bf16[1024,128]{1,0:T(8,128)(2,1)S(1)}, u32[]{:S(2)}, u32[]{:S(2)}) collective-permute-start(bf16[1024,128]{1,0:T(8,128)(2,1)S(1)} %get-tuple-element.68), channel_id=1, source_target_pairs={{0,2},{2,0},{1,3},{3,1},{4,6},{6,4},{5,7},{7,5},{8,10},{10,8},{9,1... | collective-permute-start | bytes 786440 | tf_op jit(solution)/shard_map/ppermute | solution.py:60
  47.6 1.9 %collective-permute-start.12 = (bf16[384,128]{1,0:T(8,128)(2,1)S(1)}, bf16[384,128]{1,0:T(8,128)(2,1)S(1)}, u32[]{:S(2)}, u32[]{:S(2)}) collective-permute-start(bf16[384,128]{1,0:T(8,128)(2,1)S(1)} %get-tuple-element.54), channel_id=1, source_target_pairs={{0,2},{2,0},{1,3},{3,1},{4,6},{6,4},{5,7},{7,5},{8,10},{10,8},{9,1... | collective-permute-start | bytes 294920 | tf_op jit(solution)/shard_map/ppermute | solution.py:60
  49.6 3.2 %collective-permute-start.19 = (bf16[768,128]{1,0:T(8,128)(2,1)S(1)}, bf16[768,128]{1,0:T(8,128)(2,1)S(1)}, u32[]{:S(2)}, u32[]{:S(2)}) collective-permute-start(bf16[768,128]{1,0:T(8,128)(2,1)S(1)} %shard_map.105), channel_id=1, source_target_pairs={{12,0},{8,4},{4,8},{0,12},{13,1},{9,5},{5,9},{1,13},{14,2},{10,6},... | collective-permute-start | bytes 589832 | tf_op jit(solution)/shard_map/ppermute | solution.py:60
  52.8 2.1 %collective-permute-done.14.refs_1_ = bf16[384,128]{1,0:T(8,128)(2,1)S(1)} collective-permute-done((bf16[384,128]{1,0:T(8,128)(2,1)S(1)}, bf16[384,128]{1,0:T(8,128)(2,1)S(1)}, u32[]{:S(2)}, u32[]{:S(2)}) %collective-permute-start.14) | collective-permute-done | bytes 98336 | tf_op jit(solution)/shard_map/ppermute | solution.py:60
  54.9 3.4 %collective-permute-start.15 = (bf16[384,128]{1,0:T(8,128)(2,1)S(1)}, bf16[384,128]{1,0:T(8,128)(2,1)S(1)}, u32[]{:S(2)}, u32[]{:S(2)}) collective-permute-start(bf16[384,128]{1,0:T(8,128)(2,1)S(1)} %shard_map.102), channel_id=1, source_target_pairs={{8,0},{12,4},{0,8},{4,12},{9,1},{13,5},{1,9},{5,13},{10,2},{14,6},... | collective-permute-start | bytes 294920 | tf_op jit(solution)/shard_map/ppermute | solution.py:60
  58.4 1.0 %collective-permute-start.13 = (bf16[384,128]{1,0:T(8,128)(2,1)S(1)}, bf16[384,128]{1,0:T(8,128)(2,1)S(1)}, u32[]{:S(2)}, u32[]{:S(2)}) collective-permute-start(bf16[384,128]{1,0:T(8,128)(2,1)S(1)} %shard_map.100), channel_id=1, source_target_pairs={{8,0},{12,4},{0,8},{4,12},{9,1},{13,5},{1,9},{5,13},{10,2},{14,6},... | collective-permute-start | bytes 294920 | tf_op jit(solution)/shard_map/ppermute | solution.py:60
  59.4 6.4 %collective-permute-done.15.refs_3_ = bf16[384,128]{1,0:T(8,128)(2,1)S(1)} collective-permute-done((bf16[384,128]{1,0:T(8,128)(2,1)S(1)}, bf16[384,128]{1,0:T(8,128)(2,1)S(1)}, u32[]{:S(2)}, u32[]{:S(2)}) %collective-permute-start.15) | collective-permute-done | bytes 98336 | tf_op jit(solution)/shard_map/ppermute | solution.py:60
  65.8 1.1 %collective-permute-done.13.refs_2_ = bf16[384,128]{1,0:T(8,128)(2,1)S(1)} collective-permute-done((bf16[384,128]{1,0:T(8,128)(2,1)S(1)}, bf16[384,128]{1,0:T(8,128)(2,1)S(1)}, u32[]{:S(2)}, u32[]{:S(2)}) %collective-permute-start.13) | collective-permute-done | bytes 98336 | tf_op jit(solution)/shard_map/ppermute | solution.py:60
  67.5 1.1 %shard_map.106 = bf16[64,2048]{1,0:T(8,128)(2,1)} custom-call(f32[64,2048]{1,0:T(8,128)S(1)} %get-tuple-element.57.partial, f32[64,2048]{1,0:T(8,128)S(1)} %get-tuple-element.62.kept_sum, bf16[48,64]{1,0:T(8,128)(2,1)S(1)} %get-tuple-element.63.refs_0_, bf16[48,64]{1,0:T(8,128)(2,1)S(1)} %get-tuple-element.64.refs_1_, ...), custom_call_target="tpu_custom_call" | custom-call | tf_op jit(solution)/shard_map/pallas_call | solution.py:22
  (50 shorter events, 3.3 us)
Async XLA Ops:
  1.4 15.2 %collective-permute-start.3 = (bf16[784,128]{1,0:T(8,128)(2,1)S(1)}, bf16[784,128]{1,0:T(8,128)(2,1)S(1)}, u32[]{:S(2)}, u32[]{:S(2)}) collective-permute-start(bf16[784,128]{1,0:T(8,128)(2,1)S(1)} %get-tuple-element.39), channel_id=1, source_target_pairs={{0,8},{4,12},{8,0},{12,4},{1,9},{5,13},{9,1},{13,5},{2,10},{6,14},... | collective-permute-start | bytes 602120 | tf_op jit(solution)/shard_map/ppermute | solution.py:60
  5.5 22.2 %slice-start = ((s8[6291456]{0:T(1024)(128)(4,1)}), s8[4194304]{0:T(1024)(128)(4,1)S(1)}, s32[]{:S(2)}) async-start(s8[6291456]{0:T(1024)(128)(4,1)} %bitcast.8), calls=%async_computation | async-start | bytes 8388608
  5.5 22.2 %slice-start.2 = ((s8[6291456]{0:T(1024)(128)(4,1)}), s8[4194304]{0:T(1024)(128)(4,1)S(1)}, s32[]{:S(2)}) async-start(s8[6291456]{0:T(1024)(128)(4,1)} %bitcast.11), calls=%async_computation.2 | async-start | bytes 8388608
  5.5 22.2 %slice-start.4 = ((s8[6291456]{0:T(1024)(128)(4,1)}), s8[4194304]{0:T(1024)(128)(4,1)S(1)}, s32[]{:S(2)}) async-start(s8[6291456]{0:T(1024)(128)(4,1)} %bitcast.14), calls=%async_computation.4 | async-start | bytes 8388608
  5.5 21.5 %copy-start = (bf16[1,2048,128]{2,1,0:T(8,128)(2,1)S(1)}, bf16[1,2048,128]{2,1,0:T(8,128)(2,1)}, u32[]{:S(2)}) copy-start(bf16[1,2048,128]{2,1,0:T(8,128)(2,1)} %param.16) | copy-start | bytes 1572868
  5.5 22.2 %slice-start.1 = ((s8[6291456]{0:T(1024)(128)(4,1)}), s8[2097152]{0:T(1024)(128)(4,1)S(1)}, s32[]{:S(2)}) async-start(s8[6291456]{0:T(1024)(128)(4,1)} %bitcast.8), calls=%async_computation.1 | async-start | bytes 4194304
  5.5 22.2 %slice-start.3 = ((s8[6291456]{0:T(1024)(128)(4,1)}), s8[2097152]{0:T(1024)(128)(4,1)S(1)}, s32[]{:S(2)}) async-start(s8[6291456]{0:T(1024)(128)(4,1)} %bitcast.11), calls=%async_computation.3 | async-start | bytes 4194304
  5.5 22.2 %slice-start.5 = ((s8[6291456]{0:T(1024)(128)(4,1)}), s8[2097152]{0:T(1024)(128)(4,1)S(1)}, s32[]{:S(2)}) async-start(s8[6291456]{0:T(1024)(128)(4,1)} %bitcast.14), calls=%async_computation.5 | async-start | bytes 4194304
  5.6 19.4 %collective-permute-start = (bf16[784,128]{1,0:T(8,128)(2,1)S(1)}, bf16[784,128]{1,0:T(8,128)(2,1)S(1)}, u32[]{:S(2)}, u32[]{:S(2)}) collective-permute-start(bf16[784,128]{1,0:T(8,128)(2,1)S(1)} %shard_map.92.refs_0_.refs_6_.refs_4_), channel_id=1, source_target_pairs={{0,2},{2,0},{1,3},{3,1},{4,6},{6,4},{5,7},{7,5},{8,10},{10,8},{9,1... | collective-permute-start | bytes 602120 | tf_op jit(solution)/shard_map/ppermute | solution.py:60
  7.1 11.4 %collective-permute-start.1 = (bf16[384,128]{1,0:T(8,128)(2,1)S(1)}, bf16[384,128]{1,0:T(8,128)(2,1)S(1)}, u32[]{:S(2)}, u32[]{:S(2)}) collective-permute-start(bf16[384,128]{1,0:T(8,128)(2,1)S(1)} %get-tuple-element.38), channel_id=1, source_target_pairs={{0,4},{4,0},{8,12},{12,8},{1,5},{5,1},{9,13},{13,9},{2,6},{6,2},{1... | collective-permute-start | bytes 294920 | tf_op jit(solution)/shard_map/ppermute | solution.py:60
  8.7 12.3 %collective-permute-start.7 = (bf16[400,128]{1,0:T(8,128)(2,1)S(1)}, bf16[400,128]{1,0:T(8,128)(2,1)S(1)}, u32[]{:S(2)}, u32[]{:S(2)}) collective-permute-start(bf16[400,128]{1,0:T(8,128)(2,1)S(1)} %get-tuple-element.41), channel_id=1, source_target_pairs={{0,4},{4,0},{8,12},{12,8},{1,5},{5,1},{9,13},{13,9},{2,6},{6,2},{1... | collective-permute-start | bytes 307208 | tf_op jit(solution)/shard_map/ppermute | solution.py:60
  9.1 12.5 %collective-permute-start.8 = (bf16[400,128]{1,0:T(8,128)(2,1)S(1)}, bf16[400,128]{1,0:T(8,128)(2,1)S(1)}, u32[]{:S(2)}, u32[]{:S(2)}) collective-permute-start(bf16[400,128]{1,0:T(8,128)(2,1)S(1)} %get-tuple-element.42), channel_id=1, source_target_pairs={{0,12},{4,8},{8,4},{12,0},{1,13},{5,9},{9,5},{13,1},{2,14},{6,10},... | collective-permute-start | bytes 307208 | tf_op jit(solution)/shard_map/ppermute | solution.py:60
  16.6 14.2 %collective-permute-start.4 = (bf16[784,128]{1,0:T(8,128)(2,1)S(1)}, bf16[784,128]{1,0:T(8,128)(2,1)S(1)}, u32[]{:S(2)}, u32[]{:S(2)}) collective-permute-start(bf16[784,128]{1,0:T(8,128)(2,1)S(1)} %collective-permute-done.3.refs_2_.refs_8_.refs_6_), channel_id=1, source_target_pairs={{0,2},{2,0},{1,3},{3,1},{4,6},{6,4},{5,7},{7,5},{8,10},{10,8},{9,1... | collective-permute-start | bytes 602120 | tf_op jit(solution)/shard_map/ppermute | solution.py:60
  18.6 6.4 %collective-permute-start.5 = (bf16[384,128]{1,0:T(8,128)(2,1)S(1)}, bf16[384,128]{1,0:T(8,128)(2,1)S(1)}, u32[]{:S(2)}, u32[]{:S(2)}) collective-permute-start(bf16[384,128]{1,0:T(8,128)(2,1)S(1)} %get-tuple-element.40), channel_id=1, source_target_pairs={{0,12},{4,8},{8,4},{12,0},{1,13},{5,9},{9,5},{13,1},{2,14},{6,10},... | collective-permute-start | bytes 294920 | tf_op jit(solution)/shard_map/ppermute | solution.py:60
  21.0 6.6 %collective-permute-start.10 = (bf16[400,128]{1,0:T(8,128)(2,1)S(1)}, bf16[400,128]{1,0:T(8,128)(2,1)S(1)}, u32[]{:S(2)}, u32[]{:S(2)}) collective-permute-start(bf16[400,128]{1,0:T(8,128)(2,1)S(1)} %collective-permute-done.7.refs_1_.refs_7_.refs_5_), channel_id=1, source_target_pairs={{0,2},{2,0},{1,3},{3,1},{4,6},{6,4},{5,7},{7,5},{8,10},{10,8},{9,1... | collective-permute-start | bytes 307208 | tf_op jit(solution)/shard_map/ppermute | solution.py:60
  21.6 9.1 %collective-permute-start.11 = (bf16[400,128]{1,0:T(8,128)(2,1)S(1)}, bf16[400,128]{1,0:T(8,128)(2,1)S(1)}, u32[]{:S(2)}, u32[]{:S(2)}) collective-permute-start(bf16[400,128]{1,0:T(8,128)(2,1)S(1)} %collective-permute-done.8.refs_3_.refs_9_.refs_7_), channel_id=1, source_target_pairs={{0,2},{2,0},{1,3},{3,1},{4,6},{6,4},{5,7},{7,5},{8,10},{10,8},{9,1... | collective-permute-start | bytes 307208 | tf_op jit(solution)/shard_map/ppermute | solution.py:60
  25.0 6.6 %collective-permute-start.2 = (bf16[384,128]{1,0:T(8,128)(2,1)S(1)}, bf16[384,128]{1,0:T(8,128)(2,1)S(1)}, u32[]{:S(2)}, u32[]{:S(2)}) collective-permute-start(bf16[384,128]{1,0:T(8,128)(2,1)S(1)} %collective-permute-done.1.refs_1_), channel_id=1, source_target_pairs={{0,2},{2,0},{1,3},{3,1},{4,6},{6,4},{5,7},{7,5},{8,10},{10,8},{9,1... | collective-permute-start | bytes 294920 | tf_op jit(solution)/shard_map/ppermute | solution.py:60
  25.0 6.6 %collective-permute-start.6 = (bf16[384,128]{1,0:T(8,128)(2,1)S(1)}, bf16[384,128]{1,0:T(8,128)(2,1)S(1)}, u32[]{:S(2)}, u32[]{:S(2)}) collective-permute-start(bf16[384,128]{1,0:T(8,128)(2,1)S(1)} %collective-permute-done.5.refs_3_), channel_id=1, source_target_pairs={{0,2},{2,0},{1,3},{3,1},{4,6},{6,4},{5,7},{7,5},{8,10},{10,8},{9,1... | collective-permute-start | bytes 294920 | tf_op jit(solution)/shard_map/ppermute | solution.py:60
  27.6 4.0 %collective-permute-start.9 = (f32[8,192]{1,0:T(8,128)S(1)}, f32[8,192]{1,0:T(8,128)S(1)}, u32[]{:S(2)}, u32[]{:S(2)}) collective-permute-start(f32[8,192]{1,0:T(8,128)S(1)} %shard_map.94.refs_8_), channel_id=1, source_target_pairs={{0,2},{2,0},{1,3},{3,1},{4,6},{6,4},{5,7},{7,5},{8,10},{10,8},{9,1... | collective-permute-start | bytes 18440 | tf_op jit(solution)/shard_map/ppermute | solution.py:60
  30.8 0.9 %copy-start.1 = (bf16[1,128,768]{2,1,0:T(8,128)(2,1)S(1)}, bf16[1,128,768]{2,1,0:T(8,128)(2,1)}, u32[]{:S(2)}) copy-start(bf16[1,128,768]{2,1,0:T(8,128)(2,1)} %param.17) | copy-start | bytes 589828
  33.0 11.4 %copy-start.2 = (s32[64,2]{0,1:T(2,128)S(1)}, s32[64,2]{0,1:T(2,128)}, u32[]{:S(2)}) copy-start(s32[64,2]{0,1:T(2,128)} %param.10) | copy-start | bytes 1540
  33.0 11.3 %copy-start.3 = (f32[64,2]{0,1:T(2,128)S(1)}, f32[64,2]{0,1:T(2,128)}, u32[]{:S(2)}) copy-start(f32[64,2]{0,1:T(2,128)} %param.11) | copy-start | bytes 1540
  34.9 7.3 %collective-permute-start.16 = (bf16[768,128]{1,0:T(8,128)(2,1)S(1)}, bf16[768,128]{1,0:T(8,128)(2,1)S(1)}, u32[]{:S(2)}, u32[]{:S(2)}) collective-permute-start(bf16[768,128]{1,0:T(8,128)(2,1)S(1)} %get-tuple-element.59), channel_id=1, source_target_pairs={{4,0},{0,4},{12,8},{8,12},{5,1},{1,5},{13,9},{9,13},{6,2},{2,6},{1... | collective-permute-start | bytes 589832 | tf_op jit(solution)/shard_map/ppermute | solution.py:60
  35.6 8.7 %collective-permute-start.17 = (bf16[768,128]{1,0:T(8,128)(2,1)S(1)}, bf16[768,128]{1,0:T(8,128)(2,1)S(1)}, u32[]{:S(2)}, u32[]{:S(2)}) collective-permute-start(bf16[768,128]{1,0:T(8,128)(2,1)S(1)} %get-tuple-element.61), channel_id=1, source_target_pairs={{4,0},{0,4},{12,8},{8,12},{5,1},{1,5},{13,9},{9,13},{6,2},{2,6},{1... | collective-permute-start | bytes 589832 | tf_op jit(solution)/shard_map/ppermute | solution.py:60
  37.0 12.5 %collective-permute-start.18 = (bf16[768,128]{1,0:T(8,128)(2,1)S(1)}, bf16[768,128]{1,0:T(8,128)(2,1)S(1)}, u32[]{:S(2)}, u32[]{:S(2)}) collective-permute-start(bf16[768,128]{1,0:T(8,128)(2,1)S(1)} %get-tuple-element.67), channel_id=1, source_target_pairs={{0,2},{2,0},{1,3},{3,1},{4,6},{6,4},{5,7},{7,5},{8,10},{10,8},{9,1... | collective-permute-start | bytes 589832 | tf_op jit(solution)/shard_map/ppermute | solution.py:60
  45.2 22.3 %collective-permute-start.20 = (bf16[1024,128]{1,0:T(8,128)(2,1)S(1)}, bf16[1024,128]{1,0:T(8,128)(2,1)S(1)}, u32[]{:S(2)}, u32[]{:S(2)}) collective-permute-start(bf16[1024,128]{1,0:T(8,128)(2,1)S(1)} %get-tuple-element.68), channel_id=1, source_target_pairs={{0,2},{2,0},{1,3},{3,1},{4,6},{6,4},{5,7},{7,5},{8,10},{10,8},{9,1... | collective-permute-start | bytes 786440 | tf_op jit(solution)/shard_map/ppermute | solution.py:60
  47.5 7.4 %collective-permute-start.14 = (bf16[384,128]{1,0:T(8,128)(2,1)S(1)}, bf16[384,128]{1,0:T(8,128)(2,1)S(1)}, u32[]{:S(2)}, u32[]{:S(2)}) collective-permute-start(bf16[384,128]{1,0:T(8,128)(2,1)S(1)} %get-tuple-element.56), channel_id=1, source_target_pairs={{0,2},{2,0},{1,3},{3,1},{4,6},{6,4},{5,7},{7,5},{8,10},{10,8},{9,1... | collective-permute-start | bytes 294920 | tf_op jit(solution)/shard_map/ppermute | solution.py:60
  47.6 10.8 %collective-permute-start.12 = (bf16[384,128]{1,0:T(8,128)(2,1)S(1)}, bf16[384,128]{1,0:T(8,128)(2,1)S(1)}, u32[]{:S(2)}, u32[]{:S(2)}) collective-permute-start(bf16[384,128]{1,0:T(8,128)(2,1)S(1)} %get-tuple-element.54), channel_id=1, source_target_pairs={{0,2},{2,0},{1,3},{3,1},{4,6},{6,4},{5,7},{7,5},{8,10},{10,8},{9,1... | collective-permute-start | bytes 294920 | tf_op jit(solution)/shard_map/ppermute | solution.py:60
  49.6 17.9 %collective-permute-start.19 = (bf16[768,128]{1,0:T(8,128)(2,1)S(1)}, bf16[768,128]{1,0:T(8,128)(2,1)S(1)}, u32[]{:S(2)}, u32[]{:S(2)}) collective-permute-start(bf16[768,128]{1,0:T(8,128)(2,1)S(1)} %shard_map.105), channel_id=1, source_target_pairs={{12,0},{8,4},{4,8},{0,12},{13,1},{9,5},{5,9},{1,13},{14,2},{10,6},... | collective-permute-start | bytes 589832 | tf_op jit(solution)/shard_map/ppermute | solution.py:60
  54.9 10.9 %collective-permute-start.15 = (bf16[384,128]{1,0:T(8,128)(2,1)S(1)}, bf16[384,128]{1,0:T(8,128)(2,1)S(1)}, u32[]{:S(2)}, u32[]{:S(2)}) collective-permute-start(bf16[384,128]{1,0:T(8,128)(2,1)S(1)} %shard_map.102), channel_id=1, source_target_pairs={{8,0},{12,4},{0,8},{4,12},{9,1},{13,5},{1,9},{5,13},{10,2},{14,6},... | collective-permute-start | bytes 294920 | tf_op jit(solution)/shard_map/ppermute | solution.py:60
  58.4 8.5 %collective-permute-start.13 = (bf16[384,128]{1,0:T(8,128)(2,1)S(1)}, bf16[384,128]{1,0:T(8,128)(2,1)S(1)}, u32[]{:S(2)}, u32[]{:S(2)}) collective-permute-start(bf16[384,128]{1,0:T(8,128)(2,1)S(1)} %shard_map.100), channel_id=1, source_target_pairs={{8,0},{12,4},{0,8},{4,12},{9,1},{13,5},{1,9},{5,13},{10,2},{14,6},... | collective-permute-start | bytes 294920 | tf_op jit(solution)/shard_map/ppermute | solution.py:60

commit v5 on v4

--- a/solution.py
+++ b/solution.py
@@ -215,24 +215,10 @@
 
     sent = [*call(pace, [there[0].shape], (sent[0],), flops=10**10), *sent[1:]]
 
-    def load(*refs):
-        sems = refs[6]
-        copies = [pltpu.make_async_copy(refs[i], refs[3 + i], sems.at[i]) for i in range(3)]
-        for c in copies:
-            c.start()
-        for c in copies:
-            c.wait()
-
-    weights = (gate_weight[0], up_weight[0], down_weight[0])
-    gate_w, up_w, down_w = pl.pallas_call(
-        load,
-        out_shape=[pltpu.VMEM(w.shape, w.dtype) for w in weights],
-        in_specs=[ANY] * 3,
-        out_specs=[VMEM] * 3,
-        scratch_shapes=[pltpu.SemaphoreType.DMA((3,))],
-        compiler_params=pltpu.CompilerParams(vmem_limit_bytes=4 << 20),
-        name="load",
-    )(*weights)
+    gate_w, up_w, down_w = (
+        pltpu.with_memory_space_constraint(w[0], pltpu.VMEM)
+        for w in (gate_weight, up_weight, down_weight)
+    )
 
     arrived = [s if p.step == 0 else permute(s, "expert", p.step) for p, s in zip(there, sent)]
     others = [[permute(a, "hidden", d) for a in arrived] for d in range(1, hiddens)]
@@ -291,7 +277,7 @@
             refs[-2][...] = gate
             refs[-1][...] = up
 
-        sums = call(own_step, acc, (*values, gate_w, up_w, *(sums or ())))
+        sums = call(own_step, acc, (*values, gate_w, up_w, *(sums or (down_w,))))
 
     def partner_parts(refs, lo, hi, gate_ref, up_ref, gate, up, pieces):
         for d in range(1, hiddens):

time: 68.8 us -> 68.8 us (level)
  waiting for transfers between devices: 22.9 us -> 25.7 us
  starting transfers between devices: 33.8 us -> 32.3 us
  Pallas kernels: 11.6 us -> 10.3 us
    ppermute x21, waiting for transfers between devices: 22.9 us -> 25.7 us  [permute(): return lax.ppermute(value, axis, pairs)]
    ppermute x21, starting transfers between devices: 33.8 us -> 32.3 us  [permute(): return lax.ppermute(value, axis, pairs)]
    pallas_call x1 -> x0, Pallas kernels: 1.29 us -> none  [local(): pl.pallas_call(load, out_shape=[pltpu.VMEM(w.shape, w.dtype) for w in wei...]
  transfers between devices with their start and end apart: 21 -> 21, of which waited for: 7 -> 10; matrix products, arithmetic and copies ran while one was open for 0% -> 0% of each run, Pallas kernels for 9% -> 7%
where the time goes in v5:
time: 68.8 us; the launch traced here: 68.6 us
  starting transfers between devices  32.3 us (47%)
  waiting for transfers between devices  25.7 us (37%)
  Pallas kernels  10.3 us (15%)
    ppermute x21, starting transfers between devices, permute(): return lax.ppermute(value, axis, pairs)  32.3 us
    ppermute x21, waiting for transfers between devices, permute(): return lax.ppermute(value, axis, pairs)  25.7 us
    pallas_call x16, Pallas kernels, call(): pl.pallas_call(body, out_shape=outs, in_specs=in_specs or [VMEM] * len(in...  10.3 us
  transfers between devices with their start and end apart: 21, of which 10 were waited for; matrix products, arithmetic and copies ran while one was open for 0% of the time, Pallas kernels for 7%

profile of v5, /device:TPU:0, one launch (start us, length us, event | category | flops | bytes accessed | tf_op | source)
XLA Modules:
  0.0 68.6 jit_solution(783591709363195028)
XLA Ops:
  0.0 1.4 %shard_map.91 = (bf16[784,128]{1,0:T(8,128)(2,1)S(1)}, bf16[400,128]{1,0:T(8,128)(2,1)S(1)}, bf16[384,128]{1,0:T(8,128)(2,1)S(1)}, bf16[784,128]{1,0:T(8,128)(2,...) custom-call(s32[2,64]{1,0:T(2,128)} %bitcast.29, s32[4,8]{1,0:T(4,128)} %bitcast.34, ...), custom_call_target="tpu_custom_call" | custom-call | tf_op jit(solution)/shard_map/pallas_call | solution.py:22
  1.4 4.1 %collective-permute-start.3 = (bf16[784,128]{1,0:T(8,128)(2,1)S(1)}, bf16[784,128]{1,0:T(8,128)(2,1)S(1)}, u32[]{:S(2)}, u32[]{:S(2)}) collective-permute-start(bf16[784,128]{1,0:T(8,128)(2,1)S(1)} %get-tuple-element.36), channel_id=1, source_target_pairs={{0,8},{4,12},{8,0},{12,4},{1,9},{5,13},{9,1},{13,5},{2,10},{6,14},... | collective-permute-start | bytes 602120 | tf_op jit(solution)/shard_map/ppermute | solution.py:60
  5.6 1.6 %collective-permute-start = (bf16[784,128]{1,0:T(8,128)(2,1)S(1)}, bf16[784,128]{1,0:T(8,128)(2,1)S(1)}, u32[]{:S(2)}, u32[]{:S(2)}) collective-permute-start(bf16[784,128]{1,0:T(8,128)(2,1)S(1)} %shard_map.92.refs_0_.refs_6_.refs_4_), channel_id=1, source_target_pairs={{0,2},{2,0},{1,3},{3,1},{4,6},{6,4},{5,7},{7,5},{8,10},{10,8},{9,1... | collective-permute-start | bytes 602120 | tf_op jit(solution)/shard_map/ppermute | solution.py:60
  7.1 1.6 %collective-permute-start.1 = (bf16[384,128]{1,0:T(8,128)(2,1)S(1)}, bf16[384,128]{1,0:T(8,128)(2,1)S(1)}, u32[]{:S(2)}, u32[]{:S(2)}) collective-permute-start(bf16[384,128]{1,0:T(8,128)(2,1)S(1)} %get-tuple-element.35), channel_id=1, source_target_pairs={{0,4},{4,0},{8,12},{12,8},{1,5},{5,1},{9,13},{13,9},{2,6},{6,2},{1... | collective-permute-start | bytes 294920 | tf_op jit(solution)/shard_map/ppermute | solution.py:60
  9.1 1.3 %collective-permute-start.8 = (bf16[400,128]{1,0:T(8,128)(2,1)S(1)}, bf16[400,128]{1,0:T(8,128)(2,1)S(1)}, u32[]{:S(2)}, u32[]{:S(2)}) collective-permute-start(bf16[400,128]{1,0:T(8,128)(2,1)S(1)} %get-tuple-element.39), channel_id=1, source_target_pairs={{0,12},{4,8},{8,4},{12,0},{1,13},{5,9},{9,5},{13,1},{2,14},{6,10},... | collective-permute-start | bytes 307208 | tf_op jit(solution)/shard_map/ppermute | solution.py:60
  10.5 6.1 %collective-permute-done.3.refs_2_.refs_8_.refs_6_ = bf16[784,128]{1,0:T(8,128)(2,1)S(1)} collective-permute-done((bf16[784,128]{1,0:T(8,128)(2,1)S(1)}, bf16[784,128]{1,0:T(8,128)(2,1)S(1)}, u32[]{:S(2)}, u32[]{:S(2)}) %collective-permute-start.3) | collective-permute-done | bytes 200736 | tf_op jit(solution)/shard_map/ppermute | solution.py:60
  16.6 2.0 %collective-permute-start.4 = (bf16[784,128]{1,0:T(8,128)(2,1)S(1)}, bf16[784,128]{1,0:T(8,128)(2,1)S(1)}, u32[]{:S(2)}, u32[]{:S(2)}) collective-permute-start(bf16[784,128]{1,0:T(8,128)(2,1)S(1)} %collective-permute-done.3.refs_2_.refs_8_.refs_6_), channel_id=1, source_target_pairs={{0,2},{2,0},{1,3},{3,1},{4,6},{6,4},{5,7},{7,5},{8,10},{10,8},{9,1... | collective-permute-start | bytes 602120 | tf_op jit(solution)/shard_map/ppermute | solution.py:60
  18.6 2.5 %collective-permute-start.5 = (bf16[384,128]{1,0:T(8,128)(2,1)S(1)}, bf16[384,128]{1,0:T(8,128)(2,1)S(1)}, u32[]{:S(2)}, u32[]{:S(2)}) collective-permute-start(bf16[384,128]{1,0:T(8,128)(2,1)S(1)} %get-tuple-element.37), channel_id=1, source_target_pairs={{0,12},{4,8},{8,4},{12,0},{1,13},{5,9},{9,5},{13,1},{2,14},{6,10},... | collective-permute-start | bytes 294920 | tf_op jit(solution)/shard_map/ppermute | solution.py:60
  21.6 1.5 %collective-permute-start.11 = (bf16[400,128]{1,0:T(8,128)(2,1)S(1)}, bf16[400,128]{1,0:T(8,128)(2,1)S(1)}, u32[]{:S(2)}, u32[]{:S(2)}) collective-permute-start(bf16[400,128]{1,0:T(8,128)(2,1)S(1)} %collective-permute-done.8.refs_3_.refs_9_.refs_7_), channel_id=1, source_target_pairs={{0,2},{2,0},{1,3},{3,1},{4,6},{6,4},{5,7},{7,5},{8,10},{10,8},{9,1... | collective-permute-start | bytes 307208 | tf_op jit(solution)/shard_map/ppermute | solution.py:60
  23.1 1.9 %collective-permute-done.5.refs_3_ = bf16[384,128]{1,0:T(8,128)(2,1)S(1)} collective-permute-done((bf16[384,128]{1,0:T(8,128)(2,1)S(1)}, bf16[384,128]{1,0:T(8,128)(2,1)S(1)}, u32[]{:S(2)}, u32[]{:S(2)}) %collective-permute-start.5) | collective-permute-done | bytes 98336 | tf_op jit(solution)/shard_map/ppermute | solution.py:60
  25.0 2.0 %collective-permute-start.6 = (bf16[384,128]{1,0:T(8,128)(2,1)S(1)}, bf16[384,128]{1,0:T(8,128)(2,1)S(1)}, u32[]{:S(2)}, u32[]{:S(2)}) collective-permute-start(bf16[384,128]{1,0:T(8,128)(2,1)S(1)} %collective-permute-done.5.refs_3_), channel_id=1, source_target_pairs={{0,2},{2,0},{1,3},{3,1},{4,6},{6,4},{5,7},{7,5},{8,10},{10,8},{9,1... | collective-permute-start | bytes 294920 | tf_op jit(solution)/shard_map/ppermute | solution.py:60
  27.8 0.8 %shard_map.95 = (f32[192,768]{1,0:T(8,128)S(1)}, f32[192,768]{1,0:T(8,128)S(1)}) custom-call(bf16[784,128]{1,0:T(8,128)(2,1)S(1)} %shard_map.92.refs_0_.refs_6_.refs_4_, bf16[400,128]{1,0:T(8,128)(2,1)S(1)} %collective-permute-done.7.refs_1_.refs_7_.refs_5_, bf16[784,128]{1,0:T(8,128)(2,1)S(1)} %collective-permute-done.3.refs_2_.refs_8_.refs_6_, ...), custom_call_target="tpu_custom_call" | custom-call | tf_op jit(solution)/shard_map/pallas_call | solution.py:22
  28.6 0.8 %shard_map.96 = (f32[192,768]{1,0:T(8,128)S(1)}, f32[192,768]{1,0:T(8,128)S(1)}) custom-call(bf16[784,128]{1,0:T(8,128)(2,1)S(1)} %shard_map.92.refs_0_.refs_6_.refs_4_, bf16[384,128]{1,0:T(8,128)(2,1)S(1)} %collective-permute-done.1.refs_1_, bf16[784,128]{1,0:T(8,128)(2,1)S(1)} %collective-permute-done.3.refs_2_.refs_8_.refs_6_, ...), custom_call_target="tpu_custom_call" | custom-call | tf_op jit(solution)/shard_map/pallas_call | solution.py:22
  29.5 0.8 %shard_map.97 = (f32[192,768]{1,0:T(8,128)S(1)}, f32[192,768]{1,0:T(8,128)S(1)}) custom-call(bf16[784,128]{1,0:T(8,128)(2,1)S(1)} %collective-permute-done.refs_0_, bf16[400,128]{1,0:T(8,128)(2,1)S(1)} %collective-permute-done.10.refs_1_, bf16[784,128]{1,0:T(8,128)(2,1)S(1)} %collective-permute-done.4.refs_2_, ...), custom_call_target="tpu_custom_call" | custom-call | tf_op jit(solution)/shard_map/pallas_call | solution.py:22
  30.5 1.1 %collective-permute-done.6.refs_3_ = bf16[384,128]{1,0:T(8,128)(2,1)S(1)} collective-permute-done((bf16[384,128]{1,0:T(8,128)(2,1)S(1)}, bf16[384,128]{1,0:T(8,128)(2,1)S(1)}, u32[]{:S(2)}, u32[]{:S(2)}) %collective-permute-start.6) | collective-permute-done | bytes 98336 | tf_op jit(solution)/shard_map/ppermute | solution.py:60
  31.6 1.3 %shard_map.98 = (bf16[192,768]{1,0:T(8,128)(2,1)S(1)}, bf16[384,128]{1,0:T(8,128)(2,1)S(1)}) custom-call(bf16[784,128]{1,0:T(8,128)(2,1)S(1)} %collective-permute-done.refs_0_, bf16[384,128]{1,0:T(8,128)(2,1)S(1)} %collective-permute-done.2.refs_1_, bf16[784,128]{1,0:T(8,128)(2,1)S(1)} %collective-permute-done.4.refs_2_, ...), custom_call_target="tpu_custom_call" | custom-call | tf_op jit(solution)/shard_map/pallas_call | solution.py:22
  33.0 1.1 %shard_map.99 = (bf16[768,128]{1,0:T(8,128)(2,1)S(1)}, bf16[768,128]{1,0:T(8,128)(2,1)S(1)}, bf16[384,128]{1,0:T(8,128)(2,1)S(1)}, bf16[768,128]{1,0:T(8,128)(2,1)S(1)}, bf16[384,128]{1,0:T(8,128)(2,1)S(1)}) custom-call(bf16[192,768]{1,0:T(8,128)(2,1)S(1)} %get-tuple-element.46.act_ref, bf16[768,4096]{1,0:T(8,128)(2,1)S(1)} %bitcast.24), custom_call_target="tpu_custom_call" | custom-call | tf_op jit(solution)/shard_map/pallas_call | solution.py:22
  34.1 0.8 %shard_map.101 = (bf16[768,128]{1,0:T(8,128)(2,1)S(1)}, bf16[768,128]{1,0:T(8,128)(2,1)S(1)}, bf16[384,128]{1,0:T(8,128)(2,1)S(1)}, bf16[768,128]{1,0:T(8,128)(2,1)S(1)}) custom-call(bf16[192,768]{1,0:T(8,128)(2,1)S(1)} %get-tuple-element.46.act_ref, bf16[768,4096]{1,0:T(8,128)(2,1)S(1)} %bitcast.25), custom_call_target="tpu_custom_call" | custom-call | tf_op jit(solution)/shard_map/pallas_call | solution.py:22
  35.1 1.9 %collective-permute-start.16 = (bf16[768,128]{1,0:T(8,128)(2,1)S(1)}, bf16[768,128]{1,0:T(8,128)(2,1)S(1)}, u32[]{:S(2)}, u32[]{:S(2)}) collective-permute-start(bf16[768,128]{1,0:T(8,128)(2,1)S(1)} %get-tuple-element.53), channel_id=1, source_target_pairs={{4,0},{0,4},{12,8},{8,12},{5,1},{1,5},{13,9},{9,13},{6,2},{2,6},{1... | collective-permute-start | bytes 589832 | tf_op jit(solution)/shard_map/ppermute | solution.py:60
  37.0 1.4 %collective-permute-start.18 = (bf16[768,128]{1,0:T(8,128)(2,1)S(1)}, bf16[768,128]{1,0:T(8,128)(2,1)S(1)}, u32[]{:S(2)}, u32[]{:S(2)}) collective-permute-start(bf16[768,128]{1,0:T(8,128)(2,1)S(1)} %get-tuple-element.61), channel_id=1, source_target_pairs={{0,2},{2,0},{1,3},{3,1},{4,6},{6,4},{5,7},{7,5},{8,10},{10,8},{9,1... | collective-permute-start | bytes 589832 | tf_op jit(solution)/shard_map/ppermute | solution.py:60
  38.4 3.9 %collective-permute-done.17.refs_3_ = bf16[768,128]{1,0:T(8,128)(2,1)S(1)} collective-permute-done((bf16[768,128]{1,0:T(8,128)(2,1)S(1)}, bf16[768,128]{1,0:T(8,128)(2,1)S(1)}, u32[]{:S(2)}, u32[]{:S(2)}) %collective-permute-start.17) | collective-permute-done | bytes 196640 | tf_op jit(solution)/shard_map/ppermute | solution.py:60
  42.2 2.1 %collective-permute-done.16.refs_1_ = bf16[768,128]{1,0:T(8,128)(2,1)S(1)} collective-permute-done((bf16[768,128]{1,0:T(8,128)(2,1)S(1)}, bf16[768,128]{1,0:T(8,128)(2,1)S(1)}, u32[]{:S(2)}, u32[]{:S(2)}) %collective-permute-start.16) | collective-permute-done | bytes 196640 | tf_op jit(solution)/shard_map/ppermute | solution.py:60
  44.4 0.8 %shard_map.104 = (f32[64,2048]{1,0:T(8,128)S(1)}, bf16[1024,128]{1,0:T(8,128)(2,1)S(1)}) custom-call(s32[2,64]{1,0:T(2,128)S(1)} %bitcast.30, f32[2,64]{1,0:T(2,128)S(1)} %bitcast.32, bf16[768,128]{1,0:T(8,128)(2,1)S(1)} %get-tuple-element.52.refs_0_, bf16[768,128]{1,0:T(8,128)(2,1)S(1)} %collective-permute-done.16.refs_1_, ...), custom_call_target="tpu_custom_call" | custom-call | tf_op jit(solution)/shard_map/pallas_call | solution.py:22
  45.2 2.3 %collective-permute-start.20 = (bf16[1024,128]{1,0:T(8,128)(2,1)S(1)}, bf16[1024,128]{1,0:T(8,128)(2,1)S(1)}, u32[]{:S(2)}, u32[]{:S(2)}) collective-permute-start(bf16[1024,128]{1,0:T(8,128)(2,1)S(1)} %get-tuple-element.62), channel_id=1, source_target_pairs={{0,2},{2,0},{1,3},{3,1},{4,6},{6,4},{5,7},{7,5},{8,10},{10,8},{9,1... | collective-permute-start | bytes 786440 | tf_op jit(solution)/shard_map/ppermute | solution.py:60
  47.6 1.9 %collective-permute-start.12 = (bf16[384,128]{1,0:T(8,128)(2,1)S(1)}, bf16[384,128]{1,0:T(8,128)(2,1)S(1)}, u32[]{:S(2)}, u32[]{:S(2)}) collective-permute-start(bf16[384,128]{1,0:T(8,128)(2,1)S(1)} %get-tuple-element.48), channel_id=1, source_target_pairs={{0,2},{2,0},{1,3},{3,1},{4,6},{6,4},{5,7},{7,5},{8,10},{10,8},{9,1... | collective-permute-start | bytes 294920 | tf_op jit(solution)/shard_map/ppermute | solution.py:60
  49.6 3.2 %collective-permute-start.19 = (bf16[768,128]{1,0:T(8,128)(2,1)S(1)}, bf16[768,128]{1,0:T(8,128)(2,1)S(1)}, u32[]{:S(2)}, u32[]{:S(2)}) collective-permute-start(bf16[768,128]{1,0:T(8,128)(2,1)S(1)} %shard_map.105), channel_id=1, source_target_pairs={{12,0},{8,4},{4,8},{0,12},{13,1},{9,5},{5,9},{1,13},{14,2},{10,6},... | collective-permute-start | bytes 589832 | tf_op jit(solution)/shard_map/ppermute | solution.py:60
  52.8 2.7 %collective-permute-done.14.refs_1_ = bf16[384,128]{1,0:T(8,128)(2,1)S(1)} collective-permute-done((bf16[384,128]{1,0:T(8,128)(2,1)S(1)}, bf16[384,128]{1,0:T(8,128)(2,1)S(1)}, u32[]{:S(2)}, u32[]{:S(2)}) %collective-permute-start.14) | collective-permute-done | bytes 98336 | tf_op jit(solution)/shard_map/ppermute | solution.py:60
  55.5 2.5 %collective-permute-start.15 = (bf16[384,128]{1,0:T(8,128)(2,1)S(1)}, bf16[384,128]{1,0:T(8,128)(2,1)S(1)}, u32[]{:S(2)}, u32[]{:S(2)}) collective-permute-start(bf16[384,128]{1,0:T(8,128)(2,1)S(1)} %shard_map.102), channel_id=1, source_target_pairs={{8,0},{12,4},{0,8},{4,12},{9,1},{13,5},{1,9},{5,13},{10,2},{14,6},... | collective-permute-start | bytes 294920 | tf_op jit(solution)/shard_map/ppermute | solution.py:60
  58.0 1.0 %collective-permute-start.13 = (bf16[384,128]{1,0:T(8,128)(2,1)S(1)}, bf16[384,128]{1,0:T(8,128)(2,1)S(1)}, u32[]{:S(2)}, u32[]{:S(2)}) collective-permute-start(bf16[384,128]{1,0:T(8,128)(2,1)S(1)} %shard_map.100), channel_id=1, source_target_pairs={{8,0},{12,4},{0,8},{4,12},{9,1},{13,5},{1,9},{5,13},{10,2},{14,6},... | collective-permute-start | bytes 294920 | tf_op jit(solution)/shard_map/ppermute | solution.py:60
  59.1 6.7 %collective-permute-done.15.refs_3_ = bf16[384,128]{1,0:T(8,128)(2,1)S(1)} collective-permute-done((bf16[384,128]{1,0:T(8,128)(2,1)S(1)}, bf16[384,128]{1,0:T(8,128)(2,1)S(1)}, u32[]{:S(2)}, u32[]{:S(2)}) %collective-permute-start.15) | collective-permute-done | bytes 98336 | tf_op jit(solution)/shard_map/ppermute | solution.py:60
  65.8 1.1 %collective-permute-done.13.refs_2_ = bf16[384,128]{1,0:T(8,128)(2,1)S(1)} collective-permute-done((bf16[384,128]{1,0:T(8,128)(2,1)S(1)}, bf16[384,128]{1,0:T(8,128)(2,1)S(1)}, u32[]{:S(2)}, u32[]{:S(2)}) %collective-permute-start.13) | collective-permute-done | bytes 98336 | tf_op jit(solution)/shard_map/ppermute | solution.py:60
  67.5 1.1 %shard_map.106 = bf16[64,2048]{1,0:T(8,128)(2,1)} custom-call(f32[64,2048]{1,0:T(8,128)S(1)} %get-tuple-element.51.partial, f32[64,2048]{1,0:T(8,128)S(1)} %get-tuple-element.56.kept_sum, bf16[48,64]{1,0:T(8,128)(2,1)S(1)} %get-tuple-element.57.refs_0_, bf16[48,64]{1,0:T(8,128)(2,1)S(1)} %get-tuple-element.58.refs_1_, ...), custom_call_target="tpu_custom_call" | custom-call | tf_op jit(solution)/shard_map/pallas_call | solution.py:22
  (49 shorter events, 3.1 us)
Async XLA Ops:
  1.4 15.2 %collective-permute-start.3 = (bf16[784,128]{1,0:T(8,128)(2,1)S(1)}, bf16[784,128]{1,0:T(8,128)(2,1)S(1)}, u32[]{:S(2)}, u32[]{:S(2)}) collective-permute-start(bf16[784,128]{1,0:T(8,128)(2,1)S(1)} %get-tuple-element.36), channel_id=1, source_target_pairs={{0,8},{4,12},{8,0},{12,4},{1,9},{5,13},{9,1},{13,5},{2,10},{6,14},... | collective-permute-start | bytes 602120 | tf_op jit(solution)/shard_map/ppermute | solution.py:60
  5.5 22.2 %slice-start = ((s8[6291456]{0:T(1024)(128)(4,1)}), s8[4194304]{0:T(1024)(128)(4,1)S(1)}, s32[]{:S(2)}) async-start(s8[6291456]{0:T(1024)(128)(4,1)} %bitcast.8), calls=%async_computation | async-start | bytes 8388608
  5.5 22.2 %slice-start.2 = ((s8[6291456]{0:T(1024)(128)(4,1)}), s8[4194304]{0:T(1024)(128)(4,1)S(1)}, s32[]{:S(2)}) async-start(s8[6291456]{0:T(1024)(128)(4,1)} %bitcast.14), calls=%async_computation.2 | async-start | bytes 8388608
  5.5 22.2 %slice-start.4 = ((s8[6291456]{0:T(1024)(128)(4,1)}), s8[4194304]{0:T(1024)(128)(4,1)S(1)}, s32[]{:S(2)}) async-start(s8[6291456]{0:T(1024)(128)(4,1)} %bitcast.20), calls=%async_computation.4 | async-start | bytes 8388608
  5.5 21.5 %copy-start = (bf16[1,2048,128]{2,1,0:T(8,128)(2,1)S(1)}, bf16[1,2048,128]{2,1,0:T(8,128)(2,1)}, u32[]{:S(2)}) copy-start(bf16[1,2048,128]{2,1,0:T(8,128)(2,1)} %param.16) | copy-start | bytes 1572868
  5.5 22.2 %slice-start.1 = ((s8[6291456]{0:T(1024)(128)(4,1)}), s8[2097152]{0:T(1024)(128)(4,1)S(1)}, s32[]{:S(2)}) async-start(s8[6291456]{0:T(1024)(128)(4,1)} %bitcast.8), calls=%async_computation.1 | async-start | bytes 4194304
  5.5 22.2 %slice-start.3 = ((s8[6291456]{0:T(1024)(128)(4,1)}), s8[2097152]{0:T(1024)(128)(4,1)S(1)}, s32[]{:S(2)}) async-start(s8[6291456]{0:T(1024)(128)(4,1)} %bitcast.14), calls=%async_computation.3 | async-start | bytes 4194304
  5.5 22.2 %slice-start.5 = ((s8[6291456]{0:T(1024)(128)(4,1)}), s8[2097152]{0:T(1024)(128)(4,1)S(1)}, s32[]{:S(2)}) async-start(s8[6291456]{0:T(1024)(128)(4,1)} %bitcast.20), calls=%async_computation.5 | async-start | bytes 4194304
  5.6 19.4 %collective-permute-start = (bf16[784,128]{1,0:T(8,128)(2,1)S(1)}, bf16[784,128]{1,0:T(8,128)(2,1)S(1)}, u32[]{:S(2)}, u32[]{:S(2)}) collective-permute-start(bf16[784,128]{1,0:T(8,128)(2,1)S(1)} %shard_map.92.refs_0_.refs_6_.refs_4_), channel_id=1, source_target_pairs={{0,2},{2,0},{1,3},{3,1},{4,6},{6,4},{5,7},{7,5},{8,10},{10,8},{9,1... | collective-permute-start | bytes 602120 | tf_op jit(solution)/shard_map/ppermute | solution.py:60
  7.1 11.4 %collective-permute-start.1 = (bf16[384,128]{1,0:T(8,128)(2,1)S(1)}, bf16[384,128]{1,0:T(8,128)(2,1)S(1)}, u32[]{:S(2)}, u32[]{:S(2)}) collective-permute-start(bf16[384,128]{1,0:T(8,128)(2,1)S(1)} %get-tuple-element.35), channel_id=1, source_target_pairs={{0,4},{4,0},{8,12},{12,8},{1,5},{5,1},{9,13},{13,9},{2,6},{6,2},{1... | collective-permute-start | bytes 294920 | tf_op jit(solution)/shard_map/ppermute | solution.py:60
  8.7 12.3 %collective-permute-start.7 = (bf16[400,128]{1,0:T(8,128)(2,1)S(1)}, bf16[400,128]{1,0:T(8,128)(2,1)S(1)}, u32[]{:S(2)}, u32[]{:S(2)}) collective-permute-start(bf16[400,128]{1,0:T(8,128)(2,1)S(1)} %get-tuple-element.38), channel_id=1, source_target_pairs={{0,4},{4,0},{8,12},{12,8},{1,5},{5,1},{9,13},{13,9},{2,6},{6,2},{1... | collective-permute-start | bytes 307208 | tf_op jit(solution)/shard_map/ppermute | solution.py:60
  9.1 12.5 %collective-permute-start.8 = (bf16[400,128]{1,0:T(8,128)(2,1)S(1)}, bf16[400,128]{1,0:T(8,128)(2,1)S(1)}, u32[]{:S(2)}, u32[]{:S(2)}) collective-permute-start(bf16[400,128]{1,0:T(8,128)(2,1)S(1)} %get-tuple-element.39), channel_id=1, source_target_pairs={{0,12},{4,8},{8,4},{12,0},{1,13},{5,9},{9,5},{13,1},{2,14},{6,10},... | collective-permute-start | bytes 307208 | tf_op jit(solution)/shard_map/ppermute | solution.py:60
  16.6 12.9 %collective-permute-start.4 = (bf16[784,128]{1,0:T(8,128)(2,1)S(1)}, bf16[784,128]{1,0:T(8,128)(2,1)S(1)}, u32[]{:S(2)}, u32[]{:S(2)}) collective-permute-start(bf16[784,128]{1,0:T(8,128)(2,1)S(1)} %collective-permute-done.3.refs_2_.refs_8_.refs_6_), channel_id=1, source_target_pairs={{0,2},{2,0},{1,3},{3,1},{4,6},{6,4},{5,7},{7,5},{8,10},{10,8},{9,1... | collective-permute-start | bytes 602120 | tf_op jit(solution)/shard_map/ppermute | solution.py:60
  18.6 6.4 %collective-permute-start.5 = (bf16[384,128]{1,0:T(8,128)(2,1)S(1)}, bf16[384,128]{1,0:T(8,128)(2,1)S(1)}, u32[]{:S(2)}, u32[]{:S(2)}) collective-permute-start(bf16[384,128]{1,0:T(8,128)(2,1)S(1)} %get-tuple-element.37), channel_id=1, source_target_pairs={{0,12},{4,8},{8,4},{12,0},{1,13},{5,9},{9,5},{13,1},{2,14},{6,10},... | collective-permute-start | bytes 294920 | tf_op jit(solution)/shard_map/ppermute | solution.py:60
  21.0 6.6 %collective-permute-start.10 = (bf16[400,128]{1,0:T(8,128)(2,1)S(1)}, bf16[400,128]{1,0:T(8,128)(2,1)S(1)}, u32[]{:S(2)}, u32[]{:S(2)}) collective-permute-start(bf16[400,128]{1,0:T(8,128)(2,1)S(1)} %collective-permute-done.7.refs_1_.refs_7_.refs_5_), channel_id=1, source_target_pairs={{0,2},{2,0},{1,3},{3,1},{4,6},{6,4},{5,7},{7,5},{8,10},{10,8},{9,1... | collective-permute-start | bytes 307208 | tf_op jit(solution)/shard_map/ppermute | solution.py:60
  21.6 7.9 %collective-permute-start.11 = (bf16[400,128]{1,0:T(8,128)(2,1)S(1)}, bf16[400,128]{1,0:T(8,128)(2,1)S(1)}, u32[]{:S(2)}, u32[]{:S(2)}) collective-permute-start(bf16[400,128]{1,0:T(8,128)(2,1)S(1)} %collective-permute-done.8.refs_3_.refs_9_.refs_7_), channel_id=1, source_target_pairs={{0,2},{2,0},{1,3},{3,1},{4,6},{6,4},{5,7},{7,5},{8,10},{10,8},{9,1... | collective-permute-start | bytes 307208 | tf_op jit(solution)/shard_map/ppermute | solution.py:60
  25.0 5.5 %collective-permute-start.2 = (bf16[384,128]{1,0:T(8,128)(2,1)S(1)}, bf16[384,128]{1,0:T(8,128)(2,1)S(1)}, u32[]{:S(2)}, u32[]{:S(2)}) collective-permute-start(bf16[384,128]{1,0:T(8,128)(2,1)S(1)} %collective-permute-done.1.refs_1_), channel_id=1, source_target_pairs={{0,2},{2,0},{1,3},{3,1},{4,6},{6,4},{5,7},{7,5},{8,10},{10,8},{9,1... | collective-permute-start | bytes 294920 | tf_op jit(solution)/shard_map/ppermute | solution.py:60
  25.0 6.5 %collective-permute-start.6 = (bf16[384,128]{1,0:T(8,128)(2,1)S(1)}, bf16[384,128]{1,0:T(8,128)(2,1)S(1)}, u32[]{:S(2)}, u32[]{:S(2)}) collective-permute-start(bf16[384,128]{1,0:T(8,128)(2,1)S(1)} %collective-permute-done.5.refs_3_), channel_id=1, source_target_pairs={{0,2},{2,0},{1,3},{3,1},{4,6},{6,4},{5,7},{7,5},{8,10},{10,8},{9,1... | collective-permute-start | bytes 294920 | tf_op jit(solution)/shard_map/ppermute | solution.py:60
  27.6 4.0 %collective-permute-start.9 = (f32[8,192]{1,0:T(8,128)S(1)}, f32[8,192]{1,0:T(8,128)S(1)}, u32[]{:S(2)}, u32[]{:S(2)}) collective-permute-start(f32[8,192]{1,0:T(8,128)S(1)} %shard_map.94.refs_8_), channel_id=1, source_target_pairs={{0,2},{2,0},{1,3},{3,1},{4,6},{6,4},{5,7},{7,5},{8,10},{10,8},{9,1... | collective-permute-start | bytes 18440 | tf_op jit(solution)/shard_map/ppermute | solution.py:60
  29.5 2.1 %copy-start.1 = (bf16[1,128,768]{2,1,0:T(8,128)(2,1)S(1)}, bf16[1,128,768]{2,1,0:T(8,128)(2,1)}, u32[]{:S(2)}) copy-start(bf16[1,128,768]{2,1,0:T(8,128)(2,1)} %param.17) | copy-start | bytes 589828
  32.9 11.4 %copy-start.2 = (s32[64,2]{0,1:T(2,128)S(1)}, s32[64,2]{0,1:T(2,128)}, u32[]{:S(2)}) copy-start(s32[64,2]{0,1:T(2,128)} %param.10) | copy-start | bytes 1540
  33.0 11.4 %copy-start.3 = (f32[64,2]{0,1:T(2,128)S(1)}, f32[64,2]{0,1:T(2,128)}, u32[]{:S(2)}) copy-start(f32[64,2]{0,1:T(2,128)} %param.11) | copy-start | bytes 1540
  34.9 7.4 %collective-permute-start.17 = (bf16[768,128]{1,0:T(8,128)(2,1)S(1)}, bf16[768,128]{1,0:T(8,128)(2,1)S(1)}, u32[]{:S(2)}, u32[]{:S(2)}) collective-permute-start(bf16[768,128]{1,0:T(8,128)(2,1)S(1)} %get-tuple-element.55), channel_id=1, source_target_pairs={{4,0},{0,4},{12,8},{8,12},{5,1},{1,5},{13,9},{9,13},{6,2},{2,6},{1... | collective-permute-start | bytes 589832 | tf_op jit(solution)/shard_map/ppermute | solution.py:60
  35.1 9.3 %collective-permute-start.16 = (bf16[768,128]{1,0:T(8,128)(2,1)S(1)}, bf16[768,128]{1,0:T(8,128)(2,1)S(1)}, u32[]{:S(2)}, u32[]{:S(2)}) collective-permute-start(bf16[768,128]{1,0:T(8,128)(2,1)S(1)} %get-tuple-element.53), channel_id=1, source_target_pairs={{4,0},{0,4},{12,8},{8,12},{5,1},{1,5},{13,9},{9,13},{6,2},{2,6},{1... | collective-permute-start | bytes 589832 | tf_op jit(solution)/shard_map/ppermute | solution.py:60
  37.0 12.5 %collective-permute-start.18 = (bf16[768,128]{1,0:T(8,128)(2,1)S(1)}, bf16[768,128]{1,0:T(8,128)(2,1)S(1)}, u32[]{:S(2)}, u32[]{:S(2)}) collective-permute-start(bf16[768,128]{1,0:T(8,128)(2,1)S(1)} %get-tuple-element.61), channel_id=1, source_target_pairs={{0,2},{2,0},{1,3},{3,1},{4,6},{6,4},{5,7},{7,5},{8,10},{10,8},{9,1... | collective-permute-start | bytes 589832 | tf_op jit(solution)/shard_map/ppermute | solution.py:60
  45.2 22.3 %collective-permute-start.20 = (bf16[1024,128]{1,0:T(8,128)(2,1)S(1)}, bf16[1024,128]{1,0:T(8,128)(2,1)S(1)}, u32[]{:S(2)}, u32[]{:S(2)}) collective-permute-start(bf16[1024,128]{1,0:T(8,128)(2,1)S(1)} %get-tuple-element.62), channel_id=1, source_target_pairs={{0,2},{2,0},{1,3},{3,1},{4,6},{6,4},{5,7},{7,5},{8,10},{10,8},{9,1... | collective-permute-start | bytes 786440 | tf_op jit(solution)/shard_map/ppermute | solution.py:60
  47.5 8.0 %collective-permute-start.14 = (bf16[384,128]{1,0:T(8,128)(2,1)S(1)}, bf16[384,128]{1,0:T(8,128)(2,1)S(1)}, u32[]{:S(2)}, u32[]{:S(2)}) collective-permute-start(bf16[384,128]{1,0:T(8,128)(2,1)S(1)} %get-tuple-element.50), channel_id=1, source_target_pairs={{0,2},{2,0},{1,3},{3,1},{4,6},{6,4},{5,7},{7,5},{8,10},{10,8},{9,1... | collective-permute-start | bytes 294920 | tf_op jit(solution)/shard_map/ppermute | solution.py:60
  47.6 10.4 %collective-permute-start.12 = (bf16[384,128]{1,0:T(8,128)(2,1)S(1)}, bf16[384,128]{1,0:T(8,128)(2,1)S(1)}, u32[]{:S(2)}, u32[]{:S(2)}) collective-permute-start(bf16[384,128]{1,0:T(8,128)(2,1)S(1)} %get-tuple-element.48), channel_id=1, source_target_pairs={{0,2},{2,0},{1,3},{3,1},{4,6},{6,4},{5,7},{7,5},{8,10},{10,8},{9,1... | collective-permute-start | bytes 294920 | tf_op jit(solution)/shard_map/ppermute | solution.py:60
  49.6 17.9 %collective-permute-start.19 = (bf16[768,128]{1,0:T(8,128)(2,1)S(1)}, bf16[768,128]{1,0:T(8,128)(2,1)S(1)}, u32[]{:S(2)}, u32[]{:S(2)}) collective-permute-start(bf16[768,128]{1,0:T(8,128)(2,1)S(1)} %shard_map.105), channel_id=1, source_target_pairs={{12,0},{8,4},{4,8},{0,12},{13,1},{9,5},{5,9},{1,13},{14,2},{10,6},... | collective-permute-start | bytes 589832 | tf_op jit(solution)/shard_map/ppermute | solution.py:60
  55.5 10.3 %collective-permute-start.15 = (bf16[384,128]{1,0:T(8,128)(2,1)S(1)}, bf16[384,128]{1,0:T(8,128)(2,1)S(1)}, u32[]{:S(2)}, u32[]{:S(2)}) collective-permute-start(bf16[384,128]{1,0:T(8,128)(2,1)S(1)} %shard_map.102), channel_id=1, source_target_pairs={{8,0},{12,4},{0,8},{4,12},{9,1},{13,5},{1,9},{5,13},{10,2},{14,6},... | collective-permute-start | bytes 294920 | tf_op jit(solution)/shard_map/ppermute | solution.py:60
  58.0 8.8 %collective-permute-start.13 = (bf16[384,128]{1,0:T(8,128)(2,1)S(1)}, bf16[384,128]{1,0:T(8,128)(2,1)S(1)}, u32[]{:S(2)}, u32[]{:S(2)}) collective-permute-start(bf16[384,128]{1,0:T(8,128)(2,1)S(1)} %shard_map.100), channel_id=1, source_target_pairs={{8,0},{12,4},{0,8},{4,12},{9,1},{13,5},{1,9},{5,13},{10,2},{14,6},... | collective-permute-start | bytes 294920 | tf_op jit(solution)/shard_map/ppermute | solution.py:60
